TPU v7x, 32 devices: a whole 2x2x4 slice. The times are simulated.
32 devices in a mesh: chan: 4 (over z), tile: 8 (over y, x, core).
Axes of the slice: x: 2, y: 2, z: 4, core: 2. Of those that a mesh axis runs over, the one named last changes fastest.
Arguments:
- visibility: bfloat16 [1024, 2, 1024], P('tile', None, 'chan'), may hold values from -6 to 6
- flags: int32 [1024, 1024], P('tile', 'chan'), may hold values 0 or 1
- u_index: int32 [1024], replicated, may hold values from 0 to 511
- v_index: int32 [1024], replicated, may hold values from 0 to 255
- fg_filter: bfloat16 [1024, 1024], replicated, may hold values from -1 to 1
Outputs:
- cleaned: float32 [1024, 2, 1024], P('tile', None, 'chan')
All inputs are finite; a program needn't handle non-finite values. No bound on the sum of `flags` on one device may be relied on, other than what follows from the above.
Results may differ from a plain program's by a relative error of at most 0.0029.
Values may be sent and summed in bfloat16 or wider, within the bound.
No kernel may reach another device: no remote copies, remote signals or barrier semaphores. Data moves between devices by JAX's collectives and lax.ppermute only.
A program may use at most 256 MiB of HBM per device.

v0:
```python
import math

import jax
import jax.numpy as jnp
from jax import lax
from jax.sharding import PartitionSpec as P

F = 1024
L = 512
M = 256


TWO_PI = 2.0 * math.pi
FINE_STEP = 8


def tables(grid_index, positions, period):
    turn_count = grid_index[:, None] * positions[None, :] % period
    angles = turn_count.astype(jnp.float32) * (TWO_PI / period)
    return (jnp.cos(angles).astype(jnp.bfloat16), jnp.sin(angles).astype(jnp.bfloat16))


def line_tables(u_rows, line_ids, chan_start, chan_count, chan_total, line_total):
    period = chan_total * line_total
    coarse_ids = (
        chan_total + chan_start + FINE_STEP * jnp.arange(chan_count // FINE_STEP, dtype=jnp.int32)
    )
    fine_ids = jnp.arange(FINE_STEP, dtype=jnp.int32)
    base = u_rows[:, None] * line_ids[None, :]
    coarse_turns = base[:, :, None] * coarse_ids[None, None, :] % period
    fine_turns = base[:, :, None] * fine_ids[None, None, :] % period
    coarse_angle = coarse_turns.astype(jnp.float32) * (TWO_PI / period)
    fine_angle = fine_turns.astype(jnp.float32) * (TWO_PI / period)
    coarse_cos = jnp.cos(coarse_angle)[:, :, :, None]
    coarse_sin = jnp.sin(coarse_angle)[:, :, :, None]
    fine_cos = jnp.cos(fine_angle)[:, :, None, :]
    fine_sin = jnp.sin(fine_angle)[:, :, None, :]
    whole_cos = coarse_cos * fine_cos - coarse_sin * fine_sin
    whole_sin = coarse_sin * fine_cos + coarse_cos * fine_sin
    shape = (u_rows.shape[0], line_ids.shape[0], chan_count)
    return (
        whole_cos.reshape(shape).astype(jnp.bfloat16),
        whole_sin.reshape(shape).astype(jnp.bfloat16),
    )


def predict(image_lines, cos_line, sin_line, cos_col, sin_col):
    line_count, chan_count, pixel_cols = image_lines.shape
    row_count = cos_col.shape[0]
    phase_both = jnp.concatenate([cos_col, sin_col], 0)
    hidden_sum = lax.dot_general(
        image_lines.reshape(line_count * chan_count, pixel_cols),
        phase_both,
        (((1,), (1,)), ((), ())),
        preferred_element_type=jnp.float32,
    )
    hidden_sum = hidden_sum.reshape(line_count, chan_count, 2, row_count)
    half_cos = hidden_sum[:, :, 0, :]
    half_sin = hidden_sum[:, :, 1, :]
    row_cos = jnp.transpose(cos_line.astype(jnp.float32), (1, 2, 0))
    row_sin = jnp.transpose(sin_line.astype(jnp.float32), (1, 2, 0))
    real_pred = jnp.sum(row_cos * half_cos - row_sin * half_sin, axis=0)
    imag_pred = -jnp.sum(row_sin * half_cos + row_cos * half_sin, axis=0)
    return jnp.transpose(jnp.stack([real_pred, imag_pred], 0), (2, 0, 1))


def local(visibility, flags, u_index, v_index, fg_filter):
    row_count = visibility.shape[0]
    chan_count = visibility.shape[2]
    total_rows = u_index.shape[0]
    line_count = L // lax.axis_size("tile")
    line_ids = lax.axis_index("tile") * line_count + jnp.arange(line_count, dtype=jnp.int32)
    chan_start = lax.axis_index("chan") * chan_count
    cos_line, sin_line = line_tables(u_index, line_ids, chan_start, chan_count, F, L)
    cos_col, sin_col = tables(v_index, jnp.arange(M, dtype=jnp.int32), 2 * M)
    weight = flags.astype(jnp.bfloat16)
    weighted = visibility * weight[:, None, :]
    shard_piece = lax.all_gather(weighted, "tile", axis=0, tiled=True)
    piece_rows = shard_piece.shape[0]
    line_cos = cos_line.astype(jnp.float32)
    line_sin = sin_line.astype(jnp.float32)
    real_part = shard_piece[:, 0, :].astype(jnp.float32)[:, None, :]
    imag_part = shard_piece[:, 1, :].astype(jnp.float32)[:, None, :]
    x_real = (real_part * line_cos - imag_part * line_sin).astype(jnp.bfloat16)
    x_imag = (real_part * line_sin + imag_part * line_cos).astype(jnp.bfloat16)
    stacked = jnp.concatenate([x_real, x_imag], 0).reshape(2 * piece_rows, line_count * chan_count)
    phase_cols = jnp.concatenate([cos_col, -sin_col], 0)
    dirty_sum = lax.dot_general(
        stacked, phase_cols, (((0,), (0,)), ((), ())), preferred_element_type=jnp.float32
    )
    dirty_image = (
        (dirty_sum * (1.0 / math.sqrt(total_rows)))
        .astype(jnp.bfloat16)
        .reshape(line_count, chan_count, M)
    )
    filtered = jnp.einsum(
        "fg,qgm->qfm",
        fg_filter,
        lax.all_to_all(dirty_image, "chan", split_axis=0, concat_axis=1, tiled=True),
        preferred_element_type=jnp.float32,
    ).astype(jnp.bfloat16)
    foreground = lax.all_to_all(filtered, "chan", split_axis=1, concat_axis=0, tiled=True)
    own_start = lax.axis_index("tile") * row_count
    u_owned = lax.dynamic_slice_in_dim(u_index, own_start, row_count, 0)
    v_owned = lax.dynamic_slice_in_dim(v_index, own_start, row_count, 0)
    full_cos, full_sin = line_tables(
        u_owned, jnp.arange(L, dtype=jnp.int32), chan_start, chan_count, F, L
    )
    own_cos, own_sin = tables(v_owned, jnp.arange(M, dtype=jnp.int32), 2 * M)
    zero_rows = jnp.zeros((row_count, 2, chan_count), jnp.float32)
    shard_piece = lax.all_gather(foreground, "tile", axis=0, tiled=True)
    piece_lines = shard_piece.shape[0]
    block_count = piece_lines // line_count
    blocks = shard_piece.reshape(block_count, line_count, chan_count, M)
    offsets = jnp.arange(block_count, dtype=jnp.int32) * line_count

    def one_block(carried, scan_item):
        block_lines, offset = scan_item
        block_cos = lax.dynamic_slice_in_dim(full_cos, offset, line_count, 1)
        block_sin = lax.dynamic_slice_in_dim(full_sin, offset, line_count, 1)
        return (carried + predict(block_lines, block_cos, block_sin, own_cos, own_sin), None)

    summed, _ = lax.scan(one_block, zero_rows, (blocks, offsets))
    predicted = summed * (1.0 / math.sqrt(L * M))
    return weight.astype(jnp.float32)[:, None, :] * (visibility.astype(jnp.float32) - predicted)


def solution(mesh):
    return jax.shard_map(
        local,
        mesh=mesh,
        in_specs=(P("tile", None, "chan"), P("tile", "chan"), P(), P(), P()),
        out_specs=P("tile", None, "chan"),
        check_vma=False,
    )
```

profile of v0, /device:TPU:0, one launch (start us, length us, event | category | flops | bytes accessed | tf_op | source)
XLA Modules:
  0.0 1037.5 jit_solution(1772755833792879278)
XLA Ops:
  10.7 8.2 fusion.57
  18.9 34.4 %fusion.32 = (f32[1024,64,32]{0,2,1:T(8,128)}, f32[1024,64,32]{0,2,1:T(8,128)}) fusion(s32[32]{0:T(128)S(1)} %multiply_add_fusion, s32[1024,64]{0,1:T(8,128)S(1)} %broadcast_multiply_fusion), kind=kLoop, calls=%fused_computation.55 | loop fusion | flops 29360128 | bytes 17039488 | tf_op jit(solution)/shard_map/cos | solution.py:34
  53.4 27.3 %add_convert_fusion.1 = (bf16[1024,64,32,8]{0,3,2,1:T(8,128)(2,1)}, bf16[1024,64,32,8]{0,3,2,1:T(8,128)(2,1)}) fusion(f32[1024,64,8]{0,2,1:T(8,128)S(1)} %get-tuple-element.152, f32[1024,64,32]{0,2,1:T(8,128)} %get-tuple-element.148, f32[1024,64,8]{0,2,1:T(8,128)S(1)} %get-tuple-element.151, f32[1024,64,32]{0,2,1:T(8,128)} %get-tuple-element.147), kind=kLoop, calls=%fused_computation.30 | loop fusion | flops 134217728 | bytes 88080384 | tf_op jit(solution)/shard_map/convert_element_type | solution.py:43
  80.7 5.0 cosine_convert_fusion
  85.6 5.2 fusion.61
  97.6 46.6 %fusion.10 = (bf16[1024,16384]{0,1:T(8,128)(2,1)}, bf16[1024,16384]{0,1:T(8,128)(2,1)}) fusion(bf16[1024,64,32,8]{0,3,2,1:T(8,128)(2,1)} %get-tuple-element.144, bf16[1024,64,32,8]{0,3,2,1:T(8,128)(2,1)} %get-tuple-element.143, f32[1024,256]{0,1:T(8,128)} %copy.24, f32[1024,256]{0,1:T(8,128)S(1)} %copy.23), kind=kLoop, calls=%fused_computation.22 | loop fusion | flops 167772160 | bytes 136314880 | tf_op jit(solution)/shard_map/convert_element_type | solution.py:84
  144.2 28.8 %fusion.22 = bf16[16384,256]{1,0:T(8,128)(2,1)} fusion(bf16[1024,16384]{0,1:T(8,128)(2,1)} %get-tuple-element.140, bf16[1024,16384]{0,1:T(8,128)(2,1)} %get-tuple-element.139, bf16[1024,256]{1,0:T(8,128)(2,1)} %fusion.61, bf16[1024,256]{1,0:T(8,128)(2,1)} %cosine_convert_fusion), kind=kOutput, calls=%fused_computation.36 | convolution fusion | flops 17324572672 | bytes 76546048 | tf_op jit(solution)/shard_map/dot_general | solution.py:88
  173.0 192.2 %all_to_all.36 = bf16[64,256,256]{2,1,0:T(8,128)(2,1)} all-to-all(bf16[64,256,256]{2,1,0:T(8,128)(2,1)} %bitcast.133), channel_id=1, replica_groups=mesh['chan'=4,'tile'=8] {'chan'}, dimensions={0} | all-to-all | bytes 16777216 | tf_op jit(solution)/shard_map/all_to_all | solution.py:99
  365.2 13.7 %copy.25 = bf16[4,16,256,256]{2,0,3,1:T(4,128)(2,1)} copy(bf16[4,16,256,256]{3,2,1,0:T(8,128)(2,1)} %bitcast.129) | data formatting | bytes 16777216 | tf_op jit(solution)/shard_map/all_to_all | solution.py:99
  378.9 14.3 %all_to_all.29 = bf16[16,1024,256]{1,2,0:T(8,128)(2,1)} reshape(bf16[16,4,256,256]{2,1,3,0:T(4,128)(2,1)} %bitcast.130) | data formatting | bytes 16777216 | tf_op jit(solution)/shard_map/all_to_all | solution.py:99
  393.2 14.6 %convert_bitcast_fusion = bf16[16,1024,256]{1,2,0:T(8,128)(2,1)} fusion(bf16[16,1024,256]{1,2,0:T(8,128)(2,1)} %all_to_all.29, bf16[1024,1024]{1,0:T(8,128)(2,1)S(1)} %copy-done), kind=kOutput, calls=%fused_computation.53 | convolution fusion | flops 8594128896 | bytes 18874368 | tf_op jit(solution)/shard_map/fg,qgm->qfm/dot_general | solution.py:96
  407.8 12.6 %copy.26 = bf16[16,1024,256]{2,0,1:T(8,128)(2,1)} copy(bf16[16,1024,256]{1,2,0:T(8,128)(2,1)} %convert_bitcast_fusion) | data formatting | bytes 16777216 | tf_op jit(solution)/shard_map/convert_element_type | solution.py:101
  420.4 190.4 %all_to_all.37 = bf16[16,1024,256]{2,0,1:T(8,128)(2,1)} all-to-all(bf16[16,1024,256]{2,0,1:T(8,128)(2,1)} %copy.26), channel_id=1, replica_groups=mesh['chan'=4,'tile'=8] {'chan'}, dimensions={1} | all-to-all | bytes 16777216 | tf_op jit(solution)/shard_map/all_to_all | solution.py:102
  610.9 9.9 copy.28
  622.3 8.2 fusion.59
  630.5 34.7 %fusion.34 = (f32[128,512,32]{0,2,1:T(8,128)}, f32[128,512,32]{0,2,1:T(8,128)}) fusion(s32[32]{0:T(128)S(1)} %copy-done.6, s32[128,512]{0,1:T(8,128)S(1)} %iota_multiply_fusion), kind=kLoop, calls=%fused_computation.57 | loop fusion | flops 29360128 | bytes 17039488 | tf_op jit(solution)/shard_map/cos | solution.py:34
  665.3 27.5 %fusion.18 = (bf16[128,512,256]{0,2,1:T(8,128)(2,1)}, bf16[128,512,256]{0,2,1:T(8,128)(2,1)}) fusion(f32[128,512,8]{0,2,1:T(8,128)S(1)} %get-tuple-element.154, f32[128,512,32]{0,2,1:T(8,128)} %get-tuple-element.150, f32[128,512,8]{0,2,1:T(8,128)S(1)} %get-tuple-element.153, f32[128,512,32]{0,2,1:T(8,128)} %get-tuple-element.149), kind=kLoop, calls=%fused_computation.34 | loop fusion | flops 134217728 | bytes 88080384 | tf_op jit(solution)/shard_map/convert_element_type | solution.py:43
  692.8 229.7 %all-gather.5.cloned.1.call-done = bf16[512,256,256]{2,1,0:T(8,128)(2,1)} async-done(((bf16[64,256,256]{2,1,0:T(8,128)(2,1)}), bf16[512,256,256]{2,1,0:T(8,128)(2,1)}) %all-gather.5.cloned.1.call-update) | async-done | bytes 67108880 | tf_op jit(solution)/shard_map/all_gather | solution.py:111
  922.4 106.1 %while.13 = (s32[]{:T(128)}, f32[128,2,256]{0,2,1:T(8,128)S(1)}, s32[8]{0:T(128)S(1)}, bf16[128,512,256]{0,2,1:T(8,128)(2,1)}, bf16[8,64,256,256]{3,2,1,0:T(8,12...) while((s32[]{:T(128)}, f32[128,2,256]{0,2,1:T(8,128)S(1)}, ...), condition=%wide.region_3.4_spmd.clone, body=%wide.region_0.3_spmd.clone.sunk | while | flops 2168619008 | bytes 51774108 | solution.py:123
  925.1 4.8 fusion.84
  929.9 5.6 fusion.85
  938.4 4.8 fusion.84
  943.2 5.6 fusion.85
  951.6 4.8 fusion.84
  956.4 5.6 fusion.85
  969.7 5.6 fusion.85
  983.0 5.6 fusion.85
  991.4 4.8 fusion.84
  996.2 5.6 fusion.85
  1004.7 4.8 fusion.84
  1009.5 5.6 fusion.85
  1022.7 5.6 fusion.85
  (63 shorter events, 34.4 us)
Async XLA Ops:
  6.5 386.7 %copy-start = (bf16[1024,1024]{1,0:T(8,128)(2,1)S(1)}, bf16[1024,1024]{1,0:T(8,128)(2,1)}, u32[]{:S(2)}) copy-start(bf16[1024,1024]{1,0:T(8,128)(2,1)} %param.11) | copy-start | bytes 6291460
  6.5 84.3 %all-gather.3.cloned.1.call-start = ((), (), s32[]{:S(2)}) async-start(), calls=%async_computation.2 | async-start | bytes 1179648 | tf_op jit(solution)/shard_map/all_gather | solution.py:78
  9.9 912.6 %all-gather.5.cloned.1.call-start = ((), (), s32[]{:S(2)}) async-start(), calls=%async_computation.3 | async-start | bytes 75497472 | tf_op jit(solution)/shard_map/all_gather | solution.py:111
  9.9 43.4 %copy-start.5 = (s32[32]{0:T(128)}, s32[32]{0:T(128)S(1)}, u32[]{:S(2)}) copy-start(s32[32]{0:T(128)S(1)} %multiply_add_fusion) | copy-start | bytes 388
  53.4 27.3 %copy-start.4 = (s32[1024]{0:T(1024)S(1)}, s32[1024]{0:T(1024)}, u32[]{:S(2)}) copy-start(s32[1024]{0:T(1024)} %param.10) | copy-start | bytes 12292
  620.8 9.7 copy-start.6
  922.4 106.2 %copy-start.2 = (bf16[128,2,256]{2,1,0:T(2,128)(2,1)S(1)}, bf16[128,2,256]{2,1,0:T(2,128)(2,1)}, u32[]{:S(2)}) copy-start(bf16[128,2,256]{2,1,0:T(2,128)(2,1)} %param.7) | copy-start | bytes 393220
  922.4 106.2 %copy-start.3 = (f32[128,256]{1,0:T(8,128)S(1)}, f32[128,256]{1,0:T(8,128)}, u32[]{:S(2)}) copy-start(f32[128,256]{1,0:T(8,128)} %get-tuple-element.137) | copy-start | bytes 393220
  1028.5 1.7 copy-start.1
Sparse Core Ops, SparseCore 0:
  10.0 26.2 all-gather.2
  620.9 301.4 all-gather.4
where the time goes:
time: 1050 us; the launch traced here: 1040 us
  blocking collectives  383 us (36%)
  other arithmetic  251 us (24%)
  waiting for transfers between devices  230 us (22%)
  matrix products  81.8 us (8%)
  local copies, waits for them, and re-layouts  61.4 us (6%)
  loops' own time  16.6 us (2%)
  between operations  14 us (1%)
    all_gather x1, waiting for transfers between devices, local(): shard_piece = lax.all_gather(foreground, 'tile', axis=0, tiled=True)  230 us
    all_to_all x1, blocking collectives, local(): lax.all_to_all(dirty_image, 'chan', split_axis=0, concat_axis=1, tiled=True)  192 us
    all_to_all x1, blocking collectives, local(): lax.all_to_all(filtered, 'chan', split_axis=1, concat_axis=0, tiled=True)  190 us
    cos x2, other arithmetic, line_tables(): coarse_cos = jnp.cos(coarse_angle)[:, :, :, None]  69.2 us
    convert_element_type x2, other arithmetic, line_tables(): whole_sin.reshape(shape).astype(jnp.bfloat16)  54.8 us
    convert_element_type x1, other arithmetic, local(): x_real = (real_part * line_cos - imag_part * line_sin).astype(jnp.bfloat16)  46.6 us
    reduce_sum x8, other arithmetic, predict(): real_pred = jnp.sum(row_cos * half_cos - row_sin * half_sin, axis=0)  45 us
    dot_general x8, matrix products, predict(): lax.dot_general(image_lines.reshape(line_count * chan_count, pixel_cols),...  38.5 us
  transfers between devices with their start and end apart: 2, of which 1 were waited for; matrix products, arithmetic and copies ran while one was open for 15% of the time, Pallas kernels for 0%

commit v1 on v0

v1 whole, which is shorter than its diff:
```python
import functools
import math

import jax
import jax.numpy as jnp
import numpy as np
from jax import lax
from jax.experimental import pallas as pl
from jax.experimental.pallas import tpu as pltpu
from jax.sharding import PartitionSpec as P

F = 1024
L = 512
M = 256

TWO_PI = 2.0 * math.pi
FINE = 8
LANES = 128
A_CHANS = 16
C_CHANS = 16
F32 = jnp.float32
BF16 = jnp.bfloat16


def tile_masks(tiles):
    bits = [1 << i for i in range(1, tiles.bit_length() - 1)]
    swapped = bits[1::-1] + bits[2:]
    return (bits, swapped)


def block_order(tiles):
    offsets = []
    for masks in tile_masks(tiles):
        held = [0]
        for mask in masks:
            held = held + [s ^ mask for s in held]
        offsets.append(held)
    rows = []
    for t in range(tiles):
        own = [t ^ s for s in offsets[t & 1]]
        rows.append(own + [(t ^ 1) ^ s for s in offsets[1 - (t & 1)]])
    return np.asarray(rows, np.int32)


def stage_pairs(tiles, stage):
    even, odd = tile_masks(tiles)
    return [(t, t ^ (odd if t & 1 else even)[stage]) for t in range(tiles)]


def gather_tile(block, tiles):
    held = block[None]
    for stage in range(len(tile_masks(tiles)[0])):
        held = jnp.concatenate([held, lax.ppermute(held, "tile", stage_pairs(tiles, stage))], 0)
    other = lax.ppermute(held, "tile", [(t, t ^ 1) for t in range(tiles)])
    return jnp.concatenate([held, other], 0)


def reduce_tile(kept, sent, tiles):
    received = lax.ppermute(sent, "tile", [(t, t ^ 1) for t in range(tiles)])
    total = kept + received.astype(F32)
    for stage in reversed(range(len(tile_masks(tiles)[0]))):
        half = total.shape[0] // 2
        received = lax.ppermute(total[half:].astype(BF16), "tile", stage_pairs(tiles, stage))
        total = total[:half] + received.astype(F32)
    return total[0]


def unit(turns, period):
    angle = (turns % period).astype(F32) * (TWO_PI / period)
    return jnp.cos(angle), jnp.sin(angle)


def times(a, b):
    return a[0] * b[0] - a[1] * b[1], a[1] * b[0] + a[0] * b[1]


def column_tables(v_rows):
    digit = 16
    high = unit(v_rows[None, :] * (digit * jnp.arange(M // digit, dtype=jnp.int32))[:, None], 2 * M)
    low = unit(v_rows[None, :] * jnp.arange(digit, dtype=jnp.int32)[:, None], 2 * M)
    both = times(
        (high[0][:, None, :], high[1][:, None, :]), (low[0][None, :, :], low[1][None, :, :])
    )
    return [part.reshape(M, -1).astype(BF16) for part in both]


def phase_tables(scaled_rows, period):
    groups = F // FINE
    digit = 16
    high_ids = F + FINE * digit * jnp.arange(groups // digit, dtype=jnp.int32)
    high = unit(scaled_rows[None, :] * high_ids[:, None], period)
    low = unit(
        scaled_rows[None, :] * (FINE * jnp.arange(digit, dtype=jnp.int32))[:, None], period
    )
    coarse = times(
        (high[0][:, None, :], high[1][:, None, :]), (low[0][None, :, :], low[1][None, :, :])
    )
    fine = unit(scaled_rows[None, :] * jnp.arange(FINE, dtype=jnp.int32)[:, None], period)
    coarse = jnp.stack([part.reshape(groups, -1, LANES) for part in coarse])
    return jnp.transpose(coarse, (0, 2, 1, 3)), jnp.stack(fine)


def phases(coarse_ref, fine_ref, group, chans, block):
    lanes = slice(block * LANES, (block + 1) * LANES)
    fine = (fine_ref[0, :, lanes], fine_ref[1, :, lanes])
    parts = []
    for step in range(chans // FINE):
        row = pl.ds(group + step, FINE, stride=0)
        coarse = (coarse_ref[0, block, row, :], coarse_ref[1, block, row, :])
        parts.append(times(coarse, fine))
    return (
        jnp.concatenate([part[0] for part in parts], 0),
        jnp.concatenate([part[1] for part in parts], 0),
    )


def paired(count, first, second):
    first(0, 0)

    def body(pair, carry):
        first(2 * pair + 1, 1)
        second(2 * pair, 0)
        first(2 * pair + 2, 0)
        second(2 * pair + 1, 1)
        return carry

    lax.fori_loop(0, count // 2 - 1, body, 0)
    first(count - 1, 1)
    second(count - 2, 0)
    second(count - 1, 1)


def image_kernel(scale, lines, place_ref, vis_ref, step_c, step_f, start_c, start_f, col_ref, out_ref, x0, x1):
    blocks, _, chans, _ = vis_ref.shape
    base = place_ref[0]
    slots = (x0, x1)

    def fill(i, slot):
        x_ref = slots[slot]
        rows = pl.ds(pl.multiple_of(i * A_CHANS, A_CHANS), A_CHANS)
        group = base + i * (A_CHANS // FINE)
        for block in range(blocks):
            step = phases(step_c, step_f, group, A_CHANS, block)
            start = phases(start_c, start_f, group, A_CHANS, block)
            value = (vis_ref[block, 0, rows, :].astype(F32), vis_ref[block, 1, rows, :].astype(F32))
            value = times(value, start)
            at = block * 2 * LANES
            for line in range(lines):
                into = slice(line * A_CHANS, (line + 1) * A_CHANS)
                x_ref[into, at : at + LANES] = value[0].astype(BF16)
                x_ref[into, at + LANES : at + 2 * LANES] = value[1].astype(BF16)
                if line < lines - 1:
                    value = times(value, step)

    def multiply(i, slot):
        rows = pl.ds(pl.multiple_of(i * A_CHANS, A_CHANS), A_CHANS)
        image = jnp.dot(slots[slot][...], col_ref[...], preferred_element_type=F32) * scale
        out_ref[:, rows, :] = image.astype(BF16).reshape(lines, A_CHANS, M)

    paired(chans // A_CHANS, fill, multiply)


def make_image(vis, place, step_t, start_t, col, lines, total_rows):
    blocks, _, chans, _ = vis.shape
    rows = blocks * LANES
    vmem = pl.BlockSpec(memory_space=pltpu.VMEM)
    flops = 2 * lines * chans * 2 * rows * M
    return pl.pallas_call(
        functools.partial(image_kernel, 1.0 / math.sqrt(total_rows), lines),
        out_shape=jax.ShapeDtypeStruct((lines, chans, M), BF16),
        in_specs=[pl.BlockSpec(memory_space=pltpu.SMEM)] + [vmem] * 6,
        out_specs=vmem,
        scratch_shapes=[pltpu.VMEM((lines * A_CHANS, 2 * rows), BF16)] * 2,
        compiler_params=pltpu.CompilerParams(vmem_limit_bytes=40 << 20),
        cost_estimate=pl.CostEstimate(flops=flops, bytes_accessed=8 << 20, transcendentals=0),
        name="image",
    )(place, vis, *step_t, *start_t, col)


def filter_kernel(groups, chans, place_ref, filter_ref, *refs):
    image_refs, out_ref = refs[:groups], refs[groups]
    lines = out_ref.shape[0]
    place = place_ref[0]
    whole = []
    for out_block in range(groups):
        rows = pl.ds(pl.multiple_of(lax.rem(place + out_block, groups) * chans, chans), chans)
        pieces = []
        for in_block in range(groups):
            at = lax.rem(place + (groups - in_block), groups) * chans
            pieces.append(filter_ref[rows, pl.ds(pl.multiple_of(at, chans), chans)])
        whole.append(jnp.concatenate(pieces, 1))
    weights = jnp.concatenate(whole, 0)
    image = jnp.concatenate(
        [jnp.concatenate([ref[line] for line in range(lines)], 1) for ref in image_refs], 0
    )
    result = jnp.dot(weights, image, preferred_element_type=F32).astype(BF16)
    for line in range(lines):
        out_ref[line] = result[:, line * M : (line + 1) * M]


def filter_images(images, place, fg_filter):
    groups = len(images)
    lines, chans, _ = images[0].shape
    step = min(4, lines)
    return pl.pallas_call(
        functools.partial(filter_kernel, groups, chans),
        out_shape=jax.ShapeDtypeStruct((lines, F, M), BF16),
        grid=(lines // step,),
        in_specs=[
            pl.BlockSpec(memory_space=pltpu.SMEM),
            pl.BlockSpec((F, F), lambda i: (0, 0), pipeline_mode=pl.Buffered(1)),
        ]
        + [pl.BlockSpec((step, chans, M), lambda i: (i, 0, 0))] * groups,
        out_specs=pl.BlockSpec((step, F, M), lambda i: (i, 0, 0)),
        compiler_params=pltpu.CompilerParams(vmem_limit_bytes=40 << 20),
        cost_estimate=pl.CostEstimate(
            flops=2 * F * F * lines * M, bytes_accessed=18 << 20, transcendentals=0
        ),
        name="filter",
    )(place, fg_filter, *images)


def predict_kernel(scale, place_ref, image_ref, col_ref, step_c, step_f, start_c, start_f, keep_ref, send_ref, h0, h1):
    lines, chans, _ = image_ref.shape
    blocks = 2 * keep_ref.shape[0]
    base = place_ref[0]
    slots = (h0, h1)

    def multiply(i, slot):
        rows = pl.ds(pl.multiple_of(i * C_CHANS, C_CHANS), C_CHANS)
        image = image_ref[:, rows, :].reshape(lines * C_CHANS, M)
        slots[slot][...] = jnp.dot(image, col_ref[...], preferred_element_type=F32)

    def collect(i, slot):
        h_ref = slots[slot]
        rows = pl.ds(pl.multiple_of(i * C_CHANS, C_CHANS), C_CHANS)
        group = base + i * (C_CHANS // FINE)
        for block in range(blocks):
            step = phases(step_c, step_f, group, C_CHANS, block)
            start = phases(start_c, start_f, group, C_CHANS, block)
            at = block * 2 * LANES
            total = None
            for line in reversed(range(lines)):
                take = slice(line * C_CHANS, (line + 1) * C_CHANS)
                value = (h_ref[take, at : at + LANES], h_ref[take, at + LANES : at + 2 * LANES])
                if total is None:
                    total = value
                else:
                    moved = times(total, step)
                    total = (moved[0] + value[0], moved[1] + value[1])
            total = times(total, start)
            if block < blocks // 2:
                keep_ref[block, 0, rows, :] = total[0] * scale
                keep_ref[block, 1, rows, :] = total[1] * -scale
            else:
                send_ref[block - blocks // 2, 0, rows, :] = (total[0] * scale).astype(BF16)
                send_ref[block - blocks // 2, 1, rows, :] = (total[1] * -scale).astype(BF16)

    paired(chans // C_CHANS, multiply, collect)


def predict_part(foreground, index, place, step_t, start_t, col, chans):
    lines = foreground.shape[0]
    rows = col.shape[1] // 2
    blocks = rows // LANES
    vmem = pl.BlockSpec(memory_space=pltpu.VMEM)
    flops = 2 * lines * chans * 2 * rows * M
    half = (blocks // 2, 2, chans, LANES)
    whole = lambda *shape: pl.BlockSpec(shape, lambda i: (0,) * len(shape), pipeline_mode=pl.Buffered(1))
    return pl.pallas_call(
        functools.partial(predict_kernel, 1.0 / math.sqrt(L * M)),
        out_shape=(jax.ShapeDtypeStruct(half, F32), jax.ShapeDtypeStruct(half, BF16)),
        grid=(1,),
        in_specs=[
            pl.BlockSpec(memory_space=pltpu.SMEM),
            pl.BlockSpec((lines, chans, M), lambda i: (0, index, 0), pipeline_mode=pl.Buffered(1)),
        ]
        + [whole(*a.shape) for a in (col, *step_t, *start_t)],
        out_specs=(whole(*half), whole(*half)),
        scratch_shapes=[pltpu.VMEM((lines * C_CHANS, 2 * rows), F32)] * 2,
        compiler_params=pltpu.CompilerParams(vmem_limit_bytes=40 << 20),
        cost_estimate=pl.CostEstimate(flops=flops, bytes_accessed=8 << 20, transcendentals=0),
        name="predict",
    )(place, foreground, col, *step_t, *start_t)


def local(visibility, flags, u_index, v_index, fg_filter):
    groups, tiles = lax.axis_size("chan"), lax.axis_size("tile")
    chan, tile = lax.axis_index("chan"), lax.axis_index("tile")
    chans = visibility.shape[2]
    total_rows = u_index.shape[0]
    lines = L // (groups * tiles)
    period = F * L

    weight = flags.astype(BF16)
    own = jnp.transpose(visibility * weight[:, None, :], (1, 2, 0))
    seen = [own]
    for away in range(1, groups):
        seen.append(
            lax.ppermute(own, "chan", [(c, (c + away) % groups) for c in range(groups)])
        )
    seen = [gather_tile(block, tiles) for block in seen]

    order = lax.dynamic_index_in_dim(jnp.asarray(block_order(tiles)), tile, 0, keepdims=False)
    u_rows = u_index.reshape(tiles, LANES)[order].reshape(-1)
    v_rows = v_index.reshape(tiles, LANES)[order].reshape(-1)
    first_line = (chan * tiles + tile) * lines
    step_t = phase_tables(u_rows, period)
    start_t = phase_tables(u_rows * first_line, period)
    cos_col, sin_col = column_tables(v_rows)
    predict_col = jnp.stack(
        [cos_col.reshape(M, tiles, LANES), sin_col.reshape(M, tiles, LANES)], 2
    ).reshape(M, 2 * total_rows)
    image_col = jnp.stack(
        [cos_col.T.reshape(tiles, LANES, M), -sin_col.T.reshape(tiles, LANES, M)], 1
    ).reshape(2 * total_rows, M)

    images = []
    for away, block in enumerate(seen):
        place = (lax.rem(chan + groups - away, groups) * (chans // FINE)).reshape(1)
        images.append(make_image(block, place, step_t, start_t, image_col, lines, total_rows))
    foreground = filter_images(images, chan.reshape(1), fg_filter)

    parts = []
    for away in list(range(1, groups)) + [0]:
        place = (lax.rem(chan + away, groups) * (chans // FINE)).reshape(1)
        kept, sent = predict_part(foreground, away, place, step_t, start_t, predict_col, chans)
        part = reduce_tile(kept, sent, tiles)
        if away:
            part = lax.ppermute(
                part.astype(BF16), "chan", [(c, (c + away) % groups) for c in range(groups)]
            ).astype(F32)
        parts.append(part)
    predicted = jnp.transpose(functools.reduce(jnp.add, parts), (2, 0, 1))
    return weight.astype(F32)[:, None, :] * (visibility.astype(F32) - predicted)


def solution(mesh):
    return jax.shard_map(
        local,
        mesh=mesh,
        in_specs=(P("tile", None, "chan"), P("tile", "chan"), P(), P(), P()),
        out_specs=P("tile", None, "chan"),
        check_vma=False,
    )
```

time: 1050 us -> 169 us (0.16); the launches traced: 1040 us -> 168 us
  blocking collectives: 383 us -> 0 us
  other arithmetic: 251 us -> 22.8 us
  waiting for transfers between devices: 230 us -> 19 us
  matrix products: 81.8 us -> 0 us
  Pallas kernels: 0 us -> 73.8 us
  local copies, waits for them, and re-layouts: 61.4 us -> 22.2 us
  starting transfers between devices: 0.04 us -> 29.5 us
  loops' own time: 16.6 us -> 0 us
  between operations: 14 us -> 0.64 us
    all_to_all x2 -> x0, blocking collectives: 383 us -> none  [the longest x1 192 us: local(): lax.all_to_all(dirty_image, 'chan', split_axis=0, concat_axis=1, tiled=True)]
    all_gather x2 -> x0, waiting for transfers between devices: 230 us -> none  [the longest x1 230 us: local(): shard_piece = lax.all_gather(foreground, 'tile', axis=0, tiled=True)]
    convert_element_type x6 -> x5, other arithmetic: 109 us -> 1.3 us  [the longest x1 0.92 us: local(): weight = flags.astype(BF16)]
    cos x4, other arithmetic: 85.5 us -> 2.49 us  [unit(): return (jnp.cos(angle), jnp.sin(angle))]
    dot_general x10 -> x0, matrix products: 81.8 us -> none  [the longest x8 38.5 us: predict(): lax.dot_general(image_lines.reshape(line_count * chan_count, pixel_cols),...]
    pallas_call x0 -> x9, Pallas kernels: none -> 73.8 us  [the longest x4 36.6 us: predict_part(): pl.pallas_call(functools.partial(predict_kernel, 1.0 / math.sqrt(L * M)),...]
    reduce_sum x8 -> x0, other arithmetic: 45 us -> none  [predict(): real_pred = jnp.sum(row_cos * half_cos - row_sin * half_sin, axis=0)]
    all_to_all x3 -> x0, local copies, waits for them, and re-layouts: 38 us -> none  [the longest x2 28 us: local(): lax.all_to_all(dirty_image, 'chan', split_axis=0, concat_axis=1, tiled=True)]
  transfers between devices with their start and end apart: 2 -> 30, of which waited for: 1 -> 7; matrix products, arithmetic and copies ran while one was open for 15% -> 19% of each run, Pallas kernels for 0% -> 23%
where the time goes in v1:
time: 169 us; the launch traced here: 168 us
  Pallas kernels  73.8 us (44%)
  starting transfers between devices  29.5 us (17%)
  other arithmetic  22.8 us (13%)
  local copies, waits for them, and re-layouts  22.2 us (13%)
  waiting for transfers between devices  19 us (11%)
    pallas_call x4, Pallas kernels, predict_part(): pl.pallas_call(functools.partial(predict_kernel, 1.0 / math.sqrt(L * M)),...  36.6 us
    pallas_call x4, Pallas kernels, make_image(): pl.pallas_call(functools.partial(image_kernel, 1.0 / math.sqrt(total_rows...  26.3 us
    ppermute x8, waiting for transfers between devices, reduce_tile(): lax.ppermute(total[half:].astype(BF16), 'tile', stage_pairs(tiles, stage))  11.9 us
    pallas_call x1, Pallas kernels, filter_images(): pl.pallas_call(functools.partial(filter_kernel, groups, chans), out_shape...  10.8 us
    concatenate x8, other arithmetic, gather_tile(): jnp.concatenate([held, lax.ppermute(held, 'tile', stage_pairs(tiles, stag...  10.2 us
    unnamed x59, local copies, waits for them, and re-layouts  10.1 us
    ppermute x8, starting transfers between devices, gather_tile(): lax.ppermute(held, 'tile', stage_pairs(tiles, stage))  9.28 us
    ppermute x8, starting transfers between devices, reduce_tile(): lax.ppermute(total[half:].astype(BF16), 'tile', stage_pairs(tiles, stage))  7.23 us
  transfers between devices with their start and end apart: 30, of which 7 were waited for; matrix products, arithmetic and copies ran while one was open for 19% of the time, Pallas kernels for 23%

profile of v1, /device:TPU:0, one launch (start us, length us, event | category | flops | bytes accessed | tf_op | source)
XLA Modules:
  0.0 167.9 jit_solution(14676996839263665997)
XLA Ops:
  3.4 5.0 %collective-permute-start.11 = (bf16[2,256,128]{2,1,0:T(8,128)(2,1)}, bf16[2,256,128]{2,1,0:T(8,128)(2,1)}, u32[]{:S(2)}, u32[]{:S(2)}) collective-permute-start(bf16[2,256,128]{2,1,0:T(8,128)(2,1)} %get-tuple-element.23), channel_id=1, source_target_pairs={{0,24},{8,0},{16,8},{24,16},{1,25},{9,1},{17,9},{25,17},{2,26},{10... | collective-permute-start | bytes 393224 | tf_op jit(solution)/shard_map/ppermute | solution.py:300
  9.5 1.5 collective-permute-start
  22.5 1.5 collective-permute-start.8
  24.9 1.6 collective-permute-start.1
  28.5 1.7 %pad_maximum_fusion.13 = bf16[2,2,256,128]{3,2,1,0:T(8,128)(2,1)} fusion(bf16[1,2,256,128]{3,2,1,0:T(8,128)(2,1)S(1)} %collective-permute-done.12, bf16[1,2,256,128]{3,2,1,0:T(8,128)(2,1)} %bitcast.25), kind=kLoop, calls=%fused_computation.51 | loop fusion | flops 131072 | bytes 524288 | tf_op jit(solution)/shard_map/concatenate | solution.py:53
  30.2 1.6 collective-permute-start.13
  31.7 1.7 pad_maximum_fusion.12
  33.9 1.8 %pad_maximum_fusion.6 = bf16[4,2,256,128]{3,2,1,0:T(8,128)(2,1)} fusion(bf16[2,2,256,128]{3,2,1,0:T(8,128)(2,1)S(1)} %collective-permute-done.1, bf16[1,2,256,128]{3,2,1,0:T(8,128)(2,1)} %collective-permute-done, bf16[1,2,256,128]{3,2,1,0:T(8,128)(2,1)S(1)} %get-tuple-element.24), kind=kLoop, calls=%fused_computation.24 | loop fusion | flops 524288 | bytes 1048576 | tf_op jit(solution)/shard_map/concatenate | solution.py:53
  36.5 1.6 collective-permute-start.5
  38.2 3.8 %copy.24 = bf16[256,8,2,128]{3,2,1,0:T(2,128)(2,1)} copy(bf16[256,8,2,128]{3,1,0,2:T(8,128)(2,1)} %pad_maximum_fusion.5) | data formatting | bytes 2097152 | tf_op jit(solution)/shard_map/stack | solution.py:311
  42.0 2.6 %reshape.999.col_ref = bf16[256,2048]{1,0:T(8,128)(2,1)} reshape(bf16[256,8,2,128]{3,2,1,0:T(2,128)(2,1)} %copy.24) | data formatting | bytes 2097152 | tf_op jit(solution)/shard_map/reshape | solution.py:313
  49.8 6.6 %image.4.refs_0_ = bf16[16,256,256]{2,1,0:T(8,128)(2,1)S(1)} custom-call(s32[1]{0:T(128)} %bitcast.2.place_ref, bf16[8,2,256,128]{3,2,1,0:T(8,128)(2,1)S(1)} %pad_maximum_fusion.vis_ref, f32[2,8,128,128]{3,2,1,0:T(8,128)S(1)} %maximum_bitcast_fusion.step_c, f32[2,8,1024]{2,1,0:T(8,128)S(1)} %get-tuple-element.51.step_f, ...), custom_call_target="tpu_custom_call" | custom-call | flops 4294967296 | bytes 8388608 | tf_op jit(solution)/shard_map/image/pallas_call | solution.py:168
  57.5 6.6 %image.7.refs_3_ = bf16[16,256,256]{2,1,0:T(8,128)(2,1)S(1)} custom-call(s32[1]{0:T(128)} %bitcast.place_ref, bf16[8,2,256,128]{3,2,1,0:T(8,128)(2,1)S(1)} %pad_maximum_fusion.4.vis_ref, f32[2,8,128,128]{3,2,1,0:T(8,128)S(1)} %maximum_bitcast_fusion.step_c, f32[2,8,1024]{2,1,0:T(8,128)S(1)} %get-tuple-element.51.step_f, ...), custom_call_target="tpu_custom_call" | custom-call | flops 4294967296 | bytes 8388608 | tf_op jit(solution)/shard_map/image/pallas_call | solution.py:168
  65.2 6.6 %image.6.refs_2_ = bf16[16,256,256]{2,1,0:T(8,128)(2,1)S(1)} custom-call(s32[1]{0:T(128)} %bitcast.23.place_ref, bf16[8,2,256,128]{3,2,1,0:T(8,128)(2,1)S(1)} %pad_maximum_fusion.3.vis_ref, f32[2,8,128,128]{3,2,1,0:T(8,128)S(1)} %maximum_bitcast_fusion.step_c, f32[2,8,1024]{2,1,0:T(8,128)S(1)} %get-tuple-element.51.step_f, ...), custom_call_target="tpu_custom_call" | custom-call | flops 4294967296 | bytes 8388608 | tf_op jit(solution)/shard_map/image/pallas_call | solution.py:168
  72.9 6.6 %image.5.refs_1_ = bf16[16,256,256]{2,1,0:T(8,128)(2,1)S(1)} custom-call(s32[1]{0:T(128)} %bitcast.21.place_ref, bf16[8,2,256,128]{3,2,1,0:T(8,128)(2,1)S(1)} %pad_maximum_fusion.2.vis_ref, f32[2,8,128,128]{3,2,1,0:T(8,128)S(1)} %maximum_bitcast_fusion.step_c, f32[2,8,1024]{2,1,0:T(8,128)S(1)} %get-tuple-element.51.step_f, ...), custom_call_target="tpu_custom_call" | custom-call | flops 4294967296 | bytes 8388608 | tf_op jit(solution)/shard_map/image/pallas_call | solution.py:168
  79.5 10.8 %filter.1.image_ref = bf16[16,1024,256]{2,1,0:T(8,128)(2,1)} custom-call(s32[1]{0:T(128)} %bitcast.1.place_ref, bf16[1024,1024]{1,0:T(8,128)(2,1)S(1)} %copy-done.3, bf16[16,256,256]{2,1,0:T(8,128)(2,1)S(1)} %image.4.refs_0_, bf16[16,256,256]{2,1,0:T(8,128)(2,1)S(1)} %image.5.refs_1_, bf16[16,256,256]{2,1,0:T(8,128)(2,1)S(1)} %image.6.refs_2_, ...), custom_call_target="tpu_custom_call" | custom-call | flops 8589934592 | bytes 18874368 | tf_op jit(solution)/shard_map/filter/pallas_call | solution.py:205
  90.3 3.4 %copy-done.4 = bf16[16,1024,256]{2,1,0:T(8,128)(2,1)S(1)} copy-done((bf16[16,1024,256]{2,1,0:T(8,128)(2,1)S(1)}, bf16[16,1024,256]{2,1,0:T(8,128)(2,1)}, u32[]{:S(2)}) %copy-start.4) | copy-done | bytes 8388632
  93.7 9.3 %predict.4 = (f32[4,2,256,128]{3,2,1,0:T(8,128)S(1)}, bf16[4,2,256,128]{3,2,1,0:T(8,128)(2,1)S(1)}) custom-call(s32[1]{0:T(128)} %bitcast.place_ref, bf16[16,1024,256]{2,1,0:T(8,128)(2,1)S(1)} %copy-done.4, bf16[256,2048]{1,0:T(8,128)(2,1)S(1)} %copy-done.2, f32[2,8,128,128]{3,2,1,0:T(8,128)S(1)} %maximum_bitcast_fusion.step_c, ...), custom_call_target="tpu_custom_call" | custom-call | flops 4294967296 | bytes 8388608 | tf_op jit(solution)/shard_map/predict/pallas_call | solution.py:270
  103.0 9.1 %predict.5 = (f32[4,2,256,128]{3,2,1,0:T(8,128)S(1)}, bf16[4,2,256,128]{3,2,1,0:T(8,128)(2,1)S(1)}) custom-call(s32[1]{0:T(128)} %bitcast.23.place_ref, bf16[16,1024,256]{2,1,0:T(8,128)(2,1)S(1)} %copy-done.4, bf16[256,2048]{1,0:T(8,128)(2,1)S(1)} %copy-done.2, f32[2,8,128,128]{3,2,1,0:T(8,128)S(1)} %maximum_bitcast_fusion.step_c, ...), custom_call_target="tpu_custom_call" | custom-call | flops 4294967296 | bytes 8388608 | tf_op jit(solution)/shard_map/predict/pallas_call | solution.py:270
  112.7 9.1 %predict.6 = (f32[4,2,256,128]{3,2,1,0:T(8,128)S(1)}, bf16[4,2,256,128]{3,2,1,0:T(8,128)(2,1)S(1)}) custom-call(s32[1]{0:T(128)} %bitcast.21.place_ref, bf16[16,1024,256]{2,1,0:T(8,128)(2,1)S(1)} %copy-done.4, bf16[256,2048]{1,0:T(8,128)(2,1)S(1)} %copy-done.2, f32[2,8,128,128]{3,2,1,0:T(8,128)S(1)} %maximum_bitcast_fusion.step_c, ...), custom_call_target="tpu_custom_call" | custom-call | flops 4294967296 | bytes 8388608 | tf_op jit(solution)/shard_map/predict/pallas_call | solution.py:270
  122.4 3.4 %copy-done.5 = bf16[16,1024,256]{2,1,0:T(8,128)(2,1)S(1)} copy-done((bf16[16,1024,256]{2,1,0:T(8,128)(2,1)S(1)}, bf16[16,1024,256]{2,1,0:T(8,128)(2,1)}, u32[]{:S(2)}) %copy-start.5) | copy-done | bytes 8388632
  125.7 9.1 %predict.7 = (f32[4,2,256,128]{3,2,1,0:T(8,128)S(1)}, bf16[4,2,256,128]{3,2,1,0:T(8,128)(2,1)S(1)}) custom-call(s32[1]{0:T(128)} %bitcast.29.place_ref, bf16[16,1024,256]{2,1,0:T(8,128)(2,1)S(1)} %copy-done.5, bf16[256,2048]{1,0:T(8,128)(2,1)S(1)} %copy-done.2, f32[2,8,128,128]{3,2,1,0:T(8,128)S(1)} %maximum_bitcast_fusion.step_c, ...), custom_call_target="tpu_custom_call" | custom-call | flops 4294967296 | bytes 8388608 | tf_op jit(solution)/shard_map/predict/pallas_call | solution.py:270
  136.0 1.4 collective-permute-start.20
  138.5 1.4 collective-permute-start.28
  139.9 1.7 %collective-permute-done.16 = bf16[2,2,256,128]{3,2,1,0:T(8,128)(2,1)S(1)} collective-permute-done((bf16[2,2,256,128]{3,2,1,0:T(8,128)(2,1)S(1)}, bf16[2,2,256,128]{3,2,1,0:T(8,128)(2,1)S(1)}, u32[]{:S(2)}, u32[]{:S(2)}) %collective-permute-start.16) | collective-permute-done | bytes 262176 | tf_op jit(solution)/shard_map/ppermute | solution.py:63
  142.3 2.4 %collective-permute-done.20 = bf16[2,2,256,128]{3,2,1,0:T(8,128)(2,1)S(1)} collective-permute-done((bf16[2,2,256,128]{3,2,1,0:T(8,128)(2,1)S(1)}, bf16[2,2,256,128]{3,2,1,0:T(8,128)(2,1)S(1)}, u32[]{:S(2)}, u32[]{:S(2)}) %collective-permute-start.20) | collective-permute-done | bytes 262176 | tf_op jit(solution)/shard_map/ppermute | solution.py:63
  145.7 4.3 %collective-permute-done.24 = bf16[2,2,256,128]{3,2,1,0:T(8,128)(2,1)S(1)} collective-permute-done((bf16[2,2,256,128]{3,2,1,0:T(8,128)(2,1)S(1)}, bf16[2,2,256,128]{3,2,1,0:T(8,128)(2,1)S(1)}, u32[]{:S(2)}, u32[]{:S(2)}) %collective-permute-start.24) | collective-permute-done | bytes 262176 | tf_op jit(solution)/shard_map/ppermute | solution.py:63
  150.8 3.4 %collective-permute-done.28 = bf16[2,2,256,128]{3,2,1,0:T(8,128)(2,1)S(1)} collective-permute-done((bf16[2,2,256,128]{3,2,1,0:T(8,128)(2,1)S(1)}, bf16[2,2,256,128]{3,2,1,0:T(8,128)(2,1)S(1)}, u32[]{:S(2)}, u32[]{:S(2)}) %collective-permute-start.28) | collective-permute-done | bytes 262176 | tf_op jit(solution)/shard_map/ppermute | solution.py:63
  155.0 2.5 %collective-permute-start.18 = (bf16[2,256,128]{2,1,0:T(8,128)(2,1)S(1)}, bf16[2,256,128]{2,1,0:T(8,128)(2,1)S(1)}, u32[]{:S(2)}, u32[]{:S(2)}) collective-permute-start(bf16[2,256,128]{2,1,0:T(8,128)(2,1)S(1)} %fusion.8), channel_id=1, source_target_pairs={{0,8},{8,16},{16,24},{24,0},{1,9},{9,17},{17,25},{25,1},{2,10},{10... | collective-permute-start | bytes 393224 | tf_op jit(solution)/shard_map/ppermute | solution.py:330
  158.6 1.5 collective-permute-start.26
  160.2 2.7 %collective-permute-done.18 = bf16[2,256,128]{2,1,0:T(8,128)(2,1)S(1)} collective-permute-done((bf16[2,256,128]{2,1,0:T(8,128)(2,1)S(1)}, bf16[2,256,128]{2,1,0:T(8,128)(2,1)S(1)}, u32[]{:S(2)}, u32[]{:S(2)}) %collective-permute-start.18) | collective-permute-done | bytes 131104 | tf_op jit(solution)/shard_map/ppermute | solution.py:330
  162.9 4.1 %collective-permute-done.22 = bf16[2,256,128]{2,1,0:T(8,128)(2,1)S(1)} collective-permute-done((bf16[2,256,128]{2,1,0:T(8,128)(2,1)S(1)}, bf16[2,256,128]{2,1,0:T(8,128)(2,1)S(1)}, u32[]{:S(2)}, u32[]{:S(2)}) %collective-permute-start.22) | collective-permute-done | bytes 131104 | tf_op jit(solution)/shard_map/ppermute | solution.py:330
  (162 shorter events, 37.0 us)
Async XLA Ops:
  3.4 18.5 %collective-permute-start.11 = (bf16[2,256,128]{2,1,0:T(8,128)(2,1)}, bf16[2,256,128]{2,1,0:T(8,128)(2,1)}, u32[]{:S(2)}, u32[]{:S(2)}) collective-permute-start(bf16[2,256,128]{2,1,0:T(8,128)(2,1)} %get-tuple-element.23), channel_id=1, source_target_pairs={{0,24},{8,0},{16,8},{24,16},{1,25},{9,1},{17,9},{25,17},{2,26},{10... | collective-permute-start | bytes 393224 | tf_op jit(solution)/shard_map/ppermute | solution.py:300
  8.5 14.0 %collective-permute-start.7 = (bf16[2,256,128]{2,1,0:T(8,128)(2,1)}, bf16[2,256,128]{2,1,0:T(8,128)(2,1)}, u32[]{:S(2)}, u32[]{:S(2)}) collective-permute-start(bf16[2,256,128]{2,1,0:T(8,128)(2,1)} %get-tuple-element.23), channel_id=1, source_target_pairs={{0,16},{8,24},{16,0},{24,8},{1,17},{9,25},{17,1},{25,9},{2,18},{10... | collective-permute-start | bytes 393224 | tf_op jit(solution)/shard_map/ppermute | solution.py:300
  8.5 19.1 %collective-permute-start.3 = (bf16[2,256,128]{2,1,0:T(8,128)(2,1)}, bf16[2,256,128]{2,1,0:T(8,128)(2,1)S(1)}, u32[]{:S(2)}, u32[]{:S(2)}) collective-permute-start(bf16[2,256,128]{2,1,0:T(8,128)(2,1)} %get-tuple-element.23), channel_id=1, source_target_pairs={{0,8},{8,16},{16,24},{24,0},{1,9},{9,17},{17,25},{25,1},{2,10},{10... | collective-permute-start | bytes 393224 | tf_op jit(solution)/shard_map/ppermute | solution.py:300
  9.5 14.5 %collective-permute-start = (bf16[1,2,256,128]{3,2,1,0:T(8,128)(2,1)S(1)}, bf16[1,2,256,128]{3,2,1,0:T(8,128)(2,1)}, u32[]{:S(2)}, u32[]{:S(2)}) collective-permute-start(bf16[1,2,256,128]{3,2,1,0:T(8,128)(2,1)S(1)} %get-tuple-element.24), channel_id=1, source_target_pairs={{0,2},{1,5},{2,0},{3,7},{4,6},{5,1},{6,4},{7,3},{8,10},{9,13},{10,... | collective-permute-start | bytes 393224 | tf_op jit(solution)/shard_map/ppermute | solution.py:53
  21.9 6.6 %collective-permute-start.12 = (bf16[1,2,256,128]{3,2,1,0:T(8,128)(2,1)}, bf16[1,2,256,128]{3,2,1,0:T(8,128)(2,1)S(1)}, u32[]{:S(2)}, u32[]{:S(2)}) collective-permute-start(bf16[1,2,256,128]{3,2,1,0:T(8,128)(2,1)} %bitcast.25), channel_id=1, source_target_pairs={{0,2},{1,5},{2,0},{3,7},{4,6},{5,1},{6,4},{7,3},{8,10},{9,13},{10,... | collective-permute-start | bytes 393224 | tf_op jit(solution)/shard_map/ppermute | solution.py:53
  22.5 9.3 %collective-permute-start.8 = (bf16[1,2,256,128]{3,2,1,0:T(8,128)(2,1)}, bf16[1,2,256,128]{3,2,1,0:T(8,128)(2,1)S(1)}, u32[]{:S(2)}, u32[]{:S(2)}) collective-permute-start(bf16[1,2,256,128]{3,2,1,0:T(8,128)(2,1)} %bitcast.24), channel_id=1, source_target_pairs={{0,2},{1,5},{2,0},{3,7},{4,6},{5,1},{6,4},{7,3},{8,10},{9,13},{10,... | collective-permute-start | bytes 393224 | tf_op jit(solution)/shard_map/ppermute | solution.py:53
  24.9 9.0 %collective-permute-start.1 = (bf16[2,2,256,128]{3,2,1,0:T(8,128)(2,1)S(1)}, bf16[2,2,256,128]{3,2,1,0:T(8,128)(2,1)S(1)}, u32[]{:S(2)}, u32[]{:S(2)}) collective-permute-start(bf16[2,2,256,128]{3,2,1,0:T(8,128)(2,1)S(1)} %pad_maximum_fusion.10), channel_id=1, source_target_pairs={{0,4},{1,3},{2,6},{3,1},{4,0},{5,7},{6,2},{7,5},{8,12},{9,11},{10,... | collective-permute-start | bytes 786440 | tf_op jit(solution)/shard_map/ppermute | solution.py:53
  27.6 8.1 %collective-permute-start.4 = (bf16[1,2,256,128]{3,2,1,0:T(8,128)(2,1)S(1)}, bf16[1,2,256,128]{3,2,1,0:T(8,128)(2,1)S(1)}, u32[]{:S(2)}, u32[]{:S(2)}) collective-permute-start(bf16[1,2,256,128]{3,2,1,0:T(8,128)(2,1)S(1)} %bitcast.105), channel_id=1, source_target_pairs={{0,2},{1,5},{2,0},{3,7},{4,6},{5,1},{6,4},{7,3},{8,10},{9,13},{10,... | collective-permute-start | bytes 393224 | tf_op jit(solution)/shard_map/ppermute | solution.py:53
  30.2 14.4 %collective-permute-start.13 = (bf16[2,2,256,128]{3,2,1,0:T(8,128)(2,1)}, bf16[2,2,256,128]{3,2,1,0:T(8,128)(2,1)}, u32[]{:S(2)}, u32[]{:S(2)}) collective-permute-start(bf16[2,2,256,128]{3,2,1,0:T(8,128)(2,1)} %pad_maximum_fusion.13), channel_id=1, source_target_pairs={{0,4},{1,3},{2,6},{3,1},{4,0},{5,7},{6,2},{7,5},{8,12},{9,11},{10,... | collective-permute-start | bytes 786440 | tf_op jit(solution)/shard_map/ppermute | solution.py:53
  33.4 12.4 %collective-permute-start.9 = (bf16[2,2,256,128]{3,2,1,0:T(8,128)(2,1)}, bf16[2,2,256,128]{3,2,1,0:T(8,128)(2,1)}, u32[]{:S(2)}, u32[]{:S(2)}) collective-permute-start(bf16[2,2,256,128]{3,2,1,0:T(8,128)(2,1)} %pad_maximum_fusion.12), channel_id=1, source_target_pairs={{0,4},{1,3},{2,6},{3,1},{4,0},{5,7},{6,2},{7,5},{8,12},{9,11},{10,... | collective-permute-start | bytes 786440 | tf_op jit(solution)/shard_map/ppermute | solution.py:53
  35.7 12.9 %collective-permute-start.2 = (bf16[4,2,256,128]{3,2,1,0:T(8,128)(2,1)}, bf16[4,2,256,128]{3,2,1,0:T(8,128)(2,1)}, u32[]{:S(2)}, u32[]{:S(2)}) collective-permute-start(bf16[4,2,256,128]{3,2,1,0:T(8,128)(2,1)} %pad_maximum_fusion.6), channel_id=1, source_target_pairs={{0,1},{1,0},{2,3},{3,2},{4,5},{5,4},{6,7},{7,6},{8,9},{9,8},{10,11... | collective-permute-start | bytes 1572872 | tf_op jit(solution)/shard_map/ppermute | solution.py:54
  36.5 11.0 %collective-permute-start.5 = (bf16[2,2,256,128]{3,2,1,0:T(8,128)(2,1)}, bf16[2,2,256,128]{3,2,1,0:T(8,128)(2,1)}, u32[]{:S(2)}, u32[]{:S(2)}) collective-permute-start(bf16[2,2,256,128]{3,2,1,0:T(8,128)(2,1)} %pad_maximum_fusion.11), channel_id=1, source_target_pairs={{0,4},{1,3},{2,6},{3,1},{4,0},{5,7},{6,2},{7,5},{8,12},{9,11},{10,... | collective-permute-start | bytes 786440 | tf_op jit(solution)/shard_map/ppermute | solution.py:53
  45.8 10.6 %collective-permute-start.14 = (bf16[4,2,256,128]{3,2,1,0:T(8,128)(2,1)S(1)}, bf16[4,2,256,128]{3,2,1,0:T(8,128)(2,1)S(1)}, u32[]{:S(2)}, u32[]{:S(2)}) collective-permute-start(bf16[4,2,256,128]{3,2,1,0:T(8,128)(2,1)S(1)} %pad_maximum_fusion.9), channel_id=1, source_target_pairs={{0,1},{1,0},{2,3},{3,2},{4,5},{5,4},{6,7},{7,6},{8,9},{9,8},{10,11... | collective-permute-start | bytes 1572872 | tf_op jit(solution)/shard_map/ppermute | solution.py:54
  47.0 17.2 %collective-permute-start.10 = (bf16[4,2,256,128]{3,2,1,0:T(8,128)(2,1)S(1)}, bf16[4,2,256,128]{3,2,1,0:T(8,128)(2,1)S(1)}, u32[]{:S(2)}, u32[]{:S(2)}) collective-permute-start(bf16[4,2,256,128]{3,2,1,0:T(8,128)(2,1)S(1)} %pad_maximum_fusion.8), channel_id=1, source_target_pairs={{0,1},{1,0},{2,3},{3,2},{4,5},{5,4},{6,7},{7,6},{8,9},{9,8},{10,11... | collective-permute-start | bytes 1572872 | tf_op jit(solution)/shard_map/ppermute | solution.py:54
  48.5 23.3 %collective-permute-start.6 = (bf16[4,2,256,128]{3,2,1,0:T(8,128)(2,1)S(1)}, bf16[4,2,256,128]{3,2,1,0:T(8,128)(2,1)S(1)}, u32[]{:S(2)}, u32[]{:S(2)}) collective-permute-start(bf16[4,2,256,128]{3,2,1,0:T(8,128)(2,1)S(1)} %pad_maximum_fusion.7), channel_id=1, source_target_pairs={{0,1},{1,0},{2,3},{3,2},{4,5},{5,4},{6,7},{7,6},{8,9},{9,8},{10,11... | collective-permute-start | bytes 1572872 | tf_op jit(solution)/shard_map/ppermute | solution.py:54
  112.1 22.8 %collective-permute-start.15 = (bf16[4,2,256,128]{3,2,1,0:T(8,128)(2,1)S(1)}, bf16[4,2,256,128]{3,2,1,0:T(8,128)(2,1)S(1)}, u32[]{:S(2)}, u32[]{:S(2)}) collective-permute-start(bf16[4,2,256,128]{3,2,1,0:T(8,128)(2,1)S(1)} %get-tuple-element.14), channel_id=1, source_target_pairs={{0,1},{1,0},{2,3},{3,2},{4,5},{5,4},{6,7},{7,6},{8,9},{9,8},{10,11... | collective-permute-start | bytes 1572872 | tf_op jit(solution)/shard_map/ppermute | solution.py:59
  121.8 14.1 %collective-permute-start.19 = (bf16[4,2,256,128]{3,2,1,0:T(8,128)(2,1)S(1)}, bf16[4,2,256,128]{3,2,1,0:T(8,128)(2,1)S(1)}, u32[]{:S(2)}, u32[]{:S(2)}) collective-permute-start(bf16[4,2,256,128]{3,2,1,0:T(8,128)(2,1)S(1)} %get-tuple-element.16), channel_id=1, source_target_pairs={{0,1},{1,0},{2,3},{3,2},{4,5},{5,4},{6,7},{7,6},{8,9},{9,8},{10,11... | collective-permute-start | bytes 1572872 | tf_op jit(solution)/shard_map/ppermute | solution.py:59
  121.9 15.6 %collective-permute-start.23 = (bf16[4,2,256,128]{3,2,1,0:T(8,128)(2,1)S(1)}, bf16[4,2,256,128]{3,2,1,0:T(8,128)(2,1)S(1)}, u32[]{:S(2)}, u32[]{:S(2)}) collective-permute-start(bf16[4,2,256,128]{3,2,1,0:T(8,128)(2,1)S(1)} %get-tuple-element.18), channel_id=1, source_target_pairs={{0,1},{1,0},{2,3},{3,2},{4,5},{5,4},{6,7},{7,6},{8,9},{9,8},{10,11... | collective-permute-start | bytes 1572872 | tf_op jit(solution)/shard_map/ppermute | solution.py:59
  134.9 3.5 %collective-permute-start.27 = (bf16[4,2,256,128]{3,2,1,0:T(8,128)(2,1)S(1)}, bf16[4,2,256,128]{3,2,1,0:T(8,128)(2,1)S(1)}, u32[]{:S(2)}, u32[]{:S(2)}) collective-permute-start(bf16[4,2,256,128]{3,2,1,0:T(8,128)(2,1)S(1)} %get-tuple-element.20), channel_id=1, source_target_pairs={{0,1},{1,0},{2,3},{3,2},{4,5},{5,4},{6,7},{7,6},{8,9},{9,8},{10,11... | collective-permute-start | bytes 1572872 | tf_op jit(solution)/shard_map/ppermute | solution.py:59
  135.1 6.4 %collective-permute-start.16 = (bf16[2,2,256,128]{3,2,1,0:T(8,128)(2,1)S(1)}, bf16[2,2,256,128]{3,2,1,0:T(8,128)(2,1)S(1)}, u32[]{:S(2)}, u32[]{:S(2)}) collective-permute-start(bf16[2,2,256,128]{3,2,1,0:T(8,128)(2,1)S(1)} %slice.133), channel_id=1, source_target_pairs={{0,4},{1,3},{2,6},{3,1},{4,0},{5,7},{6,2},{7,5},{8,12},{9,11},{10,... | collective-permute-start | bytes 786440 | tf_op jit(solution)/shard_map/ppermute | solution.py:63
  136.0 8.7 %collective-permute-start.20 = (bf16[2,2,256,128]{3,2,1,0:T(8,128)(2,1)S(1)}, bf16[2,2,256,128]{3,2,1,0:T(8,128)(2,1)S(1)}, u32[]{:S(2)}, u32[]{:S(2)}) collective-permute-start(bf16[2,2,256,128]{3,2,1,0:T(8,128)(2,1)S(1)} %slice.132), channel_id=1, source_target_pairs={{0,4},{1,3},{2,6},{3,1},{4,0},{5,7},{6,2},{7,5},{8,12},{9,11},{10,... | collective-permute-start | bytes 786440 | tf_op jit(solution)/shard_map/ppermute | solution.py:63
  137.6 12.4 %collective-permute-start.24 = (bf16[2,2,256,128]{3,2,1,0:T(8,128)(2,1)S(1)}, bf16[2,2,256,128]{3,2,1,0:T(8,128)(2,1)S(1)}, u32[]{:S(2)}, u32[]{:S(2)}) collective-permute-start(bf16[2,2,256,128]{3,2,1,0:T(8,128)(2,1)S(1)} %slice.131), channel_id=1, source_target_pairs={{0,4},{1,3},{2,6},{3,1},{4,0},{5,7},{6,2},{7,5},{8,12},{9,11},{10,... | collective-permute-start | bytes 786440 | tf_op jit(solution)/shard_map/ppermute | solution.py:63
  138.5 15.7 %collective-permute-start.28 = (bf16[2,2,256,128]{3,2,1,0:T(8,128)(2,1)S(1)}, bf16[2,2,256,128]{3,2,1,0:T(8,128)(2,1)S(1)}, u32[]{:S(2)}, u32[]{:S(2)}) collective-permute-start(bf16[2,2,256,128]{3,2,1,0:T(8,128)(2,1)S(1)} %slice.130), channel_id=1, source_target_pairs={{0,4},{1,3},{2,6},{3,1},{4,0},{5,7},{6,2},{7,5},{8,12},{9,11},{10,... | collective-permute-start | bytes 786440 | tf_op jit(solution)/shard_map/ppermute | solution.py:63
  141.6 13.4 %collective-permute-start.17 = (bf16[1,2,256,128]{3,2,1,0:T(8,128)(2,1)S(1)}, bf16[1,2,256,128]{3,2,1,0:T(8,128)(2,1)S(1)}, u32[]{:S(2)}, u32[]{:S(2)}) collective-permute-start(bf16[1,2,256,128]{3,2,1,0:T(8,128)(2,1)S(1)} %slice.137), channel_id=1, source_target_pairs={{0,2},{1,5},{2,0},{3,7},{4,6},{5,1},{6,4},{7,3},{8,10},{9,13},{10,... | collective-permute-start | bytes 393224 | tf_op jit(solution)/shard_map/ppermute | solution.py:63
  144.8 15.3 %copy-start.20 = (bf16[128,256]{1,0:T(8,128)(2,1)S(1)}, bf16[128,256]{1,0:T(8,128)(2,1)}, u32[]{:S(2)}) copy-start(bf16[128,256]{1,0:T(8,128)(2,1)} %copy-done.19) | copy-start | bytes 196612
  144.9 12.7 %collective-permute-start.21 = (bf16[1,2,256,128]{3,2,1,0:T(8,128)(2,1)S(1)}, bf16[1,2,256,128]{3,2,1,0:T(8,128)(2,1)S(1)}, u32[]{:S(2)}, u32[]{:S(2)}) collective-permute-start(bf16[1,2,256,128]{3,2,1,0:T(8,128)(2,1)S(1)} %slice.136), channel_id=1, source_target_pairs={{0,2},{1,5},{2,0},{3,7},{4,6},{5,1},{6,4},{7,3},{8,10},{9,13},{10,... | collective-permute-start | bytes 393224 | tf_op jit(solution)/shard_map/ppermute | solution.py:63
  150.1 8.5 %collective-permute-start.25 = (bf16[1,2,256,128]{3,2,1,0:T(8,128)(2,1)S(1)}, bf16[1,2,256,128]{3,2,1,0:T(8,128)(2,1)S(1)}, u32[]{:S(2)}, u32[]{:S(2)}) collective-permute-start(bf16[1,2,256,128]{3,2,1,0:T(8,128)(2,1)S(1)} %slice.135), channel_id=1, source_target_pairs={{0,2},{1,5},{2,0},{3,7},{4,6},{5,1},{6,4},{7,3},{8,10},{9,13},{10,... | collective-permute-start | bytes 393224 | tf_op jit(solution)/shard_map/ppermute | solution.py:63
  154.2 13.7 %copy-start.1 = (s32[1024]{0:T(1024)S(1)}, s32[1024]{0:T(1024)}, u32[]{:S(2)}) copy-start(s32[1024]{0:T(1024)} %param.9) | copy-start | bytes 12292
  154.3 5.9 %collective-permute-start.29 = (bf16[1,2,256,128]{3,2,1,0:T(8,128)(2,1)S(1)}, bf16[1,2,256,128]{3,2,1,0:T(8,128)(2,1)S(1)}, u32[]{:S(2)}, u32[]{:S(2)}) collective-permute-start(bf16[1,2,256,128]{3,2,1,0:T(8,128)(2,1)S(1)} %slice.134), channel_id=1, source_target_pairs={{0,2},{1,5},{2,0},{3,7},{4,6},{5,1},{6,4},{7,3},{8,10},{9,13},{10,... | collective-permute-start | bytes 393224 | tf_op jit(solution)/shard_map/ppermute | solution.py:63
  155.0 7.9 %collective-permute-start.18 = (bf16[2,256,128]{2,1,0:T(8,128)(2,1)S(1)}, bf16[2,256,128]{2,1,0:T(8,128)(2,1)S(1)}, u32[]{:S(2)}, u32[]{:S(2)}) collective-permute-start(bf16[2,256,128]{2,1,0:T(8,128)(2,1)S(1)} %fusion.8), channel_id=1, source_target_pairs={{0,8},{8,16},{16,24},{24,0},{1,9},{9,17},{17,25},{25,1},{2,10},{10... | collective-permute-start | bytes 393224 | tf_op jit(solution)/shard_map/ppermute | solution.py:330
  157.6 9.4 %collective-permute-start.22 = (bf16[2,256,128]{2,1,0:T(8,128)(2,1)S(1)}, bf16[2,256,128]{2,1,0:T(8,128)(2,1)S(1)}, u32[]{:S(2)}, u32[]{:S(2)}) collective-permute-start(bf16[2,256,128]{2,1,0:T(8,128)(2,1)S(1)} %fusion.9), channel_id=1, source_target_pairs={{0,16},{8,24},{16,0},{24,8},{1,17},{9,25},{17,1},{25,9},{2,18},{10... | collective-permute-start | bytes 393224 | tf_op jit(solution)/shard_map/ppermute | solution.py:330
  158.6 8.4 %collective-permute-start.26 = (bf16[2,256,128]{2,1,0:T(8,128)(2,1)S(1)}, bf16[2,256,128]{2,1,0:T(8,128)(2,1)S(1)}, u32[]{:S(2)}, u32[]{:S(2)}) collective-permute-start(bf16[2,256,128]{2,1,0:T(8,128)(2,1)S(1)} %fusion.10), channel_id=1, source_target_pairs={{0,24},{8,0},{16,8},{24,16},{1,25},{9,1},{17,9},{25,17},{2,26},{10... | collective-permute-start | bytes 393224 | tf_op jit(solution)/shard_map/ppermute | solution.py:330
  (24 other events, 155.6 us)

commit v2 on v1

v2 whole, which is shorter than its diff:
```python
import functools
import math

import jax
import jax.numpy as jnp
import numpy as np
from jax import lax
from jax.experimental import pallas as pl
from jax.experimental.pallas import tpu as pltpu
from jax.sharding import PartitionSpec as P

F = 1024
L = 512
M = 256

TWO_PI = 2.0 * math.pi
FINE = 8
LANES = 128
A_CHANS = 16
C_CHANS = 64
C_UNIT = 16
C_SLOTS = 2
F32 = jnp.float32
BF16 = jnp.bfloat16


def chip_masks(tiles):
    return [mask for mask in range(0, tiles, 2)]


def tile_swap(block, tiles, mask):
    return lax.ppermute(block, "tile", [(t, t ^ mask) for t in range(tiles)])


def chan_shift(block, groups, away):
    return lax.ppermute(block, "chan", [(c, (c + away) % groups) for c in range(groups)])


def after(value, *others):
    return lax.optimization_barrier((value, *others))[0]


def unit(turns, period):
    angle = (turns % period).astype(F32) * (TWO_PI / period)
    return jnp.cos(angle), jnp.sin(angle)


def times(a, b):
    return a[0] * b[0] - a[1] * b[1], a[1] * b[0] + a[0] * b[1]


def conj_times(a, b):
    return a[0] * b[0] + a[1] * b[1], a[1] * b[0] - a[0] * b[1]


def column_tables(v_rows):
    digit = 16
    high = unit(v_rows[None, :] * (digit * jnp.arange(M // digit, dtype=jnp.int32))[:, None], 2 * M)
    low = unit(v_rows[None, :] * jnp.arange(digit, dtype=jnp.int32)[:, None], 2 * M)
    both = times(
        (high[0][:, None, :], high[1][:, None, :]), (low[0][None, :, :], low[1][None, :, :])
    )
    return [part.reshape(M, -1).astype(BF16) for part in both]


def phase_tables(scaled_rows, period):
    groups = F // FINE
    digit = 16
    high_ids = F + FINE * digit * jnp.arange(groups // digit, dtype=jnp.int32)
    high = unit(scaled_rows[None, :] * high_ids[:, None], period)
    low = unit(
        scaled_rows[None, :] * (FINE * jnp.arange(digit, dtype=jnp.int32))[:, None], period
    )
    coarse = times(
        (high[0][:, None, :], high[1][:, None, :]), (low[0][None, :, :], low[1][None, :, :])
    )
    fine = unit(scaled_rows[None, :] * jnp.arange(FINE, dtype=jnp.int32)[:, None], period)
    coarse = jnp.stack([part.reshape(groups, -1, LANES) for part in coarse])
    fine = jnp.stack([part.reshape(FINE, -1, LANES) for part in fine])
    return jnp.transpose(coarse, (0, 2, 1, 3)), jnp.transpose(fine, (0, 2, 1, 3))


def phases(coarse_ref, fine_ref, group, chans, block):
    fine = (fine_ref[0, block], fine_ref[1, block])
    parts = []
    for step in range(chans // FINE):
        row = pl.ds(group + step, FINE, stride=0)
        coarse = (coarse_ref[0, block, row, :], coarse_ref[1, block, row, :])
        parts.append(times(coarse, fine))
    return (
        jnp.concatenate([part[0] for part in parts], 0),
        jnp.concatenate([part[1] for part in parts], 0),
    )


def paired(count, first, second):
    first(0, 0)

    def body(pair, carry):
        first(2 * pair + 1, 1)
        second(2 * pair, 0)
        first(jnp.minimum(2 * pair + 2, count - 1), 0)
        second(2 * pair + 1, 1)
        return carry

    lax.fori_loop(0, count // 2, body, 0)


def image_kernel(scale, lines, blocks, place_ref, step_c, step_f, start_c, start_f, col_ref, *refs):
    vis_refs, out_ref, slots = refs[:blocks], refs[blocks], refs[blocks + 1 :]
    chans = out_ref.shape[1]
    base = place_ref[0]

    def fill(i, slot):
        x_ref = slots[slot]
        rows = pl.ds(pl.multiple_of(i * A_CHANS, A_CHANS), A_CHANS)
        group = base + i * (A_CHANS // FINE)
        for block in range(blocks):
            step = phases(step_c, step_f, group, A_CHANS, block)
            start = phases(start_c, start_f, group, A_CHANS, block)
            vis_ref = vis_refs[block]
            value = conj_times((vis_ref[0, rows, :].astype(F32), -vis_ref[1, rows, :].astype(F32)), start)
            at = block * 2 * LANES
            for line in range(lines):
                into = slice(line * A_CHANS, (line + 1) * A_CHANS)
                x_ref[into, at : at + LANES] = value[0].astype(BF16)
                x_ref[into, at + LANES : at + 2 * LANES] = value[1].astype(BF16)
                if line < lines - 1:
                    value = conj_times(value, step)

    def multiply(i, slot):
        rows = pl.ds(pl.multiple_of(i * A_CHANS, A_CHANS), A_CHANS)
        image = jnp.dot(slots[slot][...], col_ref[...], preferred_element_type=F32)
        out_ref[:, rows, :] = (image * scale).astype(BF16).reshape(lines, A_CHANS, M)

    paired(chans // A_CHANS, fill, multiply)


def make_image(vis, place, step_t, start_t, col, lines, total_rows):
    blocks = len(vis)
    _, chans, _ = vis[0].shape
    rows = blocks * LANES
    vmem = pl.BlockSpec(memory_space=pltpu.VMEM)
    flops = 2 * lines * chans * 2 * rows * M
    return pl.pallas_call(
        functools.partial(image_kernel, 1.0 / math.sqrt(total_rows), lines, blocks),
        out_shape=jax.ShapeDtypeStruct((lines, chans, M), BF16),
        in_specs=[pl.BlockSpec(memory_space=pltpu.SMEM)] + [vmem] * (5 + blocks),
        out_specs=vmem,
        scratch_shapes=[pltpu.VMEM((lines * A_CHANS, 2 * rows), BF16)] * 2,
        compiler_params=pltpu.CompilerParams(vmem_limit_bytes=40 << 20),
        cost_estimate=pl.CostEstimate(flops=flops, bytes_accessed=8 << 20, transcendentals=0),
        name="image",
    )(place, *step_t, *start_t, col, *vis)


def filter_kernel(groups, chans, place_ref, filter_ref, *refs):
    image_refs, out_refs = refs[:groups], refs[groups:]
    lines = out_refs[0].shape[0]
    place = place_ref[0]
    whole = []
    for out_block in range(groups):
        rows = pl.ds(pl.multiple_of(lax.rem(place + out_block, groups) * chans, chans), chans)
        pieces = []
        for in_block in range(groups):
            at = lax.rem(place + (groups - in_block), groups) * chans
            pieces.append(filter_ref[rows, pl.ds(pl.multiple_of(at, chans), chans)])
        whole.append(jnp.concatenate(pieces, 1))
    weights = jnp.concatenate(whole, 0)
    image = jnp.concatenate(
        [jnp.concatenate([ref[line] for line in range(lines)], 1) for ref in image_refs], 0
    )
    result = jnp.dot(weights, image, preferred_element_type=F32).astype(BF16)
    for block, out_ref in enumerate(out_refs):
        for line in range(lines):
            out_ref[line] = result[block * chans : (block + 1) * chans, line * M : (line + 1) * M]


def filter_images(images, place, fg_filter):
    groups = len(images)
    lines, chans, _ = images[0].shape
    step = min(4, lines)
    return pl.pallas_call(
        functools.partial(filter_kernel, groups, chans),
        out_shape=[jax.ShapeDtypeStruct((lines, chans, M), BF16)] * groups,
        grid=(lines // step,),
        in_specs=[
            pl.BlockSpec(memory_space=pltpu.SMEM),
            pl.BlockSpec((F, F), lambda i: (0, 0), pipeline_mode=pl.Buffered(1)),
        ]
        + [pl.BlockSpec((step, chans, M), lambda i: (i, 0, 0))] * groups,
        out_specs=[pl.BlockSpec((step, chans, M), lambda i: (i, 0, 0))] * groups,
        compiler_params=pltpu.CompilerParams(vmem_limit_bytes=40 << 20),
        cost_estimate=pl.CostEstimate(
            flops=2 * F * F * lines * M, bytes_accessed=18 << 20, transcendentals=0
        ),
        name="filter",
    )(place, fg_filter, *images)


def predict_kernel(scale, place_ref, image_ref, col_ref, step_c, step_f, start_c, start_f, keep_ref, send_ref, *slots):
    lines, chans, _ = image_ref.shape
    blocks = 2 * keep_ref.shape[0]
    count = chans // C_CHANS
    base = place_ref[0]

    def rows_of(i):
        return pl.ds(pl.multiple_of(i * C_CHANS, C_CHANS), C_CHANS)

    def multiply(i, slot, block):
        image = image_ref[:, rows_of(i), :].reshape(lines * C_CHANS, M)
        at = slice(block * 2 * LANES, (block + 1) * 2 * LANES)
        slots[slot][...] = jnp.dot(image, col_ref[:, at], preferred_element_type=F32)

    def collect(i, slot, block):
        h_ref = slots[slot]
        rows = rows_of(i)
        for first in range(0, C_CHANS, C_UNIT):
            group = base + i * (C_CHANS // FINE) + first // FINE
            step = phases(step_c, step_f, group, C_UNIT, block)
            start = phases(start_c, start_f, group, C_UNIT, block)
            total = None
            for line in reversed(range(lines)):
                take = slice(line * C_CHANS + first, line * C_CHANS + first + C_UNIT)
                value = (h_ref[take, :LANES], h_ref[take, LANES:])
                if total is None:
                    total = value
                else:
                    moved = times(total, step)
                    total = (moved[0] + value[0], moved[1] + value[1])
            total = times(total, start)
            real, imag = total[0] * scale, total[1] * -scale
            into = pl.ds(pl.multiple_of(i * C_CHANS + first, C_UNIT), C_UNIT)
            if block < blocks // 2:
                keep_ref[block, 0, into, :] = real
                keep_ref[block, 1, into, :] = imag
            else:
                send_ref[block - blocks // 2, 0, into, :] = real.astype(BF16)
                send_ref[block - blocks // 2, 1, into, :] = imag.astype(BF16)

    def body(i, carry):
        for block in range(blocks):
            if block < blocks - 1:
                multiply(i, (block + 1) % len(slots), block + 1)
            else:
                multiply(jnp.minimum(i + 1, count - 1), 0, 0)
            collect(i, block % len(slots), block)
        return carry

    multiply(0, 0, 0)
    lax.fori_loop(0, count, body, 0)


def predict_part(foreground, place, step_t, start_t, col):
    lines, chans, _ = foreground.shape
    rows = col.shape[1] // 2
    vmem = pl.BlockSpec(memory_space=pltpu.VMEM)
    flops = 2 * lines * chans * 2 * rows * M
    half = (rows // LANES // 2, 2, chans, LANES)
    return pl.pallas_call(
        functools.partial(predict_kernel, 1.0 / math.sqrt(L * M)),
        out_shape=(jax.ShapeDtypeStruct(half, F32), jax.ShapeDtypeStruct(half, BF16)),
        in_specs=[pl.BlockSpec(memory_space=pltpu.SMEM)] + [vmem] * 6,
        out_specs=(vmem, vmem),
        scratch_shapes=[pltpu.VMEM((lines * C_CHANS, 2 * LANES), F32)] * C_SLOTS,
        compiler_params=pltpu.CompilerParams(vmem_limit_bytes=40 << 20),
        cost_estimate=pl.CostEstimate(flops=flops, bytes_accessed=8 << 20, transcendentals=0),
        name="predict",
    )(place, foreground, col, *step_t, *start_t)


def turn_kernel(col_ref, out_ref):
    for at in range(0, col_ref.shape[1], 2 * LANES):
        out_ref[at : at + 2 * LANES, :] = col_ref[:, at : at + 2 * LANES].T


def turned(col):
    vmem = pl.BlockSpec(memory_space=pltpu.VMEM)
    return pl.pallas_call(
        turn_kernel,
        out_shape=jax.ShapeDtypeStruct(col.shape[::-1], col.dtype),
        in_specs=[vmem],
        out_specs=vmem,
        cost_estimate=pl.CostEstimate(flops=1 << 20, bytes_accessed=2 << 20, transcendentals=0),
        name="turn",
    )(col)


def local(visibility, flags, u_index, v_index, fg_filter):
    groups, tiles = lax.axis_size("chan"), lax.axis_size("tile")
    chan, tile = lax.axis_index("chan"), lax.axis_index("tile")
    chans = visibility.shape[2]
    total_rows = u_index.shape[0]
    lines = L // (groups * tiles)
    period = F * L
    masks = chip_masks(tiles)

    weight = flags.astype(BF16)
    own = jnp.transpose(visibility * weight[:, None, :], (1, 2, 0))
    seen = [own] + [chan_shift(own, groups, away) for away in range(1, groups)]
    near, far = [], []
    for away in range(groups):
        block = seen[away] if away < 2 else after(seen[away], *near[away - 2][1:])
        near.append([block] + [tile_swap(block, tiles, mask) for mask in masks[1:]])
        far.append([tile_swap(piece, tiles, 1) for piece in near[away]])

    order = tile ^ jnp.asarray(np.asarray(masks + [mask ^ 1 for mask in masks], np.int32))
    u_rows = u_index.reshape(tiles, LANES)[order].reshape(-1)
    v_rows = v_index.reshape(tiles, LANES)[order].reshape(-1)
    first_line = (chan * tiles + tile) * lines
    step_t = phase_tables(u_rows, period)
    start_t = phase_tables(u_rows * first_line, period)
    cos_col, sin_col = column_tables(v_rows)
    predict_col = jnp.stack(
        [cos_col.reshape(M, tiles, LANES), sin_col.reshape(M, tiles, LANES)], 2
    ).reshape(M, 2 * total_rows)
    image_col = turned(predict_col)

    images = []
    for away in range(groups):
        place = (lax.rem(chan + groups - away, groups) * (chans // FINE)).reshape(1)
        if away + 1 < groups:
            place = after(place, *near[away + 1][1:])
        blocks = near[away] + far[away]
        images.append(make_image(blocks, place, step_t, start_t, image_col, lines, total_rows))
    foreground = filter_images(images, chan.reshape(1), fg_filter)

    parts, first_halves, second_halves = [], [], []
    for turn, away in enumerate(list(range(1, groups)) + [0]):
        place = (lax.rem(chan + away, groups) * (chans // FINE)).reshape(1)
        if turn >= 2:
            place = after(place, first_halves[turn - 2])
        if turn >= 3:
            place = after(place, *second_halves[turn - 3])
        kept, sent = predict_part(foreground[away], place, step_t, start_t, predict_col)
        received = tile_swap(sent, tiles, 1)
        first_halves.append(received)
        total = kept + received.astype(F32)
        received = [
            tile_swap(total[spot].astype(BF16), tiles, mask)
            for spot, mask in enumerate(masks)
            if mask
        ]
        second_halves.append(received)
        part = total[0] + functools.reduce(jnp.add, [piece.astype(F32) for piece in received])
        if away:
            part = chan_shift(part.astype(BF16), groups, away).astype(F32)
        parts.append(part)
    predicted = jnp.transpose(functools.reduce(jnp.add, parts), (2, 0, 1))
    return weight.astype(F32)[:, None, :] * (visibility.astype(F32) - predicted)


def solution(mesh):
    return jax.shard_map(
        local,
        mesh=mesh,
        in_specs=(P("tile", None, "chan"), P("tile", "chan"), P(), P(), P()),
        out_specs=P("tile", None, "chan"),
        check_vma=False,
    )
```

time: 169 us -> 165 us (0.976)
  starting transfers between devices: 29.5 us -> 45.4 us
  other arithmetic: 22.8 us -> 9.75 us
  local copies, waits for them, and re-layouts: 22.2 us -> 17 us
    ppermute x30 -> x50, starting transfers between devices: 29.5 us -> 45.4 us  [the longest x44 34.8 us: tile_swap(): return lax.ppermute(block, 'tile', [(t, t ^ mask) for t in range(tiles)])]
    concatenate x12 -> x0, other arithmetic: 14.6 us -> none  [the longest x8 10.2 us: gather_tile(): jnp.concatenate([held, lax.ppermute(held, 'tile', stage_pairs(tiles, stag...]
    pallas_call x4, Pallas kernels: 36.6 us -> 32.6 us  [predict_part(): pl.pallas_call(functools.partial(predict_kernel, 1.0 / math.sqrt(L * M)),...]
    unnamed x59 -> x55, local copies, waits for them, and re-layouts: 10.1 us -> 6.94 us
    pallas_call x0 -> x1, Pallas kernels: none -> 2.52 us  [turned(): pl.pallas_call(turn_kernel, out_shape=jax.ShapeDtypeStruct(col.shape[::-1...]
    another operation x1, local copies, waits for them, and re-layouts: 3.84 us -> 1.62 us  [local(): jnp.stack([cos_col.reshape(M, tiles, LANES), sin_col.reshape(M, tiles, LA...]
    ppermute x30 -> x50, waiting for transfers between devices: 19 us -> 19.2 us  [the longest x44 18.5 us: tile_swap(): return lax.ppermute(block, 'tile', [(t, t ^ mask) for t in range(tiles)])]
  transfers between devices with their start and end apart: 30 -> 50, of which waited for: 7 -> 9; matrix products, arithmetic and copies ran while one was open for 19% -> 12% of each run, Pallas kernels for 23% -> 28%
where the time goes in v2:
time: 165 us; the launch traced here: 164 us
  Pallas kernels  72.2 us (44%)
  starting transfers between devices  45.4 us (28%)
  waiting for transfers between devices  19.2 us (12%)
  local copies, waits for them, and re-layouts  17 us (10%)
  other arithmetic  9.75 us (6%)
    ppermute x44, starting transfers between devices, tile_swap(): return lax.ppermute(block, 'tile', [(t, t ^ mask) for t in range(tiles)])  34.8 us
    pallas_call x4, Pallas kernels, predict_part(): pl.pallas_call(functools.partial(predict_kernel, 1.0 / math.sqrt(L * M)),...  32.6 us
    pallas_call x4, Pallas kernels, make_image(): pl.pallas_call(functools.partial(image_kernel, 1.0 / math.sqrt(total_rows...  26.2 us
    ppermute x44, waiting for transfers between devices, tile_swap(): return lax.ppermute(block, 'tile', [(t, t ^ mask) for t in range(tiles)])  18.5 us
    pallas_call x1, Pallas kernels, filter_images(): pl.pallas_call(functools.partial(filter_kernel, groups, chans), out_shape...  10.9 us
    ppermute x6, starting transfers between devices, chan_shift(): lax.ppermute(block, 'chan', [(c, (c + away) % groups) for c in range(grou...  10.6 us
    unnamed x55, local copies, waits for them, and re-layouts  6.94 us
  transfers between devices with their start and end apart: 50, of which 9 were waited for; matrix products, arithmetic and copies ran while one was open for 12% of the time, Pallas kernels for 28%

profile of v2, /device:TPU:0, one launch (start us, length us, event | category | flops | bytes accessed | tf_op | source)
XLA Modules:
  0.0 164.2 jit_solution(5183140431314316597)
XLA Ops:
  2.1 3.1 %collective-permute-start = (bf16[2,256,128]{2,1,0:T(8,128)(2,1)S(1)}, bf16[2,256,128]{2,1,0:T(8,128)(2,1)S(1)}, u32[]{:S(2)}, u32[]{:S(2)}) collective-permute-start(bf16[2,256,128]{2,1,0:T(8,128)(2,1)S(1)} %multiply_bitcast_fusion.refs_0_), channel_id=1, source_target_pairs={{0,8},{8,16},{16,24},{24,0},{1,9},{9,17},{17,25},{25,1},{2,10},{10... | collective-permute-start | bytes 393224 | tf_op jit(solution)/shard_map/ppermute | solution.py:36
  5.2 2.1 %collective-permute-start.19 = (bf16[2,256,128]{2,1,0:T(8,128)(2,1)S(1)}, bf16[2,256,128]{2,1,0:T(8,128)(2,1)S(1)}, u32[]{:S(2)}, u32[]{:S(2)}) collective-permute-start(bf16[2,256,128]{2,1,0:T(8,128)(2,1)S(1)} %multiply_bitcast_fusion.refs_0_), channel_id=1, source_target_pairs={{0,24},{8,0},{16,8},{24,16},{1,25},{9,1},{17,9},{25,17},{2,26},{10... | collective-permute-start | bytes 393224 | tf_op jit(solution)/shard_map/ppermute | solution.py:36
  7.3 1.6 %collective-permute-start.4 = (bf16[2,256,128]{2,1,0:T(8,128)(2,1)S(1)}, bf16[2,256,128]{2,1,0:T(8,128)(2,1)S(1)}, u32[]{:S(2)}, u32[]{:S(2)}) collective-permute-start(bf16[2,256,128]{2,1,0:T(8,128)(2,1)S(1)} %multiply_bitcast_fusion.refs_0_), channel_id=1, source_target_pairs={{0,2},{1,3},{2,0},{3,1},{4,6},{5,7},{6,4},{7,5},{8,10},{9,11},{10,... | collective-permute-start | bytes 393224 | tf_op jit(solution)/shard_map/ppermute | solution.py:32
  9.0 1.5 collective-permute-start.5
  20.6 1.5 collective-permute-start.2
  27.3 1.6 copy.20
  29.0 1.8 %reshape.887.col_ref = bf16[256,2048]{1,0:T(8,128)(2,1)} reshape(bf16[256,8,2,128]{3,2,1,0:T(2,128)(2,1)S(1)} %copy.20) | data formatting | bytes 2097152 | tf_op jit(solution)/shard_map/reshape | solution.py:316
  30.8 2.5 %turn.1.col_ref = bf16[2048,256]{1,0:T(8,128)(2,1)} custom-call(bf16[256,2048]{1,0:T(8,128)(2,1)} %reshape.887.col_ref), custom_call_target="tpu_custom_call" | custom-call | flops 1048576 | bytes 2097152 | tf_op jit(solution)/shard_map/turn/pallas_call | solution.py:279
  34.6 2.4 %collective-permute-start.14 = (bf16[2,256,128]{2,1,0:T(8,128)(2,1)S(1)}, bf16[2,256,128]{2,1,0:T(8,128)(2,1)S(1)}, u32[]{:S(2)}, u32[]{:S(2)}) collective-permute-start(bf16[2,256,128]{2,1,0:T(8,128)(2,1)S(1)} %collective-permute-done.11.refs_0_), channel_id=1, source_target_pairs={{0,6},{1,7},{2,4},{3,5},{4,2},{5,3},{6,0},{7,1},{8,14},{9,15},{10,... | collective-permute-start | bytes 393224 | tf_op jit(solution)/shard_map/ppermute | solution.py:32
  38.8 6.3 %collective-permute-done.3.refs_3_ = bf16[2,256,128]{2,1,0:T(8,128)(2,1)S(1)} collective-permute-done((bf16[2,256,128]{2,1,0:T(8,128)(2,1)S(1)}, bf16[2,256,128]{2,1,0:T(8,128)(2,1)S(1)}, u32[]{:S(2)}, u32[]{:S(2)}) %collective-permute-start.3) | collective-permute-done | bytes 131104 | tf_op jit(solution)/shard_map/ppermute | solution.py:32
  47.9 1.5 collective-permute-start.22
  49.6 1.9 %collective-permute-done.20.refs_1_ = bf16[2,256,128]{2,1,0:T(8,128)(2,1)S(1)} collective-permute-done((bf16[2,256,128]{2,1,0:T(8,128)(2,1)S(1)}, bf16[2,256,128]{2,1,0:T(8,128)(2,1)S(1)}, u32[]{:S(2)}, u32[]{:S(2)}) %collective-permute-start.20) | collective-permute-done | bytes 131104 | tf_op jit(solution)/shard_map/ppermute | solution.py:32
  52.0 6.6 %image.4.refs_0_ = bf16[16,256,256]{2,1,0:T(8,128)(2,1)S(1)} custom-call(s32[1]{0:T(128)} %bitcast.2.place_ref, f32[2,8,128,128]{3,2,1,0:T(8,128)S(1)} %maximum_bitcast_fusion.step_c, f32[2,8,8,128]{3,2,1,0:T(8,128)S(1)} %get-tuple-element.93.step_f, f32[2,8,128,128]{3,2,1,0:T(8,128)S(1)} %maximum_bitcast_fusion.1.start_c, ...), custom_call_target="tpu_custom_call" | custom-call | flops 4294967296 | bytes 8388608 | tf_op jit(solution)/shard_map/image/pallas_call | solution.py:145
  59.9 6.6 %image.6.refs_2_ = bf16[16,256,256]{2,1,0:T(8,128)(2,1)S(1)} custom-call(s32[1]{0:T(128)} %bitcast.13.place_ref, f32[2,8,128,128]{3,2,1,0:T(8,128)S(1)} %maximum_bitcast_fusion.step_c, f32[2,8,8,128]{3,2,1,0:T(8,128)S(1)} %get-tuple-element.93.step_f, f32[2,8,128,128]{3,2,1,0:T(8,128)S(1)} %maximum_bitcast_fusion.1.start_c, ...), custom_call_target="tpu_custom_call" | custom-call | flops 4294967296 | bytes 8388608 | tf_op jit(solution)/shard_map/image/pallas_call | solution.py:145
  67.4 6.6 %image.5.refs_1_ = bf16[16,256,256]{2,1,0:T(8,128)(2,1)S(1)} custom-call(s32[1]{0:T(128)} %bitcast.12.place_ref, f32[2,8,128,128]{3,2,1,0:T(8,128)S(1)} %maximum_bitcast_fusion.step_c, f32[2,8,8,128]{3,2,1,0:T(8,128)S(1)} %get-tuple-element.93.step_f, f32[2,8,128,128]{3,2,1,0:T(8,128)S(1)} %maximum_bitcast_fusion.1.start_c, ...), custom_call_target="tpu_custom_call" | custom-call | flops 4294967296 | bytes 8388608 | tf_op jit(solution)/shard_map/image/pallas_call | solution.py:145
  74.0 6.6 %image.7.refs_3_ = bf16[16,256,256]{2,1,0:T(8,128)(2,1)S(1)} custom-call(s32[1]{0:T(128)} %bitcast.place_ref, f32[2,8,128,128]{3,2,1,0:T(8,128)S(1)} %maximum_bitcast_fusion.step_c, f32[2,8,8,128]{3,2,1,0:T(8,128)S(1)} %get-tuple-element.93.step_f, f32[2,8,128,128]{3,2,1,0:T(8,128)S(1)} %maximum_bitcast_fusion.1.start_c, ...), custom_call_target="tpu_custom_call" | custom-call | flops 4294967296 | bytes 8388608 | tf_op jit(solution)/shard_map/image/pallas_call | solution.py:145
  81.9 10.9 %filter.1 = (bf16[16,256,256]{2,1,0:T(8,128)(2,1)S(1)}, bf16[16,256,256]{2,1,0:T(8,128)(2,1)S(1)}, bf16[16,256,256]{2,1,0:T(8,128)(2,1)S(1)}, bf16[16,256,256]{2,1,0:T(8,128)(2,1)S(1)}) custom-call(s32[1]{0:T(128)} %bitcast.1.place_ref, bf16[1024,1024]{1,0:T(8,128)(2,1)S(1)} %copy-done.5, bf16[16,256,256]{2,1,0:T(8,128)(2,1)S(1)} %image.4.refs_0_, ...), custom_call_target="tpu_custom_call" | custom-call | flops 8589934592 | bytes 18874368 | tf_op jit(solution)/shard_map/filter/pallas_call | solution.py:183
  92.9 8.7 %predict.4 = (f32[4,2,256,128]{3,2,1,0:T(8,128)S(1)}, bf16[4,2,256,128]{3,2,1,0:T(8,128)(2,1)}) custom-call(s32[1]{0:T(128)} %bitcast.place_ref, bf16[16,256,256]{2,1,0:T(8,128)(2,1)S(1)} %get-tuple-element.30.image_ref, bf16[256,2048]{1,0:T(8,128)(2,1)S(1)} %copy-done.1, f32[2,8,128,128]{3,2,1,0:T(8,128)S(1)} %maximum_bitcast_fusion.step_c, ...), custom_call_target="tpu_custom_call" | custom-call | flops 4294967296 | bytes 8388608 | tf_op jit(solution)/shard_map/predict/pallas_call | solution.py:260
  103.1 1.6 copy-done.14
  104.7 8.1 %predict.5 = (f32[4,2,256,128]{3,2,1,0:T(8,128)S(1)}, bf16[4,2,256,128]{3,2,1,0:T(8,128)(2,1)S(1)}) custom-call(s32[1]{0:T(128)} %bitcast.13.place_ref, bf16[16,256,256]{2,1,0:T(8,128)(2,1)S(1)} %copy-done.14, bf16[256,2048]{1,0:T(8,128)(2,1)S(1)} %copy-done.1, f32[2,8,128,128]{3,2,1,0:T(8,128)S(1)} %copy-done.3, ...), custom_call_target="tpu_custom_call" | custom-call | flops 4294967296 | bytes 8388608 | tf_op jit(solution)/shard_map/predict/pallas_call | solution.py:260
  114.4 3.1 %collective-permute-start.32 = (bf16[2,256,128]{2,1,0:T(8,128)(2,1)S(1)}, bf16[2,256,128]{2,1,0:T(8,128)(2,1)S(1)}, u32[]{:S(2)}, u32[]{:S(2)}) collective-permute-start(bf16[2,256,128]{2,1,0:T(8,128)(2,1)S(1)} %get-tuple-element.64), channel_id=1, source_target_pairs={{0,2},{1,3},{2,0},{3,1},{4,6},{5,7},{6,4},{7,5},{8,10},{9,11},{10,... | collective-permute-start | bytes 393224 | tf_op jit(solution)/shard_map/ppermute | solution.py:32
  117.5 2.5 %collective-permute-start.33 = (bf16[2,256,128]{2,1,0:T(8,128)(2,1)S(1)}, bf16[2,256,128]{2,1,0:T(8,128)(2,1)S(1)}, u32[]{:S(2)}, u32[]{:S(2)}) collective-permute-start(bf16[2,256,128]{2,1,0:T(8,128)(2,1)S(1)} %get-tuple-element.63), channel_id=1, source_target_pairs={{0,4},{1,5},{2,6},{3,7},{4,0},{5,1},{6,2},{7,3},{8,12},{9,13},{10,... | collective-permute-start | bytes 393224 | tf_op jit(solution)/shard_map/ppermute | solution.py:32
  121.8 2.0 %collective-permute-start.38 = (bf16[2,256,128]{2,1,0:T(8,128)(2,1)S(1)}, bf16[2,256,128]{2,1,0:T(8,128)(2,1)S(1)}, u32[]{:S(2)}, u32[]{:S(2)}) collective-permute-start(bf16[2,256,128]{2,1,0:T(8,128)(2,1)S(1)} %get-tuple-element.55), channel_id=1, source_target_pairs={{0,4},{1,5},{2,6},{3,7},{4,0},{5,1},{6,2},{7,3},{8,12},{9,13},{10,... | collective-permute-start | bytes 393224 | tf_op jit(solution)/shard_map/ppermute | solution.py:32
  123.8 7.9 %predict.6 = (f32[4,2,256,128]{3,2,1,0:T(8,128)S(1)}, bf16[4,2,256,128]{3,2,1,0:T(8,128)(2,1)S(1)}) custom-call(s32[1]{0:T(128)} %bitcast.12.place_ref, bf16[16,256,256]{2,1,0:T(8,128)(2,1)S(1)} %copy-done.12, bf16[256,2048]{1,0:T(8,128)(2,1)S(1)} %copy-done.1, f32[2,8,128,128]{3,2,1,0:T(8,128)S(1)} %copy-done.3, ...), custom_call_target="tpu_custom_call" | custom-call | flops 4294967296 | bytes 8388608 | tf_op jit(solution)/shard_map/predict/pallas_call | solution.py:260
  131.9 1.6 collective-permute-start.35
  133.6 7.9 %predict.7 = (f32[4,2,256,128]{3,2,1,0:T(8,128)S(1)}, bf16[4,2,256,128]{3,2,1,0:T(8,128)(2,1)S(1)}) custom-call(s32[1]{0:T(128)} %bitcast.26.place_ref, bf16[16,256,256]{2,1,0:T(8,128)(2,1)S(1)} %copy-done.10, bf16[256,2048]{1,0:T(8,128)(2,1)S(1)} %copy-done.1, f32[2,8,128,128]{3,2,1,0:T(8,128)S(1)} %copy-done.3, ...), custom_call_target="tpu_custom_call" | custom-call | flops 4294967296 | bytes 8388608 | tf_op jit(solution)/shard_map/predict/pallas_call | solution.py:260
  143.4 2.0 %collective-permute-start.43 = (bf16[2,256,128]{2,1,0:T(8,128)(2,1)S(1)}, bf16[2,256,128]{2,1,0:T(8,128)(2,1)S(1)}, u32[]{:S(2)}, u32[]{:S(2)}) collective-permute-start(bf16[2,256,128]{2,1,0:T(8,128)(2,1)S(1)} %get-tuple-element.58), channel_id=1, source_target_pairs={{0,4},{1,5},{2,6},{3,7},{4,0},{5,1},{6,2},{7,3},{8,12},{9,13},{10,... | collective-permute-start | bytes 393224 | tf_op jit(solution)/shard_map/ppermute | solution.py:32
  145.7 2.2 %collective-permute-done.42 = bf16[2,256,128]{2,1,0:T(8,128)(2,1)S(1)} collective-permute-done((bf16[2,256,128]{2,1,0:T(8,128)(2,1)S(1)}, bf16[2,256,128]{2,1,0:T(8,128)(2,1)S(1)}, u32[]{:S(2)}, u32[]{:S(2)}) %collective-permute-start.42) | collective-permute-done | bytes 131104 | tf_op jit(solution)/shard_map/ppermute | solution.py:32
  148.5 2.7 %collective-permute-done.43 = bf16[2,256,128]{2,1,0:T(8,128)(2,1)S(1)} collective-permute-done((bf16[2,256,128]{2,1,0:T(8,128)(2,1)S(1)}, bf16[2,256,128]{2,1,0:T(8,128)(2,1)S(1)}, u32[]{:S(2)}, u32[]{:S(2)}) %collective-permute-start.43) | collective-permute-done | bytes 131104 | tf_op jit(solution)/shard_map/ppermute | solution.py:32
  152.1 2.3 %collective-permute-start.45 = (bf16[2,256,128]{2,1,0:T(8,128)(2,1)S(1)}, bf16[2,256,128]{2,1,0:T(8,128)(2,1)S(1)}, u32[]{:S(2)}, u32[]{:S(2)}) collective-permute-start(bf16[2,256,128]{2,1,0:T(8,128)(2,1)S(1)} %fusion.6), channel_id=1, source_target_pairs={{0,24},{8,0},{16,8},{24,16},{1,25},{9,1},{17,9},{25,17},{2,26},{10... | collective-permute-start | bytes 393224 | tf_op jit(solution)/shard_map/ppermute | solution.py:36
  159.0 1.6 collective-permute-done.47
  160.6 2.6 %collective-permute-done.48 = bf16[2,256,128]{2,1,0:T(8,128)(2,1)S(1)} collective-permute-done((bf16[2,256,128]{2,1,0:T(8,128)(2,1)S(1)}, bf16[2,256,128]{2,1,0:T(8,128)(2,1)S(1)}, u32[]{:S(2)}, u32[]{:S(2)}) %collective-permute-start.48) | collective-permute-done | bytes 131104 | tf_op jit(solution)/shard_map/ppermute | solution.py:32
  (176 shorter events, 41.5 us)
Async XLA Ops:
  2.1 16.0 %collective-permute-start = (bf16[2,256,128]{2,1,0:T(8,128)(2,1)S(1)}, bf16[2,256,128]{2,1,0:T(8,128)(2,1)S(1)}, u32[]{:S(2)}, u32[]{:S(2)}) collective-permute-start(bf16[2,256,128]{2,1,0:T(8,128)(2,1)S(1)} %multiply_bitcast_fusion.refs_0_), channel_id=1, source_target_pairs={{0,8},{8,16},{16,24},{24,0},{1,9},{9,17},{17,25},{25,1},{2,10},{10... | collective-permute-start | bytes 393224 | tf_op jit(solution)/shard_map/ppermute | solution.py:36
  5.2 28.9 %collective-permute-start.19 = (bf16[2,256,128]{2,1,0:T(8,128)(2,1)S(1)}, bf16[2,256,128]{2,1,0:T(8,128)(2,1)S(1)}, u32[]{:S(2)}, u32[]{:S(2)}) collective-permute-start(bf16[2,256,128]{2,1,0:T(8,128)(2,1)S(1)} %multiply_bitcast_fusion.refs_0_), channel_id=1, source_target_pairs={{0,24},{8,0},{16,8},{24,16},{1,25},{9,1},{17,9},{25,17},{2,26},{10... | collective-permute-start | bytes 393224 | tf_op jit(solution)/shard_map/ppermute | solution.py:36
  7.3 11.8 %collective-permute-start.4 = (bf16[2,256,128]{2,1,0:T(8,128)(2,1)S(1)}, bf16[2,256,128]{2,1,0:T(8,128)(2,1)S(1)}, u32[]{:S(2)}, u32[]{:S(2)}) collective-permute-start(bf16[2,256,128]{2,1,0:T(8,128)(2,1)S(1)} %multiply_bitcast_fusion.refs_0_), channel_id=1, source_target_pairs={{0,2},{1,3},{2,0},{3,1},{4,6},{5,7},{6,4},{7,5},{8,10},{9,11},{10,... | collective-permute-start | bytes 393224 | tf_op jit(solution)/shard_map/ppermute | solution.py:32
  9.0 11.6 %collective-permute-start.5 = (bf16[2,256,128]{2,1,0:T(8,128)(2,1)S(1)}, bf16[2,256,128]{2,1,0:T(8,128)(2,1)S(1)}, u32[]{:S(2)}, u32[]{:S(2)}) collective-permute-start(bf16[2,256,128]{2,1,0:T(8,128)(2,1)S(1)} %multiply_bitcast_fusion.refs_0_), channel_id=1, source_target_pairs={{0,4},{1,5},{2,6},{3,7},{4,0},{5,1},{6,2},{7,3},{8,12},{9,13},{10,... | collective-permute-start | bytes 393224 | tf_op jit(solution)/shard_map/ppermute | solution.py:32
  10.5 22.9 %collective-permute-start.6 = (bf16[2,256,128]{2,1,0:T(8,128)(2,1)S(1)}, bf16[2,256,128]{2,1,0:T(8,128)(2,1)S(1)}, u32[]{:S(2)}, u32[]{:S(2)}) collective-permute-start(bf16[2,256,128]{2,1,0:T(8,128)(2,1)S(1)} %multiply_bitcast_fusion.refs_0_), channel_id=1, source_target_pairs={{0,6},{1,7},{2,4},{3,5},{4,2},{5,3},{6,0},{7,1},{8,14},{9,15},{10,... | collective-permute-start | bytes 393224 | tf_op jit(solution)/shard_map/ppermute | solution.py:32
  18.1 15.4 %collective-permute-start.11 = (bf16[2,256,128]{2,1,0:T(8,128)(2,1)S(1)}, bf16[2,256,128]{2,1,0:T(8,128)(2,1)S(1)}, u32[]{:S(2)}, u32[]{:S(2)}) collective-permute-start(bf16[2,256,128]{2,1,0:T(8,128)(2,1)S(1)} %multiply_bitcast_fusion.refs_0_), channel_id=1, source_target_pairs={{0,16},{8,24},{16,0},{24,8},{1,17},{9,25},{17,1},{25,9},{2,18},{10... | collective-permute-start | bytes 393224 | tf_op jit(solution)/shard_map/ppermute | solution.py:36
  19.1 15.5 %collective-permute-start.1 = (bf16[2,256,128]{2,1,0:T(8,128)(2,1)S(1)}, bf16[2,256,128]{2,1,0:T(8,128)(2,1)S(1)}, u32[]{:S(2)}, u32[]{:S(2)}) collective-permute-start(bf16[2,256,128]{2,1,0:T(8,128)(2,1)S(1)} %collective-permute-done.refs_0_), channel_id=1, source_target_pairs={{0,2},{1,3},{2,0},{3,1},{4,6},{5,7},{6,4},{7,5},{8,10},{9,11},{10,... | collective-permute-start | bytes 393224 | tf_op jit(solution)/shard_map/ppermute | solution.py:32
  20.6 16.5 %collective-permute-start.2 = (bf16[2,256,128]{2,1,0:T(8,128)(2,1)S(1)}, bf16[2,256,128]{2,1,0:T(8,128)(2,1)S(1)}, u32[]{:S(2)}, u32[]{:S(2)}) collective-permute-start(bf16[2,256,128]{2,1,0:T(8,128)(2,1)S(1)} %collective-permute-done.refs_0_), channel_id=1, source_target_pairs={{0,4},{1,5},{2,6},{3,7},{4,0},{5,1},{6,2},{7,3},{8,12},{9,13},{10,... | collective-permute-start | bytes 393224 | tf_op jit(solution)/shard_map/ppermute | solution.py:32
  33.4 11.7 %collective-permute-start.7 = (bf16[2,256,128]{2,1,0:T(8,128)(2,1)S(1)}, bf16[2,256,128]{2,1,0:T(8,128)(2,1)S(1)}, u32[]{:S(2)}, u32[]{:S(2)}) collective-permute-start(bf16[2,256,128]{2,1,0:T(8,128)(2,1)S(1)} %multiply_bitcast_fusion.refs_0_), channel_id=1, source_target_pairs={{0,1},{1,0},{2,3},{3,2},{4,5},{5,4},{6,7},{7,6},{8,9},{9,8},{10,11... | collective-permute-start | bytes 393224 | tf_op jit(solution)/shard_map/ppermute | solution.py:32
  33.5 12.1 %collective-permute-start.12 = (bf16[2,256,128]{2,1,0:T(8,128)(2,1)S(1)}, bf16[2,256,128]{2,1,0:T(8,128)(2,1)S(1)}, u32[]{:S(2)}, u32[]{:S(2)}) collective-permute-start(bf16[2,256,128]{2,1,0:T(8,128)(2,1)S(1)} %collective-permute-done.11.refs_0_), channel_id=1, source_target_pairs={{0,2},{1,3},{2,0},{3,1},{4,6},{5,7},{6,4},{7,5},{8,10},{9,11},{10,... | collective-permute-start | bytes 393224 | tf_op jit(solution)/shard_map/ppermute | solution.py:32
  34.1 11.6 %collective-permute-start.13 = (bf16[2,256,128]{2,1,0:T(8,128)(2,1)S(1)}, bf16[2,256,128]{2,1,0:T(8,128)(2,1)S(1)}, u32[]{:S(2)}, u32[]{:S(2)}) collective-permute-start(bf16[2,256,128]{2,1,0:T(8,128)(2,1)S(1)} %collective-permute-done.11.refs_0_), channel_id=1, source_target_pairs={{0,4},{1,5},{2,6},{3,7},{4,0},{5,1},{6,2},{7,3},{8,12},{9,13},{10,... | collective-permute-start | bytes 393224 | tf_op jit(solution)/shard_map/ppermute | solution.py:32
  34.6 12.2 %collective-permute-start.14 = (bf16[2,256,128]{2,1,0:T(8,128)(2,1)S(1)}, bf16[2,256,128]{2,1,0:T(8,128)(2,1)S(1)}, u32[]{:S(2)}, u32[]{:S(2)}) collective-permute-start(bf16[2,256,128]{2,1,0:T(8,128)(2,1)S(1)} %collective-permute-done.11.refs_0_), channel_id=1, source_target_pairs={{0,6},{1,7},{2,4},{3,5},{4,2},{5,3},{6,0},{7,1},{8,14},{9,15},{10,... | collective-permute-start | bytes 393224 | tf_op jit(solution)/shard_map/ppermute | solution.py:32
  37.1 8.0 %collective-permute-start.3 = (bf16[2,256,128]{2,1,0:T(8,128)(2,1)S(1)}, bf16[2,256,128]{2,1,0:T(8,128)(2,1)S(1)}, u32[]{:S(2)}, u32[]{:S(2)}) collective-permute-start(bf16[2,256,128]{2,1,0:T(8,128)(2,1)S(1)} %collective-permute-done.refs_0_), channel_id=1, source_target_pairs={{0,6},{1,7},{2,4},{3,5},{4,2},{5,3},{6,0},{7,1},{8,14},{9,15},{10,... | collective-permute-start | bytes 393224 | tf_op jit(solution)/shard_map/ppermute | solution.py:32
  47.8 11.1 %collective-permute-start.23 = (bf16[2,256,128]{2,1,0:T(8,128)(2,1)S(1)}, bf16[2,256,128]{2,1,0:T(8,128)(2,1)S(1)}, u32[]{:S(2)}, u32[]{:S(2)}) collective-permute-start(bf16[2,256,128]{2,1,0:T(8,128)(2,1)S(1)} %collective-permute-done.11.refs_0_), channel_id=1, source_target_pairs={{0,1},{1,0},{2,3},{3,2},{4,5},{5,4},{6,7},{7,6},{8,9},{9,8},{10,11... | collective-permute-start | bytes 393224 | tf_op jit(solution)/shard_map/ppermute | solution.py:32
  47.9 10.7 %collective-permute-start.22 = (bf16[2,256,128]{2,1,0:T(8,128)(2,1)S(1)}, bf16[2,256,128]{2,1,0:T(8,128)(2,1)S(1)}, u32[]{:S(2)}, u32[]{:S(2)}) collective-permute-start(bf16[2,256,128]{2,1,0:T(8,128)(2,1)S(1)} %collective-permute-done.19.refs_0_), channel_id=1, source_target_pairs={{0,6},{1,7},{2,4},{3,5},{4,2},{5,3},{6,0},{7,1},{8,14},{9,15},{10,... | collective-permute-start | bytes 393224 | tf_op jit(solution)/shard_map/ppermute | solution.py:32
  49.4 9.7 %collective-permute-start.24 = (bf16[2,256,128]{2,1,0:T(8,128)(2,1)S(1)}, bf16[2,256,128]{2,1,0:T(8,128)(2,1)S(1)}, u32[]{:S(2)}, u32[]{:S(2)}) collective-permute-start(bf16[2,256,128]{2,1,0:T(8,128)(2,1)S(1)} %collective-permute-done.12.refs_1_), channel_id=1, source_target_pairs={{0,1},{1,0},{2,3},{3,2},{4,5},{5,4},{6,7},{7,6},{8,9},{9,8},{10,11... | collective-permute-start | bytes 393224 | tf_op jit(solution)/shard_map/ppermute | solution.py:32
  51.5 7.9 %collective-permute-start.25 = (bf16[2,256,128]{2,1,0:T(8,128)(2,1)S(1)}, bf16[2,256,128]{2,1,0:T(8,128)(2,1)S(1)}, u32[]{:S(2)}, u32[]{:S(2)}) collective-permute-start(bf16[2,256,128]{2,1,0:T(8,128)(2,1)S(1)} %collective-permute-done.13.refs_2_), channel_id=1, source_target_pairs={{0,1},{1,0},{2,3},{3,2},{4,5},{5,4},{6,7},{7,6},{8,9},{9,8},{10,11... | collective-permute-start | bytes 393224 | tf_op jit(solution)/shard_map/ppermute | solution.py:32
  51.8 7.9 %collective-permute-start.26 = (bf16[2,256,128]{2,1,0:T(8,128)(2,1)S(1)}, bf16[2,256,128]{2,1,0:T(8,128)(2,1)S(1)}, u32[]{:S(2)}, u32[]{:S(2)}) collective-permute-start(bf16[2,256,128]{2,1,0:T(8,128)(2,1)S(1)} %collective-permute-done.14.refs_3_), channel_id=1, source_target_pairs={{0,1},{1,0},{2,3},{3,2},{4,5},{5,4},{6,7},{7,6},{8,9},{9,8},{10,11... | collective-permute-start | bytes 393224 | tf_op jit(solution)/shard_map/ppermute | solution.py:32
  58.6 7.9 %collective-permute-start.15 = (bf16[2,256,128]{2,1,0:T(8,128)(2,1)S(1)}, bf16[2,256,128]{2,1,0:T(8,128)(2,1)S(1)}, u32[]{:S(2)}, u32[]{:S(2)}) collective-permute-start(bf16[2,256,128]{2,1,0:T(8,128)(2,1)S(1)} %collective-permute-done.refs_0_), channel_id=1, source_target_pairs={{0,1},{1,0},{2,3},{3,2},{4,5},{5,4},{6,7},{7,6},{8,9},{9,8},{10,11... | collective-permute-start | bytes 393224 | tf_op jit(solution)/shard_map/ppermute | solution.py:32
  58.9 15.1 %collective-permute-start.27 = (bf16[2,256,128]{2,1,0:T(8,128)(2,1)S(1)}, bf16[2,256,128]{2,1,0:T(8,128)(2,1)S(1)}, u32[]{:S(2)}, u32[]{:S(2)}) collective-permute-start(bf16[2,256,128]{2,1,0:T(8,128)(2,1)S(1)} %collective-permute-done.19.refs_0_), channel_id=1, source_target_pairs={{0,1},{1,0},{2,3},{3,2},{4,5},{5,4},{6,7},{7,6},{8,9},{9,8},{10,11... | collective-permute-start | bytes 393224 | tf_op jit(solution)/shard_map/ppermute | solution.py:32
  101.6 11.6 %collective-permute-start.31 = (bf16[4,2,256,128]{3,2,1,0:T(8,128)(2,1)}, bf16[4,2,256,128]{3,2,1,0:T(8,128)(2,1)}, u32[]{:S(2)}, u32[]{:S(2)}) collective-permute-start(bf16[4,2,256,128]{3,2,1,0:T(8,128)(2,1)} %get-tuple-element.32), channel_id=1, source_target_pairs={{0,1},{1,0},{2,3},{3,2},{4,5},{5,4},{6,7},{7,6},{8,9},{9,8},{10,11... | collective-permute-start | bytes 1572872 | tf_op jit(solution)/shard_map/ppermute | solution.py:32
  114.4 17.3 %collective-permute-start.32 = (bf16[2,256,128]{2,1,0:T(8,128)(2,1)S(1)}, bf16[2,256,128]{2,1,0:T(8,128)(2,1)S(1)}, u32[]{:S(2)}, u32[]{:S(2)}) collective-permute-start(bf16[2,256,128]{2,1,0:T(8,128)(2,1)S(1)} %get-tuple-element.64), channel_id=1, source_target_pairs={{0,2},{1,3},{2,0},{3,1},{4,6},{5,7},{6,4},{7,5},{8,10},{9,11},{10,... | collective-permute-start | bytes 393224 | tf_op jit(solution)/shard_map/ppermute | solution.py:32
  117.5 14.3 %collective-permute-start.33 = (bf16[2,256,128]{2,1,0:T(8,128)(2,1)S(1)}, bf16[2,256,128]{2,1,0:T(8,128)(2,1)S(1)}, u32[]{:S(2)}, u32[]{:S(2)}) collective-permute-start(bf16[2,256,128]{2,1,0:T(8,128)(2,1)S(1)} %get-tuple-element.63), channel_id=1, source_target_pairs={{0,4},{1,5},{2,6},{3,7},{4,0},{5,1},{6,2},{7,3},{8,12},{9,13},{10,... | collective-permute-start | bytes 393224 | tf_op jit(solution)/shard_map/ppermute | solution.py:32
  120.0 11.9 %collective-permute-start.34 = (bf16[2,256,128]{2,1,0:T(8,128)(2,1)S(1)}, bf16[2,256,128]{2,1,0:T(8,128)(2,1)S(1)}, u32[]{:S(2)}, u32[]{:S(2)}) collective-permute-start(bf16[2,256,128]{2,1,0:T(8,128)(2,1)S(1)} %get-tuple-element.62), channel_id=1, source_target_pairs={{0,6},{1,7},{2,4},{3,5},{4,2},{5,3},{6,0},{7,1},{8,14},{9,15},{10,... | collective-permute-start | bytes 393224 | tf_op jit(solution)/shard_map/ppermute | solution.py:32
  120.3 21.7 %collective-permute-start.37 = (bf16[2,256,128]{2,1,0:T(8,128)(2,1)S(1)}, bf16[2,256,128]{2,1,0:T(8,128)(2,1)S(1)}, u32[]{:S(2)}, u32[]{:S(2)}) collective-permute-start(bf16[2,256,128]{2,1,0:T(8,128)(2,1)S(1)} %get-tuple-element.53), channel_id=1, source_target_pairs={{0,2},{1,3},{2,0},{3,1},{4,6},{5,7},{6,4},{7,5},{8,10},{9,11},{10,... | collective-permute-start | bytes 393224 | tf_op jit(solution)/shard_map/ppermute | solution.py:32
  121.8 21.6 %collective-permute-start.38 = (bf16[2,256,128]{2,1,0:T(8,128)(2,1)S(1)}, bf16[2,256,128]{2,1,0:T(8,128)(2,1)S(1)}, u32[]{:S(2)}, u32[]{:S(2)}) collective-permute-start(bf16[2,256,128]{2,1,0:T(8,128)(2,1)S(1)} %get-tuple-element.55), channel_id=1, source_target_pairs={{0,4},{1,5},{2,6},{3,7},{4,0},{5,1},{6,2},{7,3},{8,12},{9,13},{10,... | collective-permute-start | bytes 393224 | tf_op jit(solution)/shard_map/ppermute | solution.py:32
  131.7 13.8 %collective-permute-start.39 = (bf16[2,256,128]{2,1,0:T(8,128)(2,1)S(1)}, bf16[2,256,128]{2,1,0:T(8,128)(2,1)S(1)}, u32[]{:S(2)}, u32[]{:S(2)}) collective-permute-start(bf16[2,256,128]{2,1,0:T(8,128)(2,1)S(1)} %get-tuple-element.54), channel_id=1, source_target_pairs={{0,6},{1,7},{2,4},{3,5},{4,2},{5,3},{6,0},{7,1},{8,14},{9,15},{10,... | collective-permute-start | bytes 393224 | tf_op jit(solution)/shard_map/ppermute | solution.py:32
  131.8 9.6 %collective-permute-start.41 = (bf16[4,2,256,128]{3,2,1,0:T(8,128)(2,1)S(1)}, bf16[4,2,256,128]{3,2,1,0:T(8,128)(2,1)S(1)}, u32[]{:S(2)}, u32[]{:S(2)}) collective-permute-start(bf16[4,2,256,128]{3,2,1,0:T(8,128)(2,1)S(1)} %get-tuple-element.39), channel_id=1, source_target_pairs={{0,1},{1,0},{2,3},{3,2},{4,5},{5,4},{6,7},{7,6},{8,9},{9,8},{10,11... | collective-permute-start | bytes 1572872 | tf_op jit(solution)/shard_map/ppermute | solution.py:32
  131.9 25.0 %collective-permute-start.35 = (bf16[2,256,128]{2,1,0:T(8,128)(2,1)S(1)}, bf16[2,256,128]{2,1,0:T(8,128)(2,1)S(1)}, u32[]{:S(2)}, u32[]{:S(2)}) collective-permute-start(bf16[2,256,128]{2,1,0:T(8,128)(2,1)S(1)} %fusion.10), channel_id=1, source_target_pairs={{0,8},{8,16},{16,24},{24,0},{1,9},{9,17},{17,25},{25,1},{2,10},{10... | collective-permute-start | bytes 393224 | tf_op jit(solution)/shard_map/ppermute | solution.py:36
  141.5 12.9 %collective-permute-start.46 = (bf16[4,2,256,128]{3,2,1,0:T(8,128)(2,1)S(1)}, bf16[4,2,256,128]{3,2,1,0:T(8,128)(2,1)S(1)}, u32[]{:S(2)}, u32[]{:S(2)}) collective-permute-start(bf16[4,2,256,128]{3,2,1,0:T(8,128)(2,1)S(1)} %get-tuple-element.44), channel_id=1, source_target_pairs={{0,1},{1,0},{2,3},{3,2},{4,5},{5,4},{6,7},{7,6},{8,9},{9,8},{10,11... | collective-permute-start | bytes 1572872 | tf_op jit(solution)/shard_map/ppermute | solution.py:32
  143.4 7.8 %collective-permute-start.43 = (bf16[2,256,128]{2,1,0:T(8,128)(2,1)S(1)}, bf16[2,256,128]{2,1,0:T(8,128)(2,1)S(1)}, u32[]{:S(2)}, u32[]{:S(2)}) collective-permute-start(bf16[2,256,128]{2,1,0:T(8,128)(2,1)S(1)} %get-tuple-element.58), channel_id=1, source_target_pairs={{0,4},{1,5},{2,6},{3,7},{4,0},{5,1},{6,2},{7,3},{8,12},{9,13},{10,... | collective-permute-start | bytes 393224 | tf_op jit(solution)/shard_map/ppermute | solution.py:32
  147.9 10.4 %collective-permute-start.40 = (bf16[2,256,128]{2,1,0:T(8,128)(2,1)S(1)}, bf16[2,256,128]{2,1,0:T(8,128)(2,1)S(1)}, u32[]{:S(2)}, u32[]{:S(2)}) collective-permute-start(bf16[2,256,128]{2,1,0:T(8,128)(2,1)S(1)} %fusion.8), channel_id=1, source_target_pairs={{0,16},{8,24},{16,0},{24,8},{1,17},{9,25},{17,1},{25,9},{2,18},{10... | collective-permute-start | bytes 393224 | tf_op jit(solution)/shard_map/ppermute | solution.py:36
  (42 other events, 336.6 us)

commit v3 on v2

v3 whole, which is shorter than its diff:
```python
import functools
import math

import jax
import jax.numpy as jnp
from jax import lax
from jax.experimental import pallas as pl
from jax.experimental.pallas import tpu as pltpu
from jax.sharding import PartitionSpec as P

F = 1024
L = 512
M = 256

TWO_PI = 2.0 * math.pi
FINE = 8
DIGIT = 16
GROUPS = F // FINE
TOKEN = jax.ShapeDtypeStruct((1,), jnp.int32)
LANES = 128
A_CHANS = 16
C_CHANS = 64
C_UNIT = 16
C_SLOTS = 2
VMEM_SMALL = 8 << 20
VMEM_FILTER = 16 << 20
F32 = jnp.float32
BF16 = jnp.bfloat16


def chip_masks(tiles):
    return [mask for mask in range(0, tiles, 2)]


def tile_swap(block, tiles, mask):
    return lax.ppermute(block, "tile", [(t, t ^ mask) for t in range(tiles)])


def chan_shift(block, groups, away):
    return lax.ppermute(block, "chan", [(c, (c + away) % groups) for c in range(groups)])


def after(value, *others):
    return lax.optimization_barrier((value, *others))[0]


def times(a, b):
    return a[0] * b[0] - a[1] * b[1], a[1] * b[0] + a[0] * b[1]


def conj_times(a, b):
    return a[0] * b[0] + a[1] * b[1], a[1] * b[0] - a[0] * b[1]


def turn_unit(turns, period):
    angle = (turns & (period - 1)).astype(F32) * (TWO_PI / period)
    return jnp.cos(angle), jnp.sin(angle)


def row_of(pair, row, height):
    return tuple(jnp.broadcast_to(part[row : row + 1], (height, LANES)) for part in pair)


def table_kernel(tiles, place_ref, u_ref, v_ref, step_ref, start_ref, col_ref, turned_ref, token_ref):
    tile, first_line = place_ref[0], place_ref[1]
    ids = lax.broadcasted_iota(jnp.int32, (DIGIT, LANES), 0)
    token_ref[0] = tile
    masks = chip_masks(tiles)
    for block, mask in enumerate(masks + [mask ^ 1 for mask in masks]):
        source = pl.ds(tile ^ mask, FINE, stride=0)
        u_row, v_row = u_ref[source, :], v_ref[source, :]
        for scaled, table_ref in ((u_row, step_ref), (u_row * first_line, start_ref)):
            deep = jnp.concatenate([scaled] * (DIGIT // FINE), 0)
            high = turn_unit(deep * (F + FINE * DIGIT * ids), F * L)
            low = turn_unit(deep * (FINE * ids), F * L)
            fine = turn_unit(scaled * ids[:FINE], F * L)
            for row in range(GROUPS // DIGIT):
                both = times(row_of(high, row, DIGIT), low)
                for part in range(2):
                    table_ref[part, block, row * DIGIT : (row + 1) * DIGIT, :] = both[part]
            for part in range(2):
                table_ref[part, block, GROUPS:, :] = fine[part]
        deep = jnp.concatenate([v_row] * (DIGIT // FINE), 0)
        high = turn_unit(deep * (DIGIT * ids), 2 * M)
        low = turn_unit(deep * ids, 2 * M)
        rows = []
        for row in range(M // DIGIT):
            both = times(row_of(high, row, DIGIT), low)
            rows.append(jnp.concatenate(both, 1).astype(BF16))
        at = slice(block * 2 * LANES, (block + 1) * 2 * LANES)
        whole = jnp.concatenate(rows, 0)
        col_ref[:, at] = whole
        turned_ref[at, :] = whole.T


def tables(u_index, v_index, place, tiles):
    rows = u_index.shape[0]
    vmem = pl.BlockSpec(memory_space=pltpu.VMEM)
    digits = jax.ShapeDtypeStruct((2, tiles, GROUPS + FINE, LANES), F32)
    return pl.pallas_call(
        functools.partial(table_kernel, tiles),
        out_shape=(
            digits,
            digits,
            jax.ShapeDtypeStruct((M, 2 * rows), BF16),
            jax.ShapeDtypeStruct((2 * rows, M), BF16),
            TOKEN,
        ),
        in_specs=[pl.BlockSpec(memory_space=pltpu.SMEM), vmem, vmem],
        out_specs=(vmem,) * 4 + (pl.BlockSpec(memory_space=pltpu.SMEM),),
        compiler_params=pltpu.CompilerParams(vmem_limit_bytes=VMEM_SMALL),
        cost_estimate=pl.CostEstimate(flops=1 << 24, bytes_accessed=4 << 20, transcendentals=1 << 18),
        name="tables",
    )(place, u_index.reshape(tiles, LANES), v_index.reshape(tiles, LANES))


def phases(table_ref, group, chans, block):
    fine = (table_ref[0, block, GROUPS:, :], table_ref[1, block, GROUPS:, :])
    parts = []
    for step in range(chans // FINE):
        rows = pl.ds(group + step, FINE, stride=0)
        parts.append(times((table_ref[0, block, rows, :], table_ref[1, block, rows, :]), fine))
    return (
        jnp.concatenate([part[0] for part in parts], 0),
        jnp.concatenate([part[1] for part in parts], 0),
    )


def paired(count, first, second):
    first(0, 0)

    def body(pair, carry):
        first(2 * pair + 1, 1)
        second(2 * pair, 0)
        first(jnp.minimum(2 * pair + 2, count - 1), 0)
        second(2 * pair + 1, 1)
        return carry

    lax.fori_loop(0, count // 2, body, 0)


def image_kernel(scale, lines, blocks, groups, away, place_ref, step_ref, start_ref, col_ref, *refs):
    vis_refs, (out_ref, token_ref), slots = refs[:blocks], refs[blocks : blocks + 2], refs[blocks + 2 :]
    token_ref[0] = place_ref[0]
    chans = out_ref.shape[1]
    base = lax.rem(place_ref[2] + groups - away, groups) * (chans // FINE)

    def fill(i, slot):
        x_ref = slots[slot]
        rows = pl.ds(pl.multiple_of(i * A_CHANS, A_CHANS), A_CHANS)
        group = base + i * (A_CHANS // FINE)
        for block in range(blocks):
            step = phases(step_ref, group, A_CHANS, block)
            start = phases(start_ref, group, A_CHANS, block)
            vis_ref = vis_refs[block]
            value = conj_times((vis_ref[0, rows, :].astype(F32), -vis_ref[1, rows, :].astype(F32)), start)
            at = block * 2 * LANES
            for line in range(lines):
                into = slice(line * A_CHANS, (line + 1) * A_CHANS)
                x_ref[into, at : at + LANES] = value[0].astype(BF16)
                x_ref[into, at + LANES : at + 2 * LANES] = value[1].astype(BF16)
                if line < lines - 1:
                    value = conj_times(value, step)

    def multiply(i, slot):
        rows = pl.ds(pl.multiple_of(i * A_CHANS, A_CHANS), A_CHANS)
        image = jnp.dot(slots[slot][...], col_ref[...], preferred_element_type=F32)
        out_ref[:, rows, :] = (image * scale).astype(BF16).reshape(lines, A_CHANS, M)

    paired(chans // A_CHANS, fill, multiply)


def make_image(vis, place, step_t, start_t, col, lines, total_rows, groups, away):
    blocks = len(vis)
    _, chans, _ = vis[0].shape
    rows = blocks * LANES
    vmem = pl.BlockSpec(memory_space=pltpu.VMEM)
    flops = 2 * lines * chans * 2 * rows * M
    return pl.pallas_call(
        functools.partial(image_kernel, 1.0 / math.sqrt(total_rows), lines, blocks, groups, away),
        out_shape=(jax.ShapeDtypeStruct((lines, chans, M), BF16), TOKEN),
        in_specs=[pl.BlockSpec(memory_space=pltpu.SMEM)] + [vmem] * (3 + blocks),
        out_specs=(vmem, pl.BlockSpec(memory_space=pltpu.SMEM)),
        scratch_shapes=[pltpu.VMEM((lines * A_CHANS, 2 * rows), BF16)] * 2,
        compiler_params=pltpu.CompilerParams(vmem_limit_bytes=VMEM_SMALL),
        cost_estimate=pl.CostEstimate(flops=flops, bytes_accessed=8 << 20, transcendentals=0),
        name="image",
    )(place, step_t, start_t, col, *vis)


def filter_kernel(groups, step, place_ref, filter_ref, *refs):
    image_refs, out_refs, weight_ref = refs[:groups], refs[groups : 2 * groups], refs[-1]
    lines, chans, _ = out_refs[0].shape
    place = place_ref[2]
    for out_block in range(groups):
        rows = pl.ds(pl.multiple_of(lax.rem(place + out_block, groups) * chans, chans), chans)
        for in_block in range(groups):
            at = lax.rem(place + (groups - in_block), groups) * chans
            weight_ref[
                out_block * chans : (out_block + 1) * chans,
                in_block * chans : (in_block + 1) * chans,
            ] = filter_ref[rows, pl.ds(pl.multiple_of(at, chans), chans)]

    def body(i, carry):
        first = i * step
        image = jnp.concatenate(
            [
                jnp.concatenate([ref[first + line] for line in range(step)], 1)
                for ref in image_refs
            ],
            0,
        )
        result = jnp.dot(weight_ref[...], image, preferred_element_type=F32).astype(BF16)
        for block, out_ref in enumerate(out_refs):
            for line in range(step):
                out_ref[first + line] = result[
                    block * chans : (block + 1) * chans, line * M : (line + 1) * M
                ]
        return carry

    lax.fori_loop(0, lines // step, body, 0)


def filter_images(images, place, fg_filter):
    groups = len(images)
    lines, chans, _ = images[0].shape
    step = min(4, lines)
    vmem = pl.BlockSpec(memory_space=pltpu.VMEM)
    return pl.pallas_call(
        functools.partial(filter_kernel, groups, step),
        out_shape=[jax.ShapeDtypeStruct((lines, chans, M), BF16)] * groups,
        in_specs=[pl.BlockSpec(memory_space=pltpu.SMEM)] + [vmem] * (1 + groups),
        out_specs=[vmem] * groups,
        scratch_shapes=[pltpu.VMEM((F, F), BF16)],
        compiler_params=pltpu.CompilerParams(vmem_limit_bytes=VMEM_FILTER),
        cost_estimate=pl.CostEstimate(
            flops=2 * F * F * lines * M, bytes_accessed=18 << 20, transcendentals=0
        ),
        name="filter",
    )(place, fg_filter, *images)


def predict_kernel(scale, groups, away, place_ref, image_ref, col_ref, step_ref, start_ref, keep_ref, send_ref, *slots):
    lines, chans, _ = image_ref.shape
    blocks = 2 * keep_ref.shape[0]
    count = chans // C_CHANS
    base = lax.rem(place_ref[2] + away, groups) * (chans // FINE)

    def rows_of(i):
        return pl.ds(pl.multiple_of(i * C_CHANS, C_CHANS), C_CHANS)

    def multiply(i, slot, block):
        image = image_ref[:, rows_of(i), :].reshape(lines * C_CHANS, M)
        at = slice(block * 2 * LANES, (block + 1) * 2 * LANES)
        slots[slot][...] = jnp.dot(image, col_ref[:, at], preferred_element_type=F32)

    def collect(i, slot, block):
        h_ref = slots[slot]
        rows = rows_of(i)
        for first in range(0, C_CHANS, C_UNIT):
            group = base + i * (C_CHANS // FINE) + first // FINE
            step = phases(step_ref, group, C_UNIT, block)
            start = phases(start_ref, group, C_UNIT, block)
            total = None
            for line in reversed(range(lines)):
                take = slice(line * C_CHANS + first, line * C_CHANS + first + C_UNIT)
                value = (h_ref[take, :LANES], h_ref[take, LANES:])
                if total is None:
                    total = value
                else:
                    moved = times(total, step)
                    total = (moved[0] + value[0], moved[1] + value[1])
            total = times(total, start)
            real, imag = total[0] * scale, total[1] * -scale
            into = pl.ds(pl.multiple_of(i * C_CHANS + first, C_UNIT), C_UNIT)
            if block < blocks // 2:
                keep_ref[block, 0, into, :] = real
                keep_ref[block, 1, into, :] = imag
            else:
                send_ref[block - blocks // 2, 0, into, :] = real.astype(BF16)
                send_ref[block - blocks // 2, 1, into, :] = imag.astype(BF16)

    def body(i, carry):
        for block in range(blocks):
            if block < blocks - 1:
                multiply(i, (block + 1) % len(slots), block + 1)
            else:
                multiply(jnp.minimum(i + 1, count - 1), 0, 0)
            collect(i, block % len(slots), block)
        return carry

    multiply(0, 0, 0)
    lax.fori_loop(0, count, body, 0)


def predict_part(foreground, place, step_t, start_t, col, groups, away):
    lines, chans, _ = foreground.shape
    rows = col.shape[1] // 2
    vmem = pl.BlockSpec(memory_space=pltpu.VMEM)
    flops = 2 * lines * chans * 2 * rows * M
    half = (rows // LANES // 2, 2, chans, LANES)
    return pl.pallas_call(
        functools.partial(predict_kernel, 1.0 / math.sqrt(L * M), groups, away),
        out_shape=(jax.ShapeDtypeStruct(half, F32), jax.ShapeDtypeStruct(half, BF16)),
        in_specs=[pl.BlockSpec(memory_space=pltpu.SMEM)] + [vmem] * 4,
        out_specs=(vmem, vmem),
        scratch_shapes=[pltpu.VMEM((lines * C_CHANS, 2 * LANES), F32)] * C_SLOTS,
        compiler_params=pltpu.CompilerParams(vmem_limit_bytes=VMEM_SMALL),
        cost_estimate=pl.CostEstimate(flops=flops, bytes_accessed=8 << 20, transcendentals=0),
        name="predict",
    )(place, foreground, col, step_t, start_t)


def local(visibility, flags, u_index, v_index, fg_filter):
    groups, tiles = lax.axis_size("chan"), lax.axis_size("tile")
    chan, tile = lax.axis_index("chan"), lax.axis_index("tile")
    chans = visibility.shape[2]
    total_rows = u_index.shape[0]
    lines = L // (groups * tiles)
    masks = chip_masks(tiles)

    weight = flags.astype(BF16)
    own = jnp.transpose(visibility * weight[:, None, :], (1, 2, 0))
    seen = [own] + [chan_shift(own, groups, away) for away in range(1, groups)]
    place = jnp.stack([tile, (chan * tiles + tile) * lines, chan])
    step_t, start_t, predict_col, image_col, token = tables(u_index, v_index, place, tiles)
    images, tokens = [], [token]
    for away in range(groups):
        block = seen[away]
        if away:
            block = after(block, tokens[min(away - 1, 1)])
        pieces = [tile_swap(block, tiles, mask) for mask in masks[1:]]
        blocks = [block, *pieces]
        if away != 1:
            pieces = lax.optimization_barrier((*pieces, tokens[min(away, 2)]))[:-1]
        blocks += [tile_swap(piece, tiles, 1) for piece in (block, *pieces)]
        image, token = make_image(
            blocks, place, step_t, start_t, image_col, lines, total_rows, groups, away
        )
        images.append(image)
        tokens.append(token)
    foreground = filter_images(images, place, fg_filter)

    parts, first_halves, second_halves = [], [], []
    for turn, away in enumerate(list(range(1, groups)) + [0]):
        here = place
        if turn >= 2:
            here = after(here, first_halves[turn - 2])
        if turn >= 3:
            here = after(here, *second_halves[turn - 3])
        kept, sent = predict_part(
            foreground[away], here, step_t, start_t, predict_col, groups, away
        )
        received = tile_swap(sent, tiles, 1)
        first_halves.append(received)
        total = kept + received.astype(F32)
        received = [
            tile_swap(total[spot].astype(BF16), tiles, mask)
            for spot, mask in enumerate(masks)
            if mask
        ]
        second_halves.append(received)
        part = total[0] + functools.reduce(jnp.add, [piece.astype(F32) for piece in received])
        if away:
            part = chan_shift(part.astype(BF16), groups, away).astype(F32)
        parts.append(part)
    predicted = jnp.transpose(functools.reduce(jnp.add, parts), (2, 0, 1))
    return weight.astype(F32)[:, None, :] * (visibility.astype(F32) - predicted)


def solution(mesh):
    return jax.shard_map(
        local,
        mesh=mesh,
        in_specs=(P("tile", None, "chan"), P("tile", "chan"), P(), P(), P()),
        out_specs=P("tile", None, "chan"),
        check_vma=False,
    )
```

time: 165 us -> 146 us (0.88)
  local copies, waits for them, and re-layouts: 17 us -> 3.57 us
  other arithmetic: 9.75 us -> 2.02 us
  Pallas kernels: 72.2 us -> 76.9 us
  starting transfers between devices: 45.4 us -> 43.1 us
    unnamed x55 -> x7, local copies, waits for them, and re-layouts: 6.94 us -> 2.41 us
    pallas_call x4, Pallas kernels: 26.2 us -> 30 us  [make_image(): pl.pallas_call(functools.partial(image_kernel, 1.0 / math.sqrt(total_rows...]
    cos x5 -> x0, other arithmetic: 3.03 us -> none  [unit(): return (jnp.cos(angle), jnp.sin(angle))]
    ppermute x44, starting transfers between devices: 34.8 us -> 32.6 us  [tile_swap(): return lax.ppermute(block, 'tile', [(t, t ^ mask) for t in range(tiles)])]
    reshape x1 -> x0, local copies, waits for them, and re-layouts: 1.85 us -> none  [local(): predict_col = jnp.stack([cos_col.reshape(M, tiles, LANES), sin_col.reshap...]
    sub x2 -> x0, local copies, waits for them, and re-layouts: 1.82 us -> none  [times(): return (a[0] * b[0] - a[1] * b[1], a[1] * b[0] + a[0] * b[1])]
    gather x2 -> x0, local copies, waits for them, and re-layouts: 1.8 us -> none  [the longest x1 1.24 us: local(): v_rows = v_index.reshape(tiles, LANES)[order].reshape(-1)]
    add x2 -> x0, local copies, waits for them, and re-layouts: 1.79 us -> none  [times(): return (a[0] * b[0] - a[1] * b[1], a[1] * b[0] + a[0] * b[1])]
  transfers between devices with their start and end apart: 50 -> 50, of which waited for: 9 -> 9; matrix products, arithmetic and copies ran while one was open for 12% -> 1% of each run, Pallas kernels for 28% -> 35%
where the time goes in v3:
time: 146 us
  Pallas kernels  76.9 us (53%)
  starting transfers between devices  43.1 us (30%)
  waiting for transfers between devices  19.7 us (13%)
  local copies, waits for them, and re-layouts  3.57 us (2%)
  other arithmetic  2.02 us (1%)
    pallas_call x4, Pallas kernels, predict_part(): pl.pallas_call(functools.partial(predict_kernel, 1.0 / math.sqrt(L * M),...  34 us
    ppermute x44, starting transfers between devices, tile_swap(): return lax.ppermute(block, 'tile', [(t, t ^ mask) for t in range(tiles)])  32.6 us
    pallas_call x4, Pallas kernels, make_image(): pl.pallas_call(functools.partial(image_kernel, 1.0 / math.sqrt(total_rows...  30 us
    ppermute x44, waiting for transfers between devices, tile_swap(): return lax.ppermute(block, 'tile', [(t, t ^ mask) for t in range(tiles)])  19.1 us
    ppermute x6, starting transfers between devices, chan_shift(): lax.ppermute(block, 'chan', [(c, (c + away) % groups) for c in range(grou...  10.5 us
    pallas_call x1, Pallas kernels, filter_images(): pl.pallas_call(functools.partial(filter_kernel, groups, step), out_shape=...  10.1 us
  transfers between devices with their start and end apart: 50, of which 9 were waited for; matrix products, arithmetic and copies ran while one was open for 1% of the time, Pallas kernels for 35%

profile of v3, /device:TPU:0, one launch (start us, length us, event | category | flops | bytes accessed | tf_op | source)
XLA Modules:
  0.0 145.6 jit_solution(5001818949610033877)
XLA Ops:
  2.1 3.1 %collective-permute-start.7 = (bf16[2,256,128]{2,1,0:T(8,128)(2,1)S(1)}, bf16[2,256,128]{2,1,0:T(8,128)(2,1)S(1)}, u32[]{:S(2)}, u32[]{:S(2)}) collective-permute-start(bf16[2,256,128]{2,1,0:T(8,128)(2,1)S(1)} %multiply_bitcast_fusion.refs_0_), channel_id=1, source_target_pairs={{0,8},{8,16},{16,24},{24,0},{1,9},{9,17},{17,25},{25,1},{2,10},{10... | collective-permute-start | bytes 393224 | tf_op jit(solution)/shard_map/ppermute | solution.py:40
  6.7 1.5 %collective-permute-start.1 = (bf16[2,256,128]{2,1,0:T(8,128)(2,1)S(1)}, bf16[2,256,128]{2,1,0:T(8,128)(2,1)S(1)}, u32[]{:S(2)}, u32[]{:S(2)}) collective-permute-start(bf16[2,256,128]{2,1,0:T(8,128)(2,1)S(1)} %multiply_bitcast_fusion.refs_0_), channel_id=1, source_target_pairs={{0,4},{1,5},{2,6},{3,7},{4,0},{5,1},{6,2},{7,3},{8,12},{9,13},{10,... | collective-permute-start | bytes 393224 | tf_op jit(solution)/shard_map/ppermute | solution.py:36
  10.1 2.7 %tables.1 = (f32[2,8,136,128]{3,2,1,0:T(8,128)S(1)}, f32[2,8,136,128]{3,2,1,0:T(8,128)S(1)}, bf16[256,2048]{1,0:T(8,128)(2,1)S(1)}, bf16[2048,256]{1,0:T(8,128)(2,1)S(1)}, s32[1]{0:T(128)}) custom-call(s32[3]{0:T(128)S(1)} %pad_add_fusion.place_ref, s32[8,128]{1,0:T(8,128)S(1)} %bitcast.67, s32[8,128]{1,0:T(8,128)S(1)} %bitcast.68), custom_call_target="tpu_custom_call" | custom-call | flops 16777216 | bytes 4194304 | tf_op jit(solution)/shard_map/tables/pallas_call | solution.py:100
  12.8 2.2 %collective-permute-start.23 = (bf16[2,256,128]{2,1,0:T(8,128)(2,1)S(1)}, bf16[2,256,128]{2,1,0:T(8,128)(2,1)S(1)}, u32[]{:S(2)}, u32[]{:S(2)}) collective-permute-start(bf16[2,256,128]{2,1,0:T(8,128)(2,1)S(1)} %multiply_bitcast_fusion.refs_0_), channel_id=1, source_target_pairs={{0,24},{8,0},{16,8},{24,16},{1,25},{9,1},{17,9},{25,17},{2,26},{10... | collective-permute-start | bytes 393224 | tf_op jit(solution)/shard_map/ppermute | solution.py:40
  15.0 1.6 %collective-permute-start.8 = (bf16[2,256,128]{2,1,0:T(8,128)(2,1)S(1)}, bf16[2,256,128]{2,1,0:T(8,128)(2,1)S(1)}, u32[]{:S(2)}, u32[]{:S(2)}) collective-permute-start(bf16[2,256,128]{2,1,0:T(8,128)(2,1)S(1)} %collective-permute-done.7.refs_0_), channel_id=1, source_target_pairs={{0,2},{1,3},{2,0},{3,1},{4,6},{5,7},{6,4},{7,5},{8,10},{9,11},{10,... | collective-permute-start | bytes 393224 | tf_op jit(solution)/shard_map/ppermute | solution.py:36
  16.6 1.5 %collective-permute-start.9 = (bf16[2,256,128]{2,1,0:T(8,128)(2,1)S(1)}, bf16[2,256,128]{2,1,0:T(8,128)(2,1)S(1)}, u32[]{:S(2)}, u32[]{:S(2)}) collective-permute-start(bf16[2,256,128]{2,1,0:T(8,128)(2,1)S(1)} %collective-permute-done.7.refs_0_), channel_id=1, source_target_pairs={{0,4},{1,5},{2,6},{3,7},{4,0},{5,1},{6,2},{7,3},{8,12},{9,13},{10,... | collective-permute-start | bytes 393224 | tf_op jit(solution)/shard_map/ppermute | solution.py:36
  19.0 1.8 %collective-permute-done.8.refs_1_ = bf16[2,256,128]{2,1,0:T(8,128)(2,1)S(1)} collective-permute-done((bf16[2,256,128]{2,1,0:T(8,128)(2,1)S(1)}, bf16[2,256,128]{2,1,0:T(8,128)(2,1)S(1)}, u32[]{:S(2)}, u32[]{:S(2)}) %collective-permute-start.8) | collective-permute-done | bytes 131104 | tf_op jit(solution)/shard_map/ppermute | solution.py:36
  20.8 4.0 %collective-permute-done.9.refs_2_ = bf16[2,256,128]{2,1,0:T(8,128)(2,1)S(1)} collective-permute-done((bf16[2,256,128]{2,1,0:T(8,128)(2,1)S(1)}, bf16[2,256,128]{2,1,0:T(8,128)(2,1)S(1)}, u32[]{:S(2)}, u32[]{:S(2)}) %collective-permute-start.9) | collective-permute-done | bytes 131104 | tf_op jit(solution)/shard_map/ppermute | solution.py:36
  26.6 7.6 %image.4 = (bf16[16,256,256]{2,1,0:T(8,128)(2,1)S(1)}, s32[1]{0:T(128)}) custom-call(s32[3]{0:T(128)S(1)} %pad_add_fusion.place_ref, f32[2,8,136,128]{3,2,1,0:T(8,128)S(1)} %get-tuple-element.43.step_ref, f32[2,8,136,128]{3,2,1,0:T(8,128)S(1)} %get-tuple-element.44.start_ref, bf16[2048,256]{1,0:T(8,128)(2,1)S(1)} %get-tuple-element.45.col_ref, ...), custom_call_target="tpu_custom_call" | custom-call | flops 4294967296 | bytes 8388608 | tf_op jit(solution)/shard_map/image/pallas_call | solution.py:179
  34.7 1.6 %collective-permute-start.25 = (bf16[2,256,128]{2,1,0:T(8,128)(2,1)S(1)}, bf16[2,256,128]{2,1,0:T(8,128)(2,1)S(1)}, u32[]{:S(2)}, u32[]{:S(2)}) collective-permute-start(bf16[2,256,128]{2,1,0:T(8,128)(2,1)S(1)} %collective-permute-done.23.refs_0_), channel_id=1, source_target_pairs={{0,4},{1,5},{2,6},{3,7},{4,0},{5,1},{6,2},{7,3},{8,12},{9,13},{10,... | collective-permute-start | bytes 393224 | tf_op jit(solution)/shard_map/ppermute | solution.py:36
  38.2 1.6 %collective-permute-start.17 = (bf16[2,256,128]{2,1,0:T(8,128)(2,1)S(1)}, bf16[2,256,128]{2,1,0:T(8,128)(2,1)S(1)}, u32[]{:S(2)}, u32[]{:S(2)}) collective-permute-start(bf16[2,256,128]{2,1,0:T(8,128)(2,1)S(1)} %collective-permute-done.15.refs_0_), channel_id=1, source_target_pairs={{0,4},{1,5},{2,6},{3,7},{4,0},{5,1},{6,2},{7,3},{8,12},{9,13},{10,... | collective-permute-start | bytes 393224 | tf_op jit(solution)/shard_map/ppermute | solution.py:36
  39.9 7.5 %image.5 = (bf16[16,256,256]{2,1,0:T(8,128)(2,1)S(1)}, s32[1]{0:T(128)}) custom-call(s32[3]{0:T(128)S(1)} %pad_add_fusion.place_ref, f32[2,8,136,128]{3,2,1,0:T(8,128)S(1)} %get-tuple-element.43.step_ref, f32[2,8,136,128]{3,2,1,0:T(8,128)S(1)} %get-tuple-element.44.start_ref, bf16[2048,256]{1,0:T(8,128)(2,1)S(1)} %get-tuple-element.45.col_ref, ...), custom_call_target="tpu_custom_call" | custom-call | flops 4294967296 | bytes 8388608 | tf_op jit(solution)/shard_map/image/pallas_call | solution.py:179
  49.9 3.4 %collective-permute-done.18.refs_3_ = bf16[2,256,128]{2,1,0:T(8,128)(2,1)S(1)} collective-permute-done((bf16[2,256,128]{2,1,0:T(8,128)(2,1)S(1)}, bf16[2,256,128]{2,1,0:T(8,128)(2,1)S(1)}, u32[]{:S(2)}, u32[]{:S(2)}) %collective-permute-start.18) | collective-permute-done | bytes 131104 | tf_op jit(solution)/shard_map/ppermute | solution.py:36
  54.3 7.5 %image.7 = (bf16[16,256,256]{2,1,0:T(8,128)(2,1)S(1)}, s32[1]{0:T(128)}) custom-call(s32[3]{0:T(128)S(1)} %pad_add_fusion.place_ref, f32[2,8,136,128]{3,2,1,0:T(8,128)S(1)} %get-tuple-element.43.step_ref, f32[2,8,136,128]{3,2,1,0:T(8,128)S(1)} %get-tuple-element.44.start_ref, bf16[2048,256]{1,0:T(8,128)(2,1)S(1)} %get-tuple-element.45.col_ref, ...), custom_call_target="tpu_custom_call" | custom-call | flops 4294967296 | bytes 8388608 | tf_op jit(solution)/shard_map/image/pallas_call | solution.py:179
  61.8 7.5 %image.6 = (bf16[16,256,256]{2,1,0:T(8,128)(2,1)S(1)}, s32[1]{0:T(128)}) custom-call(s32[3]{0:T(128)S(1)} %pad_add_fusion.place_ref, f32[2,8,136,128]{3,2,1,0:T(8,128)S(1)} %get-tuple-element.43.step_ref, f32[2,8,136,128]{3,2,1,0:T(8,128)S(1)} %get-tuple-element.44.start_ref, bf16[2048,256]{1,0:T(8,128)(2,1)S(1)} %get-tuple-element.45.col_ref, ...), custom_call_target="tpu_custom_call" | custom-call | flops 4294967296 | bytes 8388608 | tf_op jit(solution)/shard_map/image/pallas_call | solution.py:179
  69.3 10.1 %filter.1 = (bf16[16,256,256]{2,1,0:T(8,128)(2,1)S(1)}, bf16[16,256,256]{2,1,0:T(8,128)(2,1)S(1)}, bf16[16,256,256]{2,1,0:T(8,128)(2,1)S(1)}, bf16[16,256,256]{2,1,0:T(8,128)(2,1)S(1)}) custom-call(s32[3]{0:T(128)S(1)} %pad_add_fusion.place_ref, bf16[1024,1024]{1,0:T(8,128)(2,1)S(1)} %copy-done, bf16[16,256,256]{2,1,0:T(8,128)(2,1)S(1)} %get-tuple-element.50.refs_0_, ...), custom_call_target="tpu_custom_call" | custom-call | flops 8589934592 | bytes 18874368 | tf_op jit(solution)/shard_map/filter/pallas_call | solution.py:229
  79.5 8.5 %predict.4 = (f32[4,2,256,128]{3,2,1,0:T(8,128)S(1)}, bf16[4,2,256,128]{3,2,1,0:T(8,128)(2,1)S(1)}) custom-call(s32[3]{0:T(128)S(1)} %pad_add_fusion.place_ref, bf16[16,256,256]{2,1,0:T(8,128)(2,1)S(1)} %get-tuple-element.65.image_ref, bf16[256,2048]{1,0:T(8,128)(2,1)S(1)} %get-tuple-element.66.col_ref, f32[2,8,136,128]{3,2,1,0:T(8,128)S(1)} %get-tuple-element.43.step_ref, ...), custom_call_target="tpu_custom_call" | custom-call | flops 4294967296 | bytes 8388608 | tf_op jit(solution)/shard_map/predict/pallas_call | solution.py:302
  88.1 8.5 %predict.5 = (f32[4,2,256,128]{3,2,1,0:T(8,128)S(1)}, bf16[4,2,256,128]{3,2,1,0:T(8,128)(2,1)S(1)}) custom-call(s32[3]{0:T(128)S(1)} %pad_add_fusion.place_ref, bf16[16,256,256]{2,1,0:T(8,128)(2,1)S(1)} %get-tuple-element.69.image_ref, bf16[256,2048]{1,0:T(8,128)(2,1)S(1)} %get-tuple-element.66.col_ref, f32[2,8,136,128]{3,2,1,0:T(8,128)S(1)} %get-tuple-element.43.step_ref, ...), custom_call_target="tpu_custom_call" | custom-call | flops 4294967296 | bytes 8388608 | tf_op jit(solution)/shard_map/predict/pallas_call | solution.py:302
  97.2 1.6 %collective-permute-start.32 = (bf16[2,256,128]{2,1,0:T(8,128)(2,1)S(1)}, bf16[2,256,128]{2,1,0:T(8,128)(2,1)S(1)}, u32[]{:S(2)}, u32[]{:S(2)}) collective-permute-start(bf16[2,256,128]{2,1,0:T(8,128)(2,1)S(1)} %get-tuple-element.100), channel_id=1, source_target_pairs={{0,2},{1,3},{2,0},{3,1},{4,6},{5,7},{6,4},{7,5},{8,10},{9,11},{10,... | collective-permute-start | bytes 393224 | tf_op jit(solution)/shard_map/ppermute | solution.py:36
  99.3 1.5 %collective-permute-start.34 = (bf16[2,256,128]{2,1,0:T(8,128)(2,1)S(1)}, bf16[2,256,128]{2,1,0:T(8,128)(2,1)S(1)}, u32[]{:S(2)}, u32[]{:S(2)}) collective-permute-start(bf16[2,256,128]{2,1,0:T(8,128)(2,1)S(1)} %get-tuple-element.98), channel_id=1, source_target_pairs={{0,6},{1,7},{2,4},{3,5},{4,2},{5,3},{6,0},{7,1},{8,14},{9,15},{10,... | collective-permute-start | bytes 393224 | tf_op jit(solution)/shard_map/ppermute | solution.py:36
  101.0 1.6 %collective-permute-start.37 = (bf16[2,256,128]{2,1,0:T(8,128)(2,1)S(1)}, bf16[2,256,128]{2,1,0:T(8,128)(2,1)S(1)}, u32[]{:S(2)}, u32[]{:S(2)}) collective-permute-start(bf16[2,256,128]{2,1,0:T(8,128)(2,1)S(1)} %get-tuple-element.89), channel_id=1, source_target_pairs={{0,2},{1,3},{2,0},{3,1},{4,6},{5,7},{6,4},{7,5},{8,10},{9,11},{10,... | collective-permute-start | bytes 393224 | tf_op jit(solution)/shard_map/ppermute | solution.py:36
  103.1 8.7 %predict.6 = (f32[4,2,256,128]{3,2,1,0:T(8,128)S(1)}, bf16[4,2,256,128]{3,2,1,0:T(8,128)(2,1)S(1)}) custom-call(s32[3]{0:T(128)S(1)} %pad_add_fusion.place_ref, bf16[16,256,256]{2,1,0:T(8,128)(2,1)S(1)} %get-tuple-element.73.image_ref, bf16[256,2048]{1,0:T(8,128)(2,1)S(1)} %get-tuple-element.66.col_ref, f32[2,8,136,128]{3,2,1,0:T(8,128)S(1)} %get-tuple-element.43.step_ref, ...), custom_call_target="tpu_custom_call" | custom-call | flops 4294967296 | bytes 8388608 | tf_op jit(solution)/shard_map/predict/pallas_call | solution.py:302
  111.8 1.6 %collective-permute-start.39 = (bf16[2,256,128]{2,1,0:T(8,128)(2,1)S(1)}, bf16[2,256,128]{2,1,0:T(8,128)(2,1)S(1)}, u32[]{:S(2)}, u32[]{:S(2)}) collective-permute-start(bf16[2,256,128]{2,1,0:T(8,128)(2,1)S(1)} %get-tuple-element.90), channel_id=1, source_target_pairs={{0,6},{1,7},{2,4},{3,5},{4,2},{5,3},{6,0},{7,1},{8,14},{9,15},{10,... | collective-permute-start | bytes 393224 | tf_op jit(solution)/shard_map/ppermute | solution.py:36
  113.4 1.6 %collective-permute-start.35 = (bf16[2,256,128]{2,1,0:T(8,128)(2,1)S(1)}, bf16[2,256,128]{2,1,0:T(8,128)(2,1)S(1)}, u32[]{:S(2)}, u32[]{:S(2)}) collective-permute-start(bf16[2,256,128]{2,1,0:T(8,128)(2,1)S(1)} %fusion.10), channel_id=1, source_target_pairs={{0,8},{8,16},{16,24},{24,0},{1,9},{9,17},{17,25},{25,1},{2,10},{10... | collective-permute-start | bytes 393224 | tf_op jit(solution)/shard_map/ppermute | solution.py:40
  115.0 8.5 %predict.7 = (f32[4,2,256,128]{3,2,1,0:T(8,128)S(1)}, bf16[4,2,256,128]{3,2,1,0:T(8,128)(2,1)S(1)}) custom-call(s32[3]{0:T(128)S(1)} %pad_add_fusion.place_ref, bf16[16,256,256]{2,1,0:T(8,128)(2,1)S(1)} %get-tuple-element.78.image_ref, bf16[256,2048]{1,0:T(8,128)(2,1)S(1)} %get-tuple-element.66.col_ref, f32[2,8,136,128]{3,2,1,0:T(8,128)S(1)} %get-tuple-element.43.step_ref, ...), custom_call_target="tpu_custom_call" | custom-call | flops 4294967296 | bytes 8388608 | tf_op jit(solution)/shard_map/predict/pallas_call | solution.py:302
  124.0 1.6 %collective-permute-start.42 = (bf16[2,256,128]{2,1,0:T(8,128)(2,1)S(1)}, bf16[2,256,128]{2,1,0:T(8,128)(2,1)S(1)}, u32[]{:S(2)}, u32[]{:S(2)}) collective-permute-start(bf16[2,256,128]{2,1,0:T(8,128)(2,1)S(1)} %get-tuple-element.92), channel_id=1, source_target_pairs={{0,2},{1,3},{2,0},{3,1},{4,6},{5,7},{6,4},{7,5},{8,10},{9,11},{10,... | collective-permute-start | bytes 393224 | tf_op jit(solution)/shard_map/ppermute | solution.py:36
  127.6 2.5 %collective-permute-done.42 = bf16[2,256,128]{2,1,0:T(8,128)(2,1)S(1)} collective-permute-done((bf16[2,256,128]{2,1,0:T(8,128)(2,1)S(1)}, bf16[2,256,128]{2,1,0:T(8,128)(2,1)S(1)}, u32[]{:S(2)}, u32[]{:S(2)}) %collective-permute-start.42) | collective-permute-done | bytes 131104 | tf_op jit(solution)/shard_map/ppermute | solution.py:36
  130.7 3.1 %collective-permute-done.43 = bf16[2,256,128]{2,1,0:T(8,128)(2,1)S(1)} collective-permute-done((bf16[2,256,128]{2,1,0:T(8,128)(2,1)S(1)}, bf16[2,256,128]{2,1,0:T(8,128)(2,1)S(1)}, u32[]{:S(2)}, u32[]{:S(2)}) %collective-permute-start.43) | collective-permute-done | bytes 131104 | tf_op jit(solution)/shard_map/ppermute | solution.py:36
  133.9 2.3 %collective-permute-start.45 = (bf16[2,256,128]{2,1,0:T(8,128)(2,1)S(1)}, bf16[2,256,128]{2,1,0:T(8,128)(2,1)S(1)}, u32[]{:S(2)}, u32[]{:S(2)}) collective-permute-start(bf16[2,256,128]{2,1,0:T(8,128)(2,1)S(1)} %fusion.6), channel_id=1, source_target_pairs={{0,24},{8,0},{16,8},{24,16},{1,25},{9,1},{17,9},{25,17},{2,26},{10... | collective-permute-start | bytes 393224 | tf_op jit(solution)/shard_map/ppermute | solution.py:40
  138.2 1.8 %collective-permute-start.49 = (bf16[2,256,128]{2,1,0:T(8,128)(2,1)S(1)}, bf16[2,256,128]{2,1,0:T(8,128)(2,1)S(1)}, u32[]{:S(2)}, u32[]{:S(2)}) collective-permute-start(bf16[2,256,128]{2,1,0:T(8,128)(2,1)S(1)} %get-tuple-element.96), channel_id=1, source_target_pairs={{0,6},{1,7},{2,4},{3,5},{4,2},{5,3},{6,0},{7,1},{8,14},{9,15},{10,... | collective-permute-start | bytes 393224 | tf_op jit(solution)/shard_map/ppermute | solution.py:36
  140.3 1.9 %collective-permute-done.47 = bf16[2,256,128]{2,1,0:T(8,128)(2,1)S(1)} collective-permute-done((bf16[2,256,128]{2,1,0:T(8,128)(2,1)S(1)}, bf16[2,256,128]{2,1,0:T(8,128)(2,1)S(1)}, u32[]{:S(2)}, u32[]{:S(2)}) %collective-permute-start.47) | collective-permute-done | bytes 131104 | tf_op jit(solution)/shard_map/ppermute | solution.py:36
  142.2 2.4 %collective-permute-done.48 = bf16[2,256,128]{2,1,0:T(8,128)(2,1)S(1)} collective-permute-done((bf16[2,256,128]{2,1,0:T(8,128)(2,1)S(1)}, bf16[2,256,128]{2,1,0:T(8,128)(2,1)S(1)}, u32[]{:S(2)}, u32[]{:S(2)}) %collective-permute-start.48) | collective-permute-done | bytes 131104 | tf_op jit(solution)/shard_map/ppermute | solution.py:36
  (103 shorter events, 22.8 us)
Async XLA Ops:
  2.1 10.7 %collective-permute-start.7 = (bf16[2,256,128]{2,1,0:T(8,128)(2,1)S(1)}, bf16[2,256,128]{2,1,0:T(8,128)(2,1)S(1)}, u32[]{:S(2)}, u32[]{:S(2)}) collective-permute-start(bf16[2,256,128]{2,1,0:T(8,128)(2,1)S(1)} %multiply_bitcast_fusion.refs_0_), channel_id=1, source_target_pairs={{0,8},{8,16},{16,24},{24,0},{1,9},{9,17},{17,25},{25,1},{2,10},{10... | collective-permute-start | bytes 393224 | tf_op jit(solution)/shard_map/ppermute | solution.py:40
  5.2 9.8 %collective-permute-start = (bf16[2,256,128]{2,1,0:T(8,128)(2,1)S(1)}, bf16[2,256,128]{2,1,0:T(8,128)(2,1)S(1)}, u32[]{:S(2)}, u32[]{:S(2)}) collective-permute-start(bf16[2,256,128]{2,1,0:T(8,128)(2,1)S(1)} %multiply_bitcast_fusion.refs_0_), channel_id=1, source_target_pairs={{0,2},{1,3},{2,0},{3,1},{4,6},{5,7},{6,4},{7,5},{8,10},{9,11},{10,... | collective-permute-start | bytes 393224 | tf_op jit(solution)/shard_map/ppermute | solution.py:36
  6.7 9.9 %collective-permute-start.1 = (bf16[2,256,128]{2,1,0:T(8,128)(2,1)S(1)}, bf16[2,256,128]{2,1,0:T(8,128)(2,1)S(1)}, u32[]{:S(2)}, u32[]{:S(2)}) collective-permute-start(bf16[2,256,128]{2,1,0:T(8,128)(2,1)S(1)} %multiply_bitcast_fusion.refs_0_), channel_id=1, source_target_pairs={{0,4},{1,5},{2,6},{3,7},{4,0},{5,1},{6,2},{7,3},{8,12},{9,13},{10,... | collective-permute-start | bytes 393224 | tf_op jit(solution)/shard_map/ppermute | solution.py:36
  8.2 9.9 %collective-permute-start.2 = (bf16[2,256,128]{2,1,0:T(8,128)(2,1)S(1)}, bf16[2,256,128]{2,1,0:T(8,128)(2,1)S(1)}, u32[]{:S(2)}, u32[]{:S(2)}) collective-permute-start(bf16[2,256,128]{2,1,0:T(8,128)(2,1)S(1)} %multiply_bitcast_fusion.refs_0_), channel_id=1, source_target_pairs={{0,6},{1,7},{2,4},{3,5},{4,2},{5,3},{6,0},{7,1},{8,14},{9,15},{10,... | collective-permute-start | bytes 393224 | tf_op jit(solution)/shard_map/ppermute | solution.py:36
  8.7 9.8 %collective-permute-start.3 = (bf16[2,256,128]{2,1,0:T(8,128)(2,1)S(1)}, bf16[2,256,128]{2,1,0:T(8,128)(2,1)S(1)}, u32[]{:S(2)}, u32[]{:S(2)}) collective-permute-start(bf16[2,256,128]{2,1,0:T(8,128)(2,1)S(1)} %multiply_bitcast_fusion.refs_0_), channel_id=1, source_target_pairs={{0,1},{1,0},{2,3},{3,2},{4,5},{5,4},{6,7},{7,6},{8,9},{9,8},{10,11... | collective-permute-start | bytes 393224 | tf_op jit(solution)/shard_map/ppermute | solution.py:36
  16.6 8.2 %collective-permute-start.9 = (bf16[2,256,128]{2,1,0:T(8,128)(2,1)S(1)}, bf16[2,256,128]{2,1,0:T(8,128)(2,1)S(1)}, u32[]{:S(2)}, u32[]{:S(2)}) collective-permute-start(bf16[2,256,128]{2,1,0:T(8,128)(2,1)S(1)} %collective-permute-done.7.refs_0_), channel_id=1, source_target_pairs={{0,4},{1,5},{2,6},{3,7},{4,0},{5,1},{6,2},{7,3},{8,12},{9,13},{10,... | collective-permute-start | bytes 393224 | tf_op jit(solution)/shard_map/ppermute | solution.py:36
  24.8 9.5 %collective-permute-start.15 = (bf16[2,256,128]{2,1,0:T(8,128)(2,1)S(1)}, bf16[2,256,128]{2,1,0:T(8,128)(2,1)S(1)}, u32[]{:S(2)}, u32[]{:S(2)}) collective-permute-start(bf16[2,256,128]{2,1,0:T(8,128)(2,1)S(1)} %multiply_bitcast_fusion.refs_0_), channel_id=1, source_target_pairs={{0,16},{8,24},{16,0},{24,8},{1,17},{9,25},{17,1},{25,9},{2,18},{10... | collective-permute-start | bytes 393224 | tf_op jit(solution)/shard_map/ppermute | solution.py:40
  25.6 9.2 %collective-permute-start.11 = (bf16[2,256,128]{2,1,0:T(8,128)(2,1)S(1)}, bf16[2,256,128]{2,1,0:T(8,128)(2,1)S(1)}, u32[]{:S(2)}, u32[]{:S(2)}) collective-permute-start(bf16[2,256,128]{2,1,0:T(8,128)(2,1)S(1)} %collective-permute-done.7.refs_0_), channel_id=1, source_target_pairs={{0,1},{1,0},{2,3},{3,2},{4,5},{5,4},{6,7},{7,6},{8,9},{9,8},{10,11... | collective-permute-start | bytes 393224 | tf_op jit(solution)/shard_map/ppermute | solution.py:36
  25.6 10.8 %collective-permute-start.12 = (bf16[2,256,128]{2,1,0:T(8,128)(2,1)S(1)}, bf16[2,256,128]{2,1,0:T(8,128)(2,1)S(1)}, u32[]{:S(2)}, u32[]{:S(2)}) collective-permute-start(bf16[2,256,128]{2,1,0:T(8,128)(2,1)S(1)} %collective-permute-done.8.refs_1_), channel_id=1, source_target_pairs={{0,1},{1,0},{2,3},{3,2},{4,5},{5,4},{6,7},{7,6},{8,9},{9,8},{10,11... | collective-permute-start | bytes 393224 | tf_op jit(solution)/shard_map/ppermute | solution.py:36
  26.1 11.7 %collective-permute-start.13 = (bf16[2,256,128]{2,1,0:T(8,128)(2,1)S(1)}, bf16[2,256,128]{2,1,0:T(8,128)(2,1)S(1)}, u32[]{:S(2)}, u32[]{:S(2)}) collective-permute-start(bf16[2,256,128]{2,1,0:T(8,128)(2,1)S(1)} %collective-permute-done.9.refs_2_), channel_id=1, source_target_pairs={{0,1},{1,0},{2,3},{3,2},{4,5},{5,4},{6,7},{7,6},{8,9},{9,8},{10,11... | collective-permute-start | bytes 393224 | tf_op jit(solution)/shard_map/ppermute | solution.py:36
  26.1 12.1 %collective-permute-start.14 = (bf16[2,256,128]{2,1,0:T(8,128)(2,1)S(1)}, bf16[2,256,128]{2,1,0:T(8,128)(2,1)S(1)}, u32[]{:S(2)}, u32[]{:S(2)}) collective-permute-start(bf16[2,256,128]{2,1,0:T(8,128)(2,1)S(1)} %collective-permute-done.10.refs_3_), channel_id=1, source_target_pairs={{0,1},{1,0},{2,3},{3,2},{4,5},{5,4},{6,7},{7,6},{8,9},{9,8},{10,11... | collective-permute-start | bytes 393224 | tf_op jit(solution)/shard_map/ppermute | solution.py:36
  34.2 13.1 %collective-permute-start.24 = (bf16[2,256,128]{2,1,0:T(8,128)(2,1)S(1)}, bf16[2,256,128]{2,1,0:T(8,128)(2,1)S(1)}, u32[]{:S(2)}, u32[]{:S(2)}) collective-permute-start(bf16[2,256,128]{2,1,0:T(8,128)(2,1)S(1)} %collective-permute-done.23.refs_0_), channel_id=1, source_target_pairs={{0,2},{1,3},{2,0},{3,1},{4,6},{5,7},{6,4},{7,5},{8,10},{9,11},{10,... | collective-permute-start | bytes 393224 | tf_op jit(solution)/shard_map/ppermute | solution.py:36
  34.7 14.1 %collective-permute-start.25 = (bf16[2,256,128]{2,1,0:T(8,128)(2,1)S(1)}, bf16[2,256,128]{2,1,0:T(8,128)(2,1)S(1)}, u32[]{:S(2)}, u32[]{:S(2)}) collective-permute-start(bf16[2,256,128]{2,1,0:T(8,128)(2,1)S(1)} %collective-permute-done.23.refs_0_), channel_id=1, source_target_pairs={{0,4},{1,5},{2,6},{3,7},{4,0},{5,1},{6,2},{7,3},{8,12},{9,13},{10,... | collective-permute-start | bytes 393224 | tf_op jit(solution)/shard_map/ppermute | solution.py:36
  36.4 12.5 %collective-permute-start.26 = (bf16[2,256,128]{2,1,0:T(8,128)(2,1)S(1)}, bf16[2,256,128]{2,1,0:T(8,128)(2,1)S(1)}, u32[]{:S(2)}, u32[]{:S(2)}) collective-permute-start(bf16[2,256,128]{2,1,0:T(8,128)(2,1)S(1)} %collective-permute-done.23.refs_0_), channel_id=1, source_target_pairs={{0,6},{1,7},{2,4},{3,5},{4,2},{5,3},{6,0},{7,1},{8,14},{9,15},{10,... | collective-permute-start | bytes 393224 | tf_op jit(solution)/shard_map/ppermute | solution.py:36
  37.8 11.6 %collective-permute-start.16 = (bf16[2,256,128]{2,1,0:T(8,128)(2,1)S(1)}, bf16[2,256,128]{2,1,0:T(8,128)(2,1)S(1)}, u32[]{:S(2)}, u32[]{:S(2)}) collective-permute-start(bf16[2,256,128]{2,1,0:T(8,128)(2,1)S(1)} %collective-permute-done.15.refs_0_), channel_id=1, source_target_pairs={{0,2},{1,3},{2,0},{3,1},{4,6},{5,7},{6,4},{7,5},{8,10},{9,11},{10,... | collective-permute-start | bytes 393224 | tf_op jit(solution)/shard_map/ppermute | solution.py:36
  38.2 11.2 %collective-permute-start.17 = (bf16[2,256,128]{2,1,0:T(8,128)(2,1)S(1)}, bf16[2,256,128]{2,1,0:T(8,128)(2,1)S(1)}, u32[]{:S(2)}, u32[]{:S(2)}) collective-permute-start(bf16[2,256,128]{2,1,0:T(8,128)(2,1)S(1)} %collective-permute-done.15.refs_0_), channel_id=1, source_target_pairs={{0,4},{1,5},{2,6},{3,7},{4,0},{5,1},{6,2},{7,3},{8,12},{9,13},{10,... | collective-permute-start | bytes 393224 | tf_op jit(solution)/shard_map/ppermute | solution.py:36
  53.3 8.5 %collective-permute-start.19 = (bf16[2,256,128]{2,1,0:T(8,128)(2,1)S(1)}, bf16[2,256,128]{2,1,0:T(8,128)(2,1)S(1)}, u32[]{:S(2)}, u32[]{:S(2)}) collective-permute-start(bf16[2,256,128]{2,1,0:T(8,128)(2,1)S(1)} %collective-permute-done.15.refs_0_), channel_id=1, source_target_pairs={{0,1},{1,0},{2,3},{3,2},{4,5},{5,4},{6,7},{7,6},{8,9},{9,8},{10,11... | collective-permute-start | bytes 393224 | tf_op jit(solution)/shard_map/ppermute | solution.py:36
  53.3 8.5 %collective-permute-start.20 = (bf16[2,256,128]{2,1,0:T(8,128)(2,1)S(1)}, bf16[2,256,128]{2,1,0:T(8,128)(2,1)S(1)}, u32[]{:S(2)}, u32[]{:S(2)}) collective-permute-start(bf16[2,256,128]{2,1,0:T(8,128)(2,1)S(1)} %collective-permute-done.16.refs_1_), channel_id=1, source_target_pairs={{0,1},{1,0},{2,3},{3,2},{4,5},{5,4},{6,7},{7,6},{8,9},{9,8},{10,11... | collective-permute-start | bytes 393224 | tf_op jit(solution)/shard_map/ppermute | solution.py:36
  53.8 8.0 %collective-permute-start.21 = (bf16[2,256,128]{2,1,0:T(8,128)(2,1)S(1)}, bf16[2,256,128]{2,1,0:T(8,128)(2,1)S(1)}, u32[]{:S(2)}, u32[]{:S(2)}) collective-permute-start(bf16[2,256,128]{2,1,0:T(8,128)(2,1)S(1)} %collective-permute-done.17.refs_2_), channel_id=1, source_target_pairs={{0,1},{1,0},{2,3},{3,2},{4,5},{5,4},{6,7},{7,6},{8,9},{9,8},{10,11... | collective-permute-start | bytes 393224 | tf_op jit(solution)/shard_map/ppermute | solution.py:36
  53.9 8.0 %collective-permute-start.22 = (bf16[2,256,128]{2,1,0:T(8,128)(2,1)S(1)}, bf16[2,256,128]{2,1,0:T(8,128)(2,1)S(1)}, u32[]{:S(2)}, u32[]{:S(2)}) collective-permute-start(bf16[2,256,128]{2,1,0:T(8,128)(2,1)S(1)} %collective-permute-done.18.refs_3_), channel_id=1, source_target_pairs={{0,1},{1,0},{2,3},{3,2},{4,5},{5,4},{6,7},{7,6},{8,9},{9,8},{10,11... | collective-permute-start | bytes 393224 | tf_op jit(solution)/shard_map/ppermute | solution.py:36
  87.9 9.1 %collective-permute-start.31 = (bf16[4,2,256,128]{3,2,1,0:T(8,128)(2,1)S(1)}, bf16[4,2,256,128]{3,2,1,0:T(8,128)(2,1)S(1)}, u32[]{:S(2)}, u32[]{:S(2)}) collective-permute-start(bf16[4,2,256,128]{3,2,1,0:T(8,128)(2,1)S(1)} %get-tuple-element.68), channel_id=1, source_target_pairs={{0,1},{1,0},{2,3},{3,2},{4,5},{5,4},{6,7},{7,6},{8,9},{9,8},{10,11... | collective-permute-start | bytes 1572872 | tf_op jit(solution)/shard_map/ppermute | solution.py:36
  97.2 14.5 %collective-permute-start.32 = (bf16[2,256,128]{2,1,0:T(8,128)(2,1)S(1)}, bf16[2,256,128]{2,1,0:T(8,128)(2,1)S(1)}, u32[]{:S(2)}, u32[]{:S(2)}) collective-permute-start(bf16[2,256,128]{2,1,0:T(8,128)(2,1)S(1)} %get-tuple-element.100), channel_id=1, source_target_pairs={{0,2},{1,3},{2,0},{3,1},{4,6},{5,7},{6,4},{7,5},{8,10},{9,11},{10,... | collective-permute-start | bytes 393224 | tf_op jit(solution)/shard_map/ppermute | solution.py:36
  98.8 14.5 %collective-permute-start.33 = (bf16[2,256,128]{2,1,0:T(8,128)(2,1)S(1)}, bf16[2,256,128]{2,1,0:T(8,128)(2,1)S(1)}, u32[]{:S(2)}, u32[]{:S(2)}) collective-permute-start(bf16[2,256,128]{2,1,0:T(8,128)(2,1)S(1)} %get-tuple-element.99), channel_id=1, source_target_pairs={{0,4},{1,5},{2,6},{3,7},{4,0},{5,1},{6,2},{7,3},{8,12},{9,13},{10,... | collective-permute-start | bytes 393224 | tf_op jit(solution)/shard_map/ppermute | solution.py:36
  99.3 14.0 %collective-permute-start.34 = (bf16[2,256,128]{2,1,0:T(8,128)(2,1)S(1)}, bf16[2,256,128]{2,1,0:T(8,128)(2,1)S(1)}, u32[]{:S(2)}, u32[]{:S(2)}) collective-permute-start(bf16[2,256,128]{2,1,0:T(8,128)(2,1)S(1)} %get-tuple-element.98), channel_id=1, source_target_pairs={{0,6},{1,7},{2,4},{3,5},{4,2},{5,3},{6,0},{7,1},{8,14},{9,15},{10,... | collective-permute-start | bytes 393224 | tf_op jit(solution)/shard_map/ppermute | solution.py:36
  101.0 23.0 %collective-permute-start.37 = (bf16[2,256,128]{2,1,0:T(8,128)(2,1)S(1)}, bf16[2,256,128]{2,1,0:T(8,128)(2,1)S(1)}, u32[]{:S(2)}, u32[]{:S(2)}) collective-permute-start(bf16[2,256,128]{2,1,0:T(8,128)(2,1)S(1)} %get-tuple-element.89), channel_id=1, source_target_pairs={{0,2},{1,3},{2,0},{3,1},{4,6},{5,7},{6,4},{7,5},{8,10},{9,11},{10,... | collective-permute-start | bytes 393224 | tf_op jit(solution)/shard_map/ppermute | solution.py:36
  102.6 23.0 %collective-permute-start.38 = (bf16[2,256,128]{2,1,0:T(8,128)(2,1)S(1)}, bf16[2,256,128]{2,1,0:T(8,128)(2,1)S(1)}, u32[]{:S(2)}, u32[]{:S(2)}) collective-permute-start(bf16[2,256,128]{2,1,0:T(8,128)(2,1)S(1)} %get-tuple-element.91), channel_id=1, source_target_pairs={{0,4},{1,5},{2,6},{3,7},{4,0},{5,1},{6,2},{7,3},{8,12},{9,13},{10,... | collective-permute-start | bytes 393224 | tf_op jit(solution)/shard_map/ppermute | solution.py:36
  111.8 14.3 %collective-permute-start.39 = (bf16[2,256,128]{2,1,0:T(8,128)(2,1)S(1)}, bf16[2,256,128]{2,1,0:T(8,128)(2,1)S(1)}, u32[]{:S(2)}, u32[]{:S(2)}) collective-permute-start(bf16[2,256,128]{2,1,0:T(8,128)(2,1)S(1)} %get-tuple-element.90), channel_id=1, source_target_pairs={{0,6},{1,7},{2,4},{3,5},{4,2},{5,3},{6,0},{7,1},{8,14},{9,15},{10,... | collective-permute-start | bytes 393224 | tf_op jit(solution)/shard_map/ppermute | solution.py:36
  113.3 10.2 %collective-permute-start.41 = (bf16[4,2,256,128]{3,2,1,0:T(8,128)(2,1)S(1)}, bf16[4,2,256,128]{3,2,1,0:T(8,128)(2,1)S(1)}, u32[]{:S(2)}, u32[]{:S(2)}) collective-permute-start(bf16[4,2,256,128]{3,2,1,0:T(8,128)(2,1)S(1)} %get-tuple-element.75), channel_id=1, source_target_pairs={{0,1},{1,0},{2,3},{3,2},{4,5},{5,4},{6,7},{7,6},{8,9},{9,8},{10,11... | collective-permute-start | bytes 1572872 | tf_op jit(solution)/shard_map/ppermute | solution.py:36
  113.4 24.8 %collective-permute-start.35 = (bf16[2,256,128]{2,1,0:T(8,128)(2,1)S(1)}, bf16[2,256,128]{2,1,0:T(8,128)(2,1)S(1)}, u32[]{:S(2)}, u32[]{:S(2)}) collective-permute-start(bf16[2,256,128]{2,1,0:T(8,128)(2,1)S(1)} %fusion.10), channel_id=1, source_target_pairs={{0,8},{8,16},{16,24},{24,0},{1,9},{9,17},{17,25},{25,1},{2,10},{10... | collective-permute-start | bytes 393224 | tf_op jit(solution)/shard_map/ppermute | solution.py:40
  123.5 12.7 %collective-permute-start.46 = (bf16[4,2,256,128]{3,2,1,0:T(8,128)(2,1)S(1)}, bf16[4,2,256,128]{3,2,1,0:T(8,128)(2,1)S(1)}, u32[]{:S(2)}, u32[]{:S(2)}) collective-permute-start(bf16[4,2,256,128]{3,2,1,0:T(8,128)(2,1)S(1)} %get-tuple-element.80), channel_id=1, source_target_pairs={{0,1},{1,0},{2,3},{3,2},{4,5},{5,4},{6,7},{7,6},{8,9},{9,8},{10,11... | collective-permute-start | bytes 1572872 | tf_op jit(solution)/shard_map/ppermute | solution.py:36
  125.6 8.2 %collective-permute-start.43 = (bf16[2,256,128]{2,1,0:T(8,128)(2,1)S(1)}, bf16[2,256,128]{2,1,0:T(8,128)(2,1)S(1)}, u32[]{:S(2)}, u32[]{:S(2)}) collective-permute-start(bf16[2,256,128]{2,1,0:T(8,128)(2,1)S(1)} %get-tuple-element.94), channel_id=1, source_target_pairs={{0,4},{1,5},{2,6},{3,7},{4,0},{5,1},{6,2},{7,3},{8,12},{9,13},{10,... | collective-permute-start | bytes 393224 | tf_op jit(solution)/shard_map/ppermute | solution.py:36
  130.1 9.9 %collective-permute-start.40 = (bf16[2,256,128]{2,1,0:T(8,128)(2,1)S(1)}, bf16[2,256,128]{2,1,0:T(8,128)(2,1)S(1)}, u32[]{:S(2)}, u32[]{:S(2)}) collective-permute-start(bf16[2,256,128]{2,1,0:T(8,128)(2,1)S(1)} %fusion.8), channel_id=1, source_target_pairs={{0,16},{8,24},{16,0},{24,8},{1,17},{9,25},{17,1},{25,9},{2,18},{10... | collective-permute-start | bytes 393224 | tf_op jit(solution)/shard_map/ppermute | solution.py:40
  (21 other events, 117.0 us)

commit v4 on v3

--- a/solution.py
+++ b/solution.py
@@ -16,7 +16,6 @@
 FINE = 8
 DIGIT = 16
 GROUPS = F // FINE
-TOKEN = jax.ShapeDtypeStruct((1,), jnp.int32)
 LANES = 128
 A_CHANS = 16
 C_CHANS = 64
@@ -40,6 +39,10 @@
     return lax.ppermute(block, "chan", [(c, (c + away) % groups) for c in range(groups)])
 
 
+def wrapped(value, count):
+    return jnp.where(value >= count, value - count, value)
+
+
 def after(value, *others):
     return lax.optimization_barrier((value, *others))[0]
 
@@ -61,25 +64,20 @@
     return tuple(jnp.broadcast_to(part[row : row + 1], (height, LANES)) for part in pair)
 
 
-def table_kernel(tiles, place_ref, u_ref, v_ref, step_ref, start_ref, col_ref, turned_ref, token_ref):
-    tile, first_line = place_ref[0], place_ref[1]
+def table_kernel(lines, tiles, u_ref, v_ref, step_c, step_f, start_c, start_f, col_ref, turned_ref):
+    tile = lax.axis_index("tile")
+    first_line = (lax.axis_index("chan") * tiles + tile) * lines
     ids = lax.broadcasted_iota(jnp.int32, (DIGIT, LANES), 0)
-    token_ref[0] = tile
+    spots = lax.broadcasted_iota(jnp.int32, (tiles, LANES), 0)
     masks = chip_masks(tiles)
+    u_all = jnp.zeros((tiles, LANES), jnp.int32)
     for block, mask in enumerate(masks + [mask ^ 1 for mask in masks]):
         source = pl.ds(tile ^ mask, FINE, stride=0)
         u_row, v_row = u_ref[source, :], v_ref[source, :]
-        for scaled, table_ref in ((u_row, step_ref), (u_row * first_line, start_ref)):
-            deep = jnp.concatenate([scaled] * (DIGIT // FINE), 0)
-            high = turn_unit(deep * (F + FINE * DIGIT * ids), F * L)
-            low = turn_unit(deep * (FINE * ids), F * L)
-            fine = turn_unit(scaled * ids[:FINE], F * L)
-            for row in range(GROUPS // DIGIT):
-                both = times(row_of(high, row, DIGIT), low)
-                for part in range(2):
-                    table_ref[part, block, row * DIGIT : (row + 1) * DIGIT, :] = both[part]
-            for part in range(2):
-                table_ref[part, block, GROUPS:, :] = fine[part]
+        u_all = jnp.where(spots == block, jnp.concatenate([u_row] * (tiles // FINE), 0), u_all)
+        step_f[0, block], step_f[1, block] = turn_unit(u_row * ids[:FINE], F * L)
+        scaled = u_row * first_line
+        start_f[0, block], start_f[1, block] = turn_unit(scaled * ids[:FINE], F * L)
         deep = jnp.concatenate([v_row] * (DIGIT // FINE), 0)
         high = turn_unit(deep * (DIGIT * ids), 2 * M)
         low = turn_unit(deep * ids, 2 * M)
@@ -91,35 +89,47 @@
         whole = jnp.concatenate(rows, 0)
         col_ref[:, at] = whole
         turned_ref[at, :] = whole.T
-
-
-def tables(u_index, v_index, place, tiles):
+    for scaled, coarse_ref in ((u_all, step_c), (u_all * first_line, start_c)):
+        low = [turn_unit(scaled * (FINE * d), F * L) for d in range(DIGIT)]
+        for row in range(GROUPS // DIGIT):
+            high = turn_unit(scaled * (F + FINE * DIGIT * row), F * L)
+            for d in range(DIGIT):
+                coarse_ref[row * DIGIT + d] = jnp.concatenate(times(high, low[d]), 0)
+
+
+def tables(u_index, v_index, lines, tiles):
     rows = u_index.shape[0]
     vmem = pl.BlockSpec(memory_space=pltpu.VMEM)
-    digits = jax.ShapeDtypeStruct((2, tiles, GROUPS + FINE, LANES), F32)
+    coarse = jax.ShapeDtypeStruct((GROUPS, 2 * tiles, LANES), F32)
+    fine = jax.ShapeDtypeStruct((2, tiles, FINE, LANES), F32)
     return pl.pallas_call(
-        functools.partial(table_kernel, tiles),
+        functools.partial(table_kernel, lines, tiles),
         out_shape=(
-            digits,
-            digits,
+            coarse,
+            fine,
+            coarse,
+            fine,
             jax.ShapeDtypeStruct((M, 2 * rows), BF16),
             jax.ShapeDtypeStruct((2 * rows, M), BF16),
-            TOKEN,
         ),
-        in_specs=[pl.BlockSpec(memory_space=pltpu.SMEM), vmem, vmem],
-        out_specs=(vmem,) * 4 + (pl.BlockSpec(memory_space=pltpu.SMEM),),
+        in_specs=[vmem, vmem],
+        out_specs=(vmem,) * 6,
         compiler_params=pltpu.CompilerParams(vmem_limit_bytes=VMEM_SMALL),
-        cost_estimate=pl.CostEstimate(flops=1 << 24, bytes_accessed=4 << 20, transcendentals=1 << 18),
+        cost_estimate=pl.CostEstimate(flops=3 << 30, bytes_accessed=4 << 20, transcendentals=0),
         name="tables",
-    )(place, u_index.reshape(tiles, LANES), v_index.reshape(tiles, LANES))
-
-
-def phases(table_ref, group, chans, block):
-    fine = (table_ref[0, block, GROUPS:, :], table_ref[1, block, GROUPS:, :])
+    )(u_index.reshape(tiles, LANES), v_index.reshape(tiles, LANES))
+
+
+def phases(coarse_ref, fine_ref, group, chans, block):
+    fine = (fine_ref[0, block], fine_ref[1, block])
+    tiles = fine_ref.shape[1]
     parts = []
     for step in range(chans // FINE):
-        rows = pl.ds(group + step, FINE, stride=0)
-        parts.append(times((table_ref[0, block, rows, :], table_ref[1, block, rows, :]), fine))
+        coarse = [
+            coarse_ref[group + step, pl.ds(part * tiles + block, FINE, stride=0), :]
+            for part in range(2)
+        ]
+        parts.append(times(coarse, fine))
     return (
         jnp.concatenate([part[0] for part in parts], 0),
         jnp.concatenate([part[1] for part in parts], 0),
@@ -139,19 +149,18 @@
     lax.fori_loop(0, count // 2, body, 0)
 
 
-def image_kernel(scale, lines, blocks, groups, away, place_ref, step_ref, start_ref, col_ref, *refs):
-    vis_refs, (out_ref, token_ref), slots = refs[:blocks], refs[blocks : blocks + 2], refs[blocks + 2 :]
-    token_ref[0] = place_ref[0]
+def image_kernel(scale, lines, blocks, groups, away, step_c, step_f, start_c, start_f, col_ref, *refs):
+    vis_refs, out_ref, slots = refs[:blocks], refs[blocks], refs[blocks + 1 :]
     chans = out_ref.shape[1]
-    base = lax.rem(place_ref[2] + groups - away, groups) * (chans // FINE)
+    base = wrapped(lax.axis_index("chan") + (groups - away), groups) * (chans // FINE)
 
     def fill(i, slot):
         x_ref = slots[slot]
         rows = pl.ds(pl.multiple_of(i * A_CHANS, A_CHANS), A_CHANS)
         group = base + i * (A_CHANS // FINE)
         for block in range(blocks):
-            step = phases(step_ref, group, A_CHANS, block)
-            start = phases(start_ref, group, A_CHANS, block)
+            step = phases(step_c, step_f, group, A_CHANS, block)
+            start = phases(start_c, start_f, group, A_CHANS, block)
             vis_ref = vis_refs[block]
             value = conj_times((vis_ref[0, rows, :].astype(F32), -vis_ref[1, rows, :].astype(F32)), start)
             at = block * 2 * LANES
@@ -170,32 +179,32 @@
     paired(chans // A_CHANS, fill, multiply)
 
 
-def make_image(vis, place, step_t, start_t, col, lines, total_rows, groups, away):
+def make_image(vis, phase_t, col, lines, total_rows, groups, away):
     blocks = len(vis)
     _, chans, _ = vis[0].shape
     rows = blocks * LANES
     vmem = pl.BlockSpec(memory_space=pltpu.VMEM)
-    flops = 2 * lines * chans * 2 * rows * M
+    flops = 4 * lines * chans * 2 * rows * M
     return pl.pallas_call(
         functools.partial(image_kernel, 1.0 / math.sqrt(total_rows), lines, blocks, groups, away),
-        out_shape=(jax.ShapeDtypeStruct((lines, chans, M), BF16), TOKEN),
-        in_specs=[pl.BlockSpec(memory_space=pltpu.SMEM)] + [vmem] * (3 + blocks),
-        out_specs=(vmem, pl.BlockSpec(memory_space=pltpu.SMEM)),
+        out_shape=jax.ShapeDtypeStruct((lines, chans, M), BF16),
+        in_specs=[vmem] * (5 + blocks),
+        out_specs=vmem,
         scratch_shapes=[pltpu.VMEM((lines * A_CHANS, 2 * rows), BF16)] * 2,
         compiler_params=pltpu.CompilerParams(vmem_limit_bytes=VMEM_SMALL),
         cost_estimate=pl.CostEstimate(flops=flops, bytes_accessed=8 << 20, transcendentals=0),
         name="image",
-    )(place, step_t, start_t, col, *vis)
-
-
-def filter_kernel(groups, step, place_ref, filter_ref, *refs):
+    )(*phase_t, col, *vis)
+
+
+def filter_kernel(groups, step, filter_ref, *refs):
     image_refs, out_refs, weight_ref = refs[:groups], refs[groups : 2 * groups], refs[-1]
     lines, chans, _ = out_refs[0].shape
-    place = place_ref[2]
+    place = lax.axis_index("chan")
     for out_block in range(groups):
-        rows = pl.ds(pl.multiple_of(lax.rem(place + out_block, groups) * chans, chans), chans)
+        rows = pl.ds(pl.multiple_of(wrapped(place + out_block, groups) * chans, chans), chans)
         for in_block in range(groups):
-            at = lax.rem(place + (groups - in_block), groups) * chans
+            at = wrapped(place + (groups - in_block), groups) * chans
             weight_ref[
                 out_block * chans : (out_block + 1) * chans,
                 in_block * chans : (in_block + 1) * chans,
@@ -221,7 +230,7 @@
     lax.fori_loop(0, lines // step, body, 0)
 
 
-def filter_images(images, place, fg_filter):
+def filter_images(images, fg_filter):
     groups = len(images)
     lines, chans, _ = images[0].shape
     step = min(4, lines)
@@ -229,7 +238,7 @@
     return pl.pallas_call(
         functools.partial(filter_kernel, groups, step),
         out_shape=[jax.ShapeDtypeStruct((lines, chans, M), BF16)] * groups,
-        in_specs=[pl.BlockSpec(memory_space=pltpu.SMEM)] + [vmem] * (1 + groups),
+        in_specs=[vmem] * (1 + groups),
         out_specs=[vmem] * groups,
         scratch_shapes=[pltpu.VMEM((F, F), BF16)],
         compiler_params=pltpu.CompilerParams(vmem_limit_bytes=VMEM_FILTER),
@@ -237,14 +246,14 @@
             flops=2 * F * F * lines * M, bytes_accessed=18 << 20, transcendentals=0
         ),
         name="filter",
-    )(place, fg_filter, *images)
-
-
-def predict_kernel(scale, groups, away, place_ref, image_ref, col_ref, step_ref, start_ref, keep_ref, send_ref, *slots):
+    )(fg_filter, *images)
+
+
+def predict_kernel(scale, groups, away, image_ref, col_ref, step_c, step_f, start_c, start_f, keep_ref, send_ref, *slots):
     lines, chans, _ = image_ref.shape
     blocks = 2 * keep_ref.shape[0]
     count = chans // C_CHANS
-    base = lax.rem(place_ref[2] + away, groups) * (chans // FINE)
+    base = wrapped(lax.axis_index("chan") + away, groups) * (chans // FINE)
 
     def rows_of(i):
         return pl.ds(pl.multiple_of(i * C_CHANS, C_CHANS), C_CHANS)
@@ -259,8 +268,8 @@
         rows = rows_of(i)
         for first in range(0, C_CHANS, C_UNIT):
             group = base + i * (C_CHANS // FINE) + first // FINE
-            step = phases(step_ref, group, C_UNIT, block)
-            start = phases(start_ref, group, C_UNIT, block)
+            step = phases(step_c, step_f, group, C_UNIT, block)
+            start = phases(start_c, start_f, group, C_UNIT, block)
             total = None
             for line in reversed(range(lines)):
                 take = slice(line * C_CHANS + first, line * C_CHANS + first + C_UNIT)
@@ -293,27 +302,26 @@
     lax.fori_loop(0, count, body, 0)
 
 
-def predict_part(foreground, place, step_t, start_t, col, groups, away):
+def predict_part(foreground, phase_t, col, groups, away):
     lines, chans, _ = foreground.shape
     rows = col.shape[1] // 2
     vmem = pl.BlockSpec(memory_space=pltpu.VMEM)
-    flops = 2 * lines * chans * 2 * rows * M
+    flops = 4 * lines * chans * 2 * rows * M
     half = (rows // LANES // 2, 2, chans, LANES)
     return pl.pallas_call(
         functools.partial(predict_kernel, 1.0 / math.sqrt(L * M), groups, away),
         out_shape=(jax.ShapeDtypeStruct(half, F32), jax.ShapeDtypeStruct(half, BF16)),
-        in_specs=[pl.BlockSpec(memory_space=pltpu.SMEM)] + [vmem] * 4,
+        in_specs=[vmem] * 6,
         out_specs=(vmem, vmem),
         scratch_shapes=[pltpu.VMEM((lines * C_CHANS, 2 * LANES), F32)] * C_SLOTS,
         compiler_params=pltpu.CompilerParams(vmem_limit_bytes=VMEM_SMALL),
         cost_estimate=pl.CostEstimate(flops=flops, bytes_accessed=8 << 20, transcendentals=0),
         name="predict",
-    )(place, foreground, col, step_t, start_t)
+    )(foreground, col, *phase_t)
 
 
 def local(visibility, flags, u_index, v_index, fg_filter):
     groups, tiles = lax.axis_size("chan"), lax.axis_size("tile")
-    chan, tile = lax.axis_index("chan"), lax.axis_index("tile")
     chans = visibility.shape[2]
     total_rows = u_index.shape[0]
     lines = L // (groups * tiles)
@@ -322,34 +330,33 @@
     weight = flags.astype(BF16)
     own = jnp.transpose(visibility * weight[:, None, :], (1, 2, 0))
     seen = [own] + [chan_shift(own, groups, away) for away in range(1, groups)]
-    place = jnp.stack([tile, (chan * tiles + tile) * lines, chan])
-    step_t, start_t, predict_col, image_col, token = tables(u_index, v_index, place, tiles)
-    images, tokens = [], [token]
+    *phase_t, predict_col, image_col = tables(u_index, v_index, lines, tiles)
+    images = []
     for away in range(groups):
         block = seen[away]
         if away:
-            block = after(block, tokens[min(away - 1, 1)])
+            block = after(block, images[min(away, 2) - 2] if away > 1 else phase_t[1])
         pieces = [tile_swap(block, tiles, mask) for mask in masks[1:]]
         blocks = [block, *pieces]
-        if away != 1:
-            pieces = lax.optimization_barrier((*pieces, tokens[min(away, 2)]))[:-1]
+        if away == 0:
+            pieces = lax.optimization_barrier((*pieces, phase_t[1]))[:-1]
+        if away > 1:
+            pieces = lax.optimization_barrier((*pieces, images[1]))[:-1]
         blocks += [tile_swap(piece, tiles, 1) for piece in (block, *pieces)]
-        image, token = make_image(
-            blocks, place, step_t, start_t, image_col, lines, total_rows, groups, away
+        images.append(
+            make_image(blocks, phase_t, image_col, lines, total_rows, groups, away)
         )
-        images.append(image)
-        tokens.append(token)
-    foreground = filter_images(images, place, fg_filter)
+    foreground = filter_images(images, fg_filter)
 
     parts, first_halves, second_halves = [], [], []
     for turn, away in enumerate(list(range(1, groups)) + [0]):
-        here = place
+        here = phase_t
         if turn >= 2:
-            here = after(here, first_halves[turn - 2])
+            here = [*here[:3], after(here[3], first_halves[turn - 2])]
         if turn >= 3:
-            here = after(here, *second_halves[turn - 3])
+            here = [*here[:3], after(here[3], *second_halves[turn - 3])]
         kept, sent = predict_part(
-            foreground[away], here, step_t, start_t, predict_col, groups, away
+            foreground[away], here, predict_col, groups, away
         )
         received = tile_swap(sent, tiles, 1)
         first_halves.append(received)

time: 146 us -> 137 us (0.938)
  Pallas kernels: 76.9 us -> 68.1 us
    pallas_call x4, Pallas kernels: 30 us -> 25.9 us  [make_image(): pl.pallas_call(functools.partial(image_kernel, 1.0 / math.sqrt(total_rows...]
    pallas_call x4, Pallas kernels: 34 us -> 30.6 us  [predict_part(): pl.pallas_call(functools.partial(predict_kernel, 1.0 / math.sqrt(L * M),...]
  transfers between devices with their start and end apart: 50 -> 50, of which waited for: 9 -> 9; matrix products, arithmetic and copies ran while one was open for 1% -> 1% of each run, Pallas kernels for 35% -> 33%
where the time goes in v4:
time: 137 us
  Pallas kernels  68.1 us (50%)
  starting transfers between devices  43.1 us (31%)
  waiting for transfers between devices  19.7 us (14%)
  local copies, waits for them, and re-layouts  3.57 us (3%)
  other arithmetic  1.9 us (1%)
    ppermute x44, starting transfers between devices, tile_swap(): return lax.ppermute(block, 'tile', [(t, t ^ mask) for t in range(tiles)])  32.6 us
    pallas_call x4, Pallas kernels, predict_part(): pl.pallas_call(functools.partial(predict_kernel, 1.0 / math.sqrt(L * M),...  30.6 us
    pallas_call x4, Pallas kernels, make_image(): pl.pallas_call(functools.partial(image_kernel, 1.0 / math.sqrt(total_rows...  25.9 us
    ppermute x44, waiting for transfers between devices, tile_swap(): return lax.ppermute(block, 'tile', [(t, t ^ mask) for t in range(tiles)])  19.2 us
    ppermute x6, starting transfers between devices, chan_shift(): lax.ppermute(block, 'chan', [(c, (c + away) % groups) for c in range(grou...  10.5 us
    pallas_call x1, Pallas kernels, filter_images(): pl.pallas_call(functools.partial(filter_kernel, groups, step), out_shape=...  9.61 us
  transfers between devices with their start and end apart: 50, of which 9 were waited for; matrix products, arithmetic and copies ran while one was open for 1% of the time, Pallas kernels for 33%

profile of v4, /device:TPU:0, one launch (start us, length us, event | category | flops | bytes accessed | tf_op | source)
XLA Modules:
  0.0 136.8 jit_solution(1598176817406075138)
XLA Ops:
  2.1 3.1 %collective-permute-start.7 = (bf16[2,256,128]{2,1,0:T(8,128)(2,1)S(1)}, bf16[2,256,128]{2,1,0:T(8,128)(2,1)S(1)}, u32[]{:S(2)}, u32[]{:S(2)}) collective-permute-start(bf16[2,256,128]{2,1,0:T(8,128)(2,1)S(1)} %multiply_bitcast_fusion.refs_0_), channel_id=1, source_target_pairs={{0,8},{8,16},{16,24},{24,0},{1,9},{9,17},{17,25},{25,1},{2,10},{10... | collective-permute-start | bytes 393224 | tf_op jit(solution)/shard_map/ppermute | solution.py:39
  6.7 1.5 %collective-permute-start.1 = (bf16[2,256,128]{2,1,0:T(8,128)(2,1)S(1)}, bf16[2,256,128]{2,1,0:T(8,128)(2,1)S(1)}, u32[]{:S(2)}, u32[]{:S(2)}) collective-permute-start(bf16[2,256,128]{2,1,0:T(8,128)(2,1)S(1)} %multiply_bitcast_fusion.refs_0_), channel_id=1, source_target_pairs={{0,4},{1,5},{2,6},{3,7},{4,0},{5,1},{6,2},{7,3},{8,12},{9,13},{10,... | collective-permute-start | bytes 393224 | tf_op jit(solution)/shard_map/ppermute | solution.py:35
  10.0 2.1 %tables.1 = (f32[128,16,128]{2,1,0:T(8,128)S(1)}, f32[2,8,8,128]{3,2,1,0:T(8,128)S(1)}, f32[128,16,128]{2,1,0:T(8,128)S(1)}, f32[2,8,8,128]{3,2,1,0:T(8,128)S(1)...) custom-call(s32[8,128]{1,0:T(8,128)S(1)} %bitcast.64, s32[8,128]{1,0:T(8,128)S(1)} %bitcast.65), custom_call_target="tpu_custom_call" | custom-call | flops 3221225472 | bytes 4194304 | tf_op jit(solution)/shard_map/tables/pallas_call | solution.py:105
  12.1 2.2 %collective-permute-start.23 = (bf16[2,256,128]{2,1,0:T(8,128)(2,1)S(1)}, bf16[2,256,128]{2,1,0:T(8,128)(2,1)S(1)}, u32[]{:S(2)}, u32[]{:S(2)}) collective-permute-start(bf16[2,256,128]{2,1,0:T(8,128)(2,1)S(1)} %multiply_bitcast_fusion.refs_0_), channel_id=1, source_target_pairs={{0,24},{8,0},{16,8},{24,16},{1,25},{9,1},{17,9},{25,17},{2,26},{10... | collective-permute-start | bytes 393224 | tf_op jit(solution)/shard_map/ppermute | solution.py:39
  14.3 1.6 %collective-permute-start.8 = (bf16[2,256,128]{2,1,0:T(8,128)(2,1)S(1)}, bf16[2,256,128]{2,1,0:T(8,128)(2,1)S(1)}, u32[]{:S(2)}, u32[]{:S(2)}) collective-permute-start(bf16[2,256,128]{2,1,0:T(8,128)(2,1)S(1)} %collective-permute-done.7.refs_0_), channel_id=1, source_target_pairs={{0,2},{1,3},{2,0},{3,1},{4,6},{5,7},{6,4},{7,5},{8,10},{9,11},{10,... | collective-permute-start | bytes 393224 | tf_op jit(solution)/shard_map/ppermute | solution.py:35
  15.9 1.5 %collective-permute-start.9 = (bf16[2,256,128]{2,1,0:T(8,128)(2,1)S(1)}, bf16[2,256,128]{2,1,0:T(8,128)(2,1)S(1)}, u32[]{:S(2)}, u32[]{:S(2)}) collective-permute-start(bf16[2,256,128]{2,1,0:T(8,128)(2,1)S(1)} %collective-permute-done.7.refs_0_), channel_id=1, source_target_pairs={{0,4},{1,5},{2,6},{3,7},{4,0},{5,1},{6,2},{7,3},{8,12},{9,13},{10,... | collective-permute-start | bytes 393224 | tf_op jit(solution)/shard_map/ppermute | solution.py:35
  18.3 1.8 %collective-permute-done.8.refs_1_ = bf16[2,256,128]{2,1,0:T(8,128)(2,1)S(1)} collective-permute-done((bf16[2,256,128]{2,1,0:T(8,128)(2,1)S(1)}, bf16[2,256,128]{2,1,0:T(8,128)(2,1)S(1)}, u32[]{:S(2)}, u32[]{:S(2)}) %collective-permute-start.8) | collective-permute-done | bytes 131104 | tf_op jit(solution)/shard_map/ppermute | solution.py:35
  20.1 4.0 %collective-permute-done.9.refs_2_ = bf16[2,256,128]{2,1,0:T(8,128)(2,1)S(1)} collective-permute-done((bf16[2,256,128]{2,1,0:T(8,128)(2,1)S(1)}, bf16[2,256,128]{2,1,0:T(8,128)(2,1)S(1)}, u32[]{:S(2)}, u32[]{:S(2)}) %collective-permute-start.9) | collective-permute-done | bytes 131104 | tf_op jit(solution)/shard_map/ppermute | solution.py:35
  25.9 6.6 %image.4.refs_0_ = bf16[16,256,256]{2,1,0:T(8,128)(2,1)S(1)} custom-call(f32[128,16,128]{2,1,0:T(8,128)S(1)} %get-tuple-element.38.step_c, f32[2,8,8,128]{3,2,1,0:T(8,128)S(1)} %get-tuple-element.39.step_f, f32[128,16,128]{2,1,0:T(8,128)S(1)} %get-tuple-element.40.start_c, f32[2,8,8,128]{3,2,1,0:T(8,128)S(1)} %get-tuple-element.63.start_f, ...), custom_call_target="tpu_custom_call" | custom-call | flops 8589934592 | bytes 8388608 | tf_op jit(solution)/shard_map/image/pallas_call | solution.py:188
  33.0 1.6 %collective-permute-start.25 = (bf16[2,256,128]{2,1,0:T(8,128)(2,1)S(1)}, bf16[2,256,128]{2,1,0:T(8,128)(2,1)S(1)}, u32[]{:S(2)}, u32[]{:S(2)}) collective-permute-start(bf16[2,256,128]{2,1,0:T(8,128)(2,1)S(1)} %collective-permute-done.23.refs_0_), channel_id=1, source_target_pairs={{0,4},{1,5},{2,6},{3,7},{4,0},{5,1},{6,2},{7,3},{8,12},{9,13},{10,... | collective-permute-start | bytes 393224 | tf_op jit(solution)/shard_map/ppermute | solution.py:35
  36.5 1.6 %collective-permute-start.17 = (bf16[2,256,128]{2,1,0:T(8,128)(2,1)S(1)}, bf16[2,256,128]{2,1,0:T(8,128)(2,1)S(1)}, u32[]{:S(2)}, u32[]{:S(2)}) collective-permute-start(bf16[2,256,128]{2,1,0:T(8,128)(2,1)S(1)} %collective-permute-done.15.refs_0_), channel_id=1, source_target_pairs={{0,4},{1,5},{2,6},{3,7},{4,0},{5,1},{6,2},{7,3},{8,12},{9,13},{10,... | collective-permute-start | bytes 393224 | tf_op jit(solution)/shard_map/ppermute | solution.py:35
  38.2 6.4 %image.5.refs_1_ = bf16[16,256,256]{2,1,0:T(8,128)(2,1)S(1)} custom-call(f32[128,16,128]{2,1,0:T(8,128)S(1)} %get-tuple-element.38.step_c, f32[2,8,8,128]{3,2,1,0:T(8,128)S(1)} %get-tuple-element.39.step_f, f32[128,16,128]{2,1,0:T(8,128)S(1)} %get-tuple-element.40.start_c, f32[2,8,8,128]{3,2,1,0:T(8,128)S(1)} %get-tuple-element.63.start_f, ...), custom_call_target="tpu_custom_call" | custom-call | flops 8589934592 | bytes 8388608 | tf_op jit(solution)/shard_map/image/pallas_call | solution.py:188
  44.6 1.5 %collective-permute-start.18 = (bf16[2,256,128]{2,1,0:T(8,128)(2,1)S(1)}, bf16[2,256,128]{2,1,0:T(8,128)(2,1)S(1)}, u32[]{:S(2)}, u32[]{:S(2)}) collective-permute-start(bf16[2,256,128]{2,1,0:T(8,128)(2,1)S(1)} %collective-permute-done.15.refs_0_), channel_id=1, source_target_pairs={{0,6},{1,7},{2,4},{3,5},{4,2},{5,3},{6,0},{7,1},{8,14},{9,15},{10,... | collective-permute-start | bytes 393224 | tf_op jit(solution)/shard_map/ppermute | solution.py:35
  47.1 3.4 %collective-permute-done.18.refs_3_ = bf16[2,256,128]{2,1,0:T(8,128)(2,1)S(1)} collective-permute-done((bf16[2,256,128]{2,1,0:T(8,128)(2,1)S(1)}, bf16[2,256,128]{2,1,0:T(8,128)(2,1)S(1)}, u32[]{:S(2)}, u32[]{:S(2)}) %collective-permute-start.18) | collective-permute-done | bytes 131104 | tf_op jit(solution)/shard_map/ppermute | solution.py:35
  51.6 6.4 %image.7.refs_3_ = bf16[16,256,256]{2,1,0:T(8,128)(2,1)S(1)} custom-call(f32[128,16,128]{2,1,0:T(8,128)S(1)} %get-tuple-element.38.step_c, f32[2,8,8,128]{3,2,1,0:T(8,128)S(1)} %get-tuple-element.39.step_f, f32[128,16,128]{2,1,0:T(8,128)S(1)} %get-tuple-element.40.start_c, f32[2,8,8,128]{3,2,1,0:T(8,128)S(1)} %get-tuple-element.63.start_f, ...), custom_call_target="tpu_custom_call" | custom-call | flops 8589934592 | bytes 8388608 | tf_op jit(solution)/shard_map/image/pallas_call | solution.py:188
  58.1 6.4 %image.6.refs_2_ = bf16[16,256,256]{2,1,0:T(8,128)(2,1)S(1)} custom-call(f32[128,16,128]{2,1,0:T(8,128)S(1)} %get-tuple-element.38.step_c, f32[2,8,8,128]{3,2,1,0:T(8,128)S(1)} %get-tuple-element.39.step_f, f32[128,16,128]{2,1,0:T(8,128)S(1)} %get-tuple-element.40.start_c, f32[2,8,8,128]{3,2,1,0:T(8,128)S(1)} %get-tuple-element.63.start_f, ...), custom_call_target="tpu_custom_call" | custom-call | flops 8589934592 | bytes 8388608 | tf_op jit(solution)/shard_map/image/pallas_call | solution.py:188
  64.5 9.6 %filter.1 = (bf16[16,256,256]{2,1,0:T(8,128)(2,1)S(1)}, bf16[16,256,256]{2,1,0:T(8,128)(2,1)S(1)}, bf16[16,256,256]{2,1,0:T(8,128)(2,1)S(1)}, bf16[16,256,256]{2,1,0:T(8,128)(2,1)S(1)}) custom-call(bf16[1024,1024]{1,0:T(8,128)(2,1)S(1)} %copy-done, bf16[16,256,256]{2,1,0:T(8,128)(2,1)S(1)} %image.4.refs_0_, bf16[16,256,256]{2,1,0:T(8,128)(2,1)S(1)} %image.5.refs_1_, ...), custom_call_target="tpu_custom_call" | custom-call | flops 8589934592 | bytes 18874368 | tf_op jit(solution)/shard_map/filter/pallas_call | solution.py:238
  74.1 7.6 %predict.4 = (f32[4,2,256,128]{3,2,1,0:T(8,128)S(1)}, bf16[4,2,256,128]{3,2,1,0:T(8,128)(2,1)S(1)}) custom-call(bf16[16,256,256]{2,1,0:T(8,128)(2,1)S(1)} %get-tuple-element.55.image_ref, bf16[256,2048]{1,0:T(8,128)(2,1)S(1)} %get-tuple-element.56.col_ref, f32[128,16,128]{2,1,0:T(8,128)S(1)} %get-tuple-element.38.step_c, ...), custom_call_target="tpu_custom_call" | custom-call | flops 8589934592 | bytes 8388608 | tf_op jit(solution)/shard_map/predict/pallas_call | solution.py:311
  81.9 7.6 %predict.5 = (f32[4,2,256,128]{3,2,1,0:T(8,128)S(1)}, bf16[4,2,256,128]{3,2,1,0:T(8,128)(2,1)S(1)}) custom-call(bf16[16,256,256]{2,1,0:T(8,128)(2,1)S(1)} %get-tuple-element.59.image_ref, bf16[256,2048]{1,0:T(8,128)(2,1)S(1)} %get-tuple-element.56.col_ref, f32[128,16,128]{2,1,0:T(8,128)S(1)} %get-tuple-element.38.step_c, ...), custom_call_target="tpu_custom_call" | custom-call | flops 8589934592 | bytes 8388608 | tf_op jit(solution)/shard_map/predict/pallas_call | solution.py:311
  90.2 1.6 %collective-permute-start.32 = (bf16[2,256,128]{2,1,0:T(8,128)(2,1)S(1)}, bf16[2,256,128]{2,1,0:T(8,128)(2,1)S(1)}, u32[]{:S(2)}, u32[]{:S(2)}) collective-permute-start(bf16[2,256,128]{2,1,0:T(8,128)(2,1)S(1)} %get-tuple-element.90), channel_id=1, source_target_pairs={{0,2},{1,3},{2,0},{3,1},{4,6},{5,7},{6,4},{7,5},{8,10},{9,11},{10,... | collective-permute-start | bytes 393224 | tf_op jit(solution)/shard_map/ppermute | solution.py:35
  93.9 1.6 %collective-permute-start.37 = (bf16[2,256,128]{2,1,0:T(8,128)(2,1)S(1)}, bf16[2,256,128]{2,1,0:T(8,128)(2,1)S(1)}, u32[]{:S(2)}, u32[]{:S(2)}) collective-permute-start(bf16[2,256,128]{2,1,0:T(8,128)(2,1)S(1)} %get-tuple-element.79), channel_id=1, source_target_pairs={{0,2},{1,3},{2,0},{3,1},{4,6},{5,7},{6,4},{7,5},{8,10},{9,11},{10,... | collective-permute-start | bytes 393224 | tf_op jit(solution)/shard_map/ppermute | solution.py:35
  96.0 7.8 %predict.6 = (f32[4,2,256,128]{3,2,1,0:T(8,128)S(1)}, bf16[4,2,256,128]{3,2,1,0:T(8,128)(2,1)S(1)}) custom-call(bf16[16,256,256]{2,1,0:T(8,128)(2,1)S(1)} %get-tuple-element.62.image_ref, bf16[256,2048]{1,0:T(8,128)(2,1)S(1)} %get-tuple-element.56.col_ref, f32[128,16,128]{2,1,0:T(8,128)S(1)} %get-tuple-element.38.step_c, ...), custom_call_target="tpu_custom_call" | custom-call | flops 8589934592 | bytes 8388608 | tf_op jit(solution)/shard_map/predict/pallas_call | solution.py:311
  103.8 1.5 %collective-permute-start.39 = (bf16[2,256,128]{2,1,0:T(8,128)(2,1)S(1)}, bf16[2,256,128]{2,1,0:T(8,128)(2,1)S(1)}, u32[]{:S(2)}, u32[]{:S(2)}) collective-permute-start(bf16[2,256,128]{2,1,0:T(8,128)(2,1)S(1)} %get-tuple-element.80), channel_id=1, source_target_pairs={{0,6},{1,7},{2,4},{3,5},{4,2},{5,3},{6,0},{7,1},{8,14},{9,15},{10,... | collective-permute-start | bytes 393224 | tf_op jit(solution)/shard_map/ppermute | solution.py:35
  105.4 1.6 %collective-permute-start.35 = (bf16[2,256,128]{2,1,0:T(8,128)(2,1)S(1)}, bf16[2,256,128]{2,1,0:T(8,128)(2,1)S(1)}, u32[]{:S(2)}, u32[]{:S(2)}) collective-permute-start(bf16[2,256,128]{2,1,0:T(8,128)(2,1)S(1)} %fusion.10), channel_id=1, source_target_pairs={{0,8},{8,16},{16,24},{24,0},{1,9},{9,17},{17,25},{25,1},{2,10},{10... | collective-permute-start | bytes 393224 | tf_op jit(solution)/shard_map/ppermute | solution.py:39
  107.1 7.6 %predict.7 = (f32[4,2,256,128]{3,2,1,0:T(8,128)S(1)}, bf16[4,2,256,128]{3,2,1,0:T(8,128)(2,1)S(1)}) custom-call(bf16[16,256,256]{2,1,0:T(8,128)(2,1)S(1)} %get-tuple-element.66.image_ref, bf16[256,2048]{1,0:T(8,128)(2,1)S(1)} %get-tuple-element.56.col_ref, f32[128,16,128]{2,1,0:T(8,128)S(1)} %get-tuple-element.38.step_c, ...), custom_call_target="tpu_custom_call" | custom-call | flops 8589934592 | bytes 8388608 | tf_op jit(solution)/shard_map/predict/pallas_call | solution.py:311
  115.2 1.6 %collective-permute-start.42 = (bf16[2,256,128]{2,1,0:T(8,128)(2,1)S(1)}, bf16[2,256,128]{2,1,0:T(8,128)(2,1)S(1)}, u32[]{:S(2)}, u32[]{:S(2)}) collective-permute-start(bf16[2,256,128]{2,1,0:T(8,128)(2,1)S(1)} %get-tuple-element.82), channel_id=1, source_target_pairs={{0,2},{1,3},{2,0},{3,1},{4,6},{5,7},{6,4},{7,5},{8,10},{9,11},{10,... | collective-permute-start | bytes 393224 | tf_op jit(solution)/shard_map/ppermute | solution.py:35
  118.8 2.5 %collective-permute-done.42 = bf16[2,256,128]{2,1,0:T(8,128)(2,1)S(1)} collective-permute-done((bf16[2,256,128]{2,1,0:T(8,128)(2,1)S(1)}, bf16[2,256,128]{2,1,0:T(8,128)(2,1)S(1)}, u32[]{:S(2)}, u32[]{:S(2)}) %collective-permute-start.42) | collective-permute-done | bytes 131104 | tf_op jit(solution)/shard_map/ppermute | solution.py:35
  121.8 3.1 %collective-permute-done.43 = bf16[2,256,128]{2,1,0:T(8,128)(2,1)S(1)} collective-permute-done((bf16[2,256,128]{2,1,0:T(8,128)(2,1)S(1)}, bf16[2,256,128]{2,1,0:T(8,128)(2,1)S(1)}, u32[]{:S(2)}, u32[]{:S(2)}) %collective-permute-start.43) | collective-permute-done | bytes 131104 | tf_op jit(solution)/shard_map/ppermute | solution.py:35
  125.0 2.3 %collective-permute-start.45 = (bf16[2,256,128]{2,1,0:T(8,128)(2,1)S(1)}, bf16[2,256,128]{2,1,0:T(8,128)(2,1)S(1)}, u32[]{:S(2)}, u32[]{:S(2)}) collective-permute-start(bf16[2,256,128]{2,1,0:T(8,128)(2,1)S(1)} %fusion.6), channel_id=1, source_target_pairs={{0,24},{8,0},{16,8},{24,16},{1,25},{9,1},{17,9},{25,17},{2,26},{10... | collective-permute-start | bytes 393224 | tf_op jit(solution)/shard_map/ppermute | solution.py:39
  129.3 1.8 %collective-permute-start.49 = (bf16[2,256,128]{2,1,0:T(8,128)(2,1)S(1)}, bf16[2,256,128]{2,1,0:T(8,128)(2,1)S(1)}, u32[]{:S(2)}, u32[]{:S(2)}) collective-permute-start(bf16[2,256,128]{2,1,0:T(8,128)(2,1)S(1)} %get-tuple-element.86), channel_id=1, source_target_pairs={{0,6},{1,7},{2,4},{3,5},{4,2},{5,3},{6,0},{7,1},{8,14},{9,15},{10,... | collective-permute-start | bytes 393224 | tf_op jit(solution)/shard_map/ppermute | solution.py:35
  131.5 1.9 %collective-permute-done.47 = bf16[2,256,128]{2,1,0:T(8,128)(2,1)S(1)} collective-permute-done((bf16[2,256,128]{2,1,0:T(8,128)(2,1)S(1)}, bf16[2,256,128]{2,1,0:T(8,128)(2,1)S(1)}, u32[]{:S(2)}, u32[]{:S(2)}) %collective-permute-start.47) | collective-permute-done | bytes 131104 | tf_op jit(solution)/shard_map/ppermute | solution.py:35
  133.4 2.4 %collective-permute-done.48 = bf16[2,256,128]{2,1,0:T(8,128)(2,1)S(1)} collective-permute-done((bf16[2,256,128]{2,1,0:T(8,128)(2,1)S(1)}, bf16[2,256,128]{2,1,0:T(8,128)(2,1)S(1)}, u32[]{:S(2)}, u32[]{:S(2)}) %collective-permute-start.48) | collective-permute-done | bytes 131104 | tf_op jit(solution)/shard_map/ppermute | solution.py:35
  (102 shorter events, 22.7 us)
Async XLA Ops:
  2.1 10.0 %collective-permute-start.7 = (bf16[2,256,128]{2,1,0:T(8,128)(2,1)S(1)}, bf16[2,256,128]{2,1,0:T(8,128)(2,1)S(1)}, u32[]{:S(2)}, u32[]{:S(2)}) collective-permute-start(bf16[2,256,128]{2,1,0:T(8,128)(2,1)S(1)} %multiply_bitcast_fusion.refs_0_), channel_id=1, source_target_pairs={{0,8},{8,16},{16,24},{24,0},{1,9},{9,17},{17,25},{25,1},{2,10},{10... | collective-permute-start | bytes 393224 | tf_op jit(solution)/shard_map/ppermute | solution.py:39
  5.2 9.1 %collective-permute-start = (bf16[2,256,128]{2,1,0:T(8,128)(2,1)S(1)}, bf16[2,256,128]{2,1,0:T(8,128)(2,1)S(1)}, u32[]{:S(2)}, u32[]{:S(2)}) collective-permute-start(bf16[2,256,128]{2,1,0:T(8,128)(2,1)S(1)} %multiply_bitcast_fusion.refs_0_), channel_id=1, source_target_pairs={{0,2},{1,3},{2,0},{3,1},{4,6},{5,7},{6,4},{7,5},{8,10},{9,11},{10,... | collective-permute-start | bytes 393224 | tf_op jit(solution)/shard_map/ppermute | solution.py:35
  6.7 9.2 %collective-permute-start.1 = (bf16[2,256,128]{2,1,0:T(8,128)(2,1)S(1)}, bf16[2,256,128]{2,1,0:T(8,128)(2,1)S(1)}, u32[]{:S(2)}, u32[]{:S(2)}) collective-permute-start(bf16[2,256,128]{2,1,0:T(8,128)(2,1)S(1)} %multiply_bitcast_fusion.refs_0_), channel_id=1, source_target_pairs={{0,4},{1,5},{2,6},{3,7},{4,0},{5,1},{6,2},{7,3},{8,12},{9,13},{10,... | collective-permute-start | bytes 393224 | tf_op jit(solution)/shard_map/ppermute | solution.py:35
  8.2 9.3 %collective-permute-start.2 = (bf16[2,256,128]{2,1,0:T(8,128)(2,1)S(1)}, bf16[2,256,128]{2,1,0:T(8,128)(2,1)S(1)}, u32[]{:S(2)}, u32[]{:S(2)}) collective-permute-start(bf16[2,256,128]{2,1,0:T(8,128)(2,1)S(1)} %multiply_bitcast_fusion.refs_0_), channel_id=1, source_target_pairs={{0,6},{1,7},{2,4},{3,5},{4,2},{5,3},{6,0},{7,1},{8,14},{9,15},{10,... | collective-permute-start | bytes 393224 | tf_op jit(solution)/shard_map/ppermute | solution.py:35
  8.7 9.1 %collective-permute-start.3 = (bf16[2,256,128]{2,1,0:T(8,128)(2,1)S(1)}, bf16[2,256,128]{2,1,0:T(8,128)(2,1)S(1)}, u32[]{:S(2)}, u32[]{:S(2)}) collective-permute-start(bf16[2,256,128]{2,1,0:T(8,128)(2,1)S(1)} %multiply_bitcast_fusion.refs_0_), channel_id=1, source_target_pairs={{0,1},{1,0},{2,3},{3,2},{4,5},{5,4},{6,7},{7,6},{8,9},{9,8},{10,11... | collective-permute-start | bytes 393224 | tf_op jit(solution)/shard_map/ppermute | solution.py:35
  15.9 8.2 %collective-permute-start.9 = (bf16[2,256,128]{2,1,0:T(8,128)(2,1)S(1)}, bf16[2,256,128]{2,1,0:T(8,128)(2,1)S(1)}, u32[]{:S(2)}, u32[]{:S(2)}) collective-permute-start(bf16[2,256,128]{2,1,0:T(8,128)(2,1)S(1)} %collective-permute-done.7.refs_0_), channel_id=1, source_target_pairs={{0,4},{1,5},{2,6},{3,7},{4,0},{5,1},{6,2},{7,3},{8,12},{9,13},{10,... | collective-permute-start | bytes 393224 | tf_op jit(solution)/shard_map/ppermute | solution.py:35
  24.1 8.4 %collective-permute-start.15 = (bf16[2,256,128]{2,1,0:T(8,128)(2,1)S(1)}, bf16[2,256,128]{2,1,0:T(8,128)(2,1)S(1)}, u32[]{:S(2)}, u32[]{:S(2)}) collective-permute-start(bf16[2,256,128]{2,1,0:T(8,128)(2,1)S(1)} %multiply_bitcast_fusion.refs_0_), channel_id=1, source_target_pairs={{0,16},{8,24},{16,0},{24,8},{1,17},{9,25},{17,1},{25,9},{2,18},{10... | collective-permute-start | bytes 393224 | tf_op jit(solution)/shard_map/ppermute | solution.py:39
  24.9 8.2 %collective-permute-start.11 = (bf16[2,256,128]{2,1,0:T(8,128)(2,1)S(1)}, bf16[2,256,128]{2,1,0:T(8,128)(2,1)S(1)}, u32[]{:S(2)}, u32[]{:S(2)}) collective-permute-start(bf16[2,256,128]{2,1,0:T(8,128)(2,1)S(1)} %collective-permute-done.7.refs_0_), channel_id=1, source_target_pairs={{0,1},{1,0},{2,3},{3,2},{4,5},{5,4},{6,7},{7,6},{8,9},{9,8},{10,11... | collective-permute-start | bytes 393224 | tf_op jit(solution)/shard_map/ppermute | solution.py:35
  24.9 9.8 %collective-permute-start.12 = (bf16[2,256,128]{2,1,0:T(8,128)(2,1)S(1)}, bf16[2,256,128]{2,1,0:T(8,128)(2,1)S(1)}, u32[]{:S(2)}, u32[]{:S(2)}) collective-permute-start(bf16[2,256,128]{2,1,0:T(8,128)(2,1)S(1)} %collective-permute-done.8.refs_1_), channel_id=1, source_target_pairs={{0,1},{1,0},{2,3},{3,2},{4,5},{5,4},{6,7},{7,6},{8,9},{9,8},{10,11... | collective-permute-start | bytes 393224 | tf_op jit(solution)/shard_map/ppermute | solution.py:35
  25.4 10.7 %collective-permute-start.13 = (bf16[2,256,128]{2,1,0:T(8,128)(2,1)S(1)}, bf16[2,256,128]{2,1,0:T(8,128)(2,1)S(1)}, u32[]{:S(2)}, u32[]{:S(2)}) collective-permute-start(bf16[2,256,128]{2,1,0:T(8,128)(2,1)S(1)} %collective-permute-done.9.refs_2_), channel_id=1, source_target_pairs={{0,1},{1,0},{2,3},{3,2},{4,5},{5,4},{6,7},{7,6},{8,9},{9,8},{10,11... | collective-permute-start | bytes 393224 | tf_op jit(solution)/shard_map/ppermute | solution.py:35
  25.5 11.1 %collective-permute-start.14 = (bf16[2,256,128]{2,1,0:T(8,128)(2,1)S(1)}, bf16[2,256,128]{2,1,0:T(8,128)(2,1)S(1)}, u32[]{:S(2)}, u32[]{:S(2)}) collective-permute-start(bf16[2,256,128]{2,1,0:T(8,128)(2,1)S(1)} %collective-permute-done.10.refs_3_), channel_id=1, source_target_pairs={{0,1},{1,0},{2,3},{3,2},{4,5},{5,4},{6,7},{7,6},{8,9},{9,8},{10,11... | collective-permute-start | bytes 393224 | tf_op jit(solution)/shard_map/ppermute | solution.py:35
  32.5 12.1 %collective-permute-start.24 = (bf16[2,256,128]{2,1,0:T(8,128)(2,1)S(1)}, bf16[2,256,128]{2,1,0:T(8,128)(2,1)S(1)}, u32[]{:S(2)}, u32[]{:S(2)}) collective-permute-start(bf16[2,256,128]{2,1,0:T(8,128)(2,1)S(1)} %collective-permute-done.23.refs_0_), channel_id=1, source_target_pairs={{0,2},{1,3},{2,0},{3,1},{4,6},{5,7},{6,4},{7,5},{8,10},{9,11},{10,... | collective-permute-start | bytes 393224 | tf_op jit(solution)/shard_map/ppermute | solution.py:35
  33.0 13.1 %collective-permute-start.25 = (bf16[2,256,128]{2,1,0:T(8,128)(2,1)S(1)}, bf16[2,256,128]{2,1,0:T(8,128)(2,1)S(1)}, u32[]{:S(2)}, u32[]{:S(2)}) collective-permute-start(bf16[2,256,128]{2,1,0:T(8,128)(2,1)S(1)} %collective-permute-done.23.refs_0_), channel_id=1, source_target_pairs={{0,4},{1,5},{2,6},{3,7},{4,0},{5,1},{6,2},{7,3},{8,12},{9,13},{10,... | collective-permute-start | bytes 393224 | tf_op jit(solution)/shard_map/ppermute | solution.py:35
  34.7 11.5 %collective-permute-start.26 = (bf16[2,256,128]{2,1,0:T(8,128)(2,1)S(1)}, bf16[2,256,128]{2,1,0:T(8,128)(2,1)S(1)}, u32[]{:S(2)}, u32[]{:S(2)}) collective-permute-start(bf16[2,256,128]{2,1,0:T(8,128)(2,1)S(1)} %collective-permute-done.23.refs_0_), channel_id=1, source_target_pairs={{0,6},{1,7},{2,4},{3,5},{4,2},{5,3},{6,0},{7,1},{8,14},{9,15},{10,... | collective-permute-start | bytes 393224 | tf_op jit(solution)/shard_map/ppermute | solution.py:35
  36.1 10.5 %collective-permute-start.16 = (bf16[2,256,128]{2,1,0:T(8,128)(2,1)S(1)}, bf16[2,256,128]{2,1,0:T(8,128)(2,1)S(1)}, u32[]{:S(2)}, u32[]{:S(2)}) collective-permute-start(bf16[2,256,128]{2,1,0:T(8,128)(2,1)S(1)} %collective-permute-done.15.refs_0_), channel_id=1, source_target_pairs={{0,2},{1,3},{2,0},{3,1},{4,6},{5,7},{6,4},{7,5},{8,10},{9,11},{10,... | collective-permute-start | bytes 393224 | tf_op jit(solution)/shard_map/ppermute | solution.py:35
  36.5 10.2 %collective-permute-start.17 = (bf16[2,256,128]{2,1,0:T(8,128)(2,1)S(1)}, bf16[2,256,128]{2,1,0:T(8,128)(2,1)S(1)}, u32[]{:S(2)}, u32[]{:S(2)}) collective-permute-start(bf16[2,256,128]{2,1,0:T(8,128)(2,1)S(1)} %collective-permute-done.15.refs_0_), channel_id=1, source_target_pairs={{0,4},{1,5},{2,6},{3,7},{4,0},{5,1},{6,2},{7,3},{8,12},{9,13},{10,... | collective-permute-start | bytes 393224 | tf_op jit(solution)/shard_map/ppermute | solution.py:35
  50.5 7.5 %collective-permute-start.19 = (bf16[2,256,128]{2,1,0:T(8,128)(2,1)S(1)}, bf16[2,256,128]{2,1,0:T(8,128)(2,1)S(1)}, u32[]{:S(2)}, u32[]{:S(2)}) collective-permute-start(bf16[2,256,128]{2,1,0:T(8,128)(2,1)S(1)} %collective-permute-done.15.refs_0_), channel_id=1, source_target_pairs={{0,1},{1,0},{2,3},{3,2},{4,5},{5,4},{6,7},{7,6},{8,9},{9,8},{10,11... | collective-permute-start | bytes 393224 | tf_op jit(solution)/shard_map/ppermute | solution.py:35
  50.5 7.5 %collective-permute-start.20 = (bf16[2,256,128]{2,1,0:T(8,128)(2,1)S(1)}, bf16[2,256,128]{2,1,0:T(8,128)(2,1)S(1)}, u32[]{:S(2)}, u32[]{:S(2)}) collective-permute-start(bf16[2,256,128]{2,1,0:T(8,128)(2,1)S(1)} %collective-permute-done.16.refs_1_), channel_id=1, source_target_pairs={{0,1},{1,0},{2,3},{3,2},{4,5},{5,4},{6,7},{7,6},{8,9},{9,8},{10,11... | collective-permute-start | bytes 393224 | tf_op jit(solution)/shard_map/ppermute | solution.py:35
  81.7 8.2 %collective-permute-start.31 = (bf16[4,2,256,128]{3,2,1,0:T(8,128)(2,1)S(1)}, bf16[4,2,256,128]{3,2,1,0:T(8,128)(2,1)S(1)}, u32[]{:S(2)}, u32[]{:S(2)}) collective-permute-start(bf16[4,2,256,128]{3,2,1,0:T(8,128)(2,1)S(1)} %get-tuple-element.58), channel_id=1, source_target_pairs={{0,1},{1,0},{2,3},{3,2},{4,5},{5,4},{6,7},{7,6},{8,9},{9,8},{10,11... | collective-permute-start | bytes 1572872 | tf_op jit(solution)/shard_map/ppermute | solution.py:35
  90.2 13.6 %collective-permute-start.32 = (bf16[2,256,128]{2,1,0:T(8,128)(2,1)S(1)}, bf16[2,256,128]{2,1,0:T(8,128)(2,1)S(1)}, u32[]{:S(2)}, u32[]{:S(2)}) collective-permute-start(bf16[2,256,128]{2,1,0:T(8,128)(2,1)S(1)} %get-tuple-element.90), channel_id=1, source_target_pairs={{0,2},{1,3},{2,0},{3,1},{4,6},{5,7},{6,4},{7,5},{8,10},{9,11},{10,... | collective-permute-start | bytes 393224 | tf_op jit(solution)/shard_map/ppermute | solution.py:35
  91.7 13.6 %collective-permute-start.33 = (bf16[2,256,128]{2,1,0:T(8,128)(2,1)S(1)}, bf16[2,256,128]{2,1,0:T(8,128)(2,1)S(1)}, u32[]{:S(2)}, u32[]{:S(2)}) collective-permute-start(bf16[2,256,128]{2,1,0:T(8,128)(2,1)S(1)} %get-tuple-element.89), channel_id=1, source_target_pairs={{0,4},{1,5},{2,6},{3,7},{4,0},{5,1},{6,2},{7,3},{8,12},{9,13},{10,... | collective-permute-start | bytes 393224 | tf_op jit(solution)/shard_map/ppermute | solution.py:35
  92.2 13.1 %collective-permute-start.34 = (bf16[2,256,128]{2,1,0:T(8,128)(2,1)S(1)}, bf16[2,256,128]{2,1,0:T(8,128)(2,1)S(1)}, u32[]{:S(2)}, u32[]{:S(2)}) collective-permute-start(bf16[2,256,128]{2,1,0:T(8,128)(2,1)S(1)} %get-tuple-element.88), channel_id=1, source_target_pairs={{0,6},{1,7},{2,4},{3,5},{4,2},{5,3},{6,0},{7,1},{8,14},{9,15},{10,... | collective-permute-start | bytes 393224 | tf_op jit(solution)/shard_map/ppermute | solution.py:35
  93.9 21.2 %collective-permute-start.37 = (bf16[2,256,128]{2,1,0:T(8,128)(2,1)S(1)}, bf16[2,256,128]{2,1,0:T(8,128)(2,1)S(1)}, u32[]{:S(2)}, u32[]{:S(2)}) collective-permute-start(bf16[2,256,128]{2,1,0:T(8,128)(2,1)S(1)} %get-tuple-element.79), channel_id=1, source_target_pairs={{0,2},{1,3},{2,0},{3,1},{4,6},{5,7},{6,4},{7,5},{8,10},{9,11},{10,... | collective-permute-start | bytes 393224 | tf_op jit(solution)/shard_map/ppermute | solution.py:35
  95.5 21.3 %collective-permute-start.38 = (bf16[2,256,128]{2,1,0:T(8,128)(2,1)S(1)}, bf16[2,256,128]{2,1,0:T(8,128)(2,1)S(1)}, u32[]{:S(2)}, u32[]{:S(2)}) collective-permute-start(bf16[2,256,128]{2,1,0:T(8,128)(2,1)S(1)} %get-tuple-element.81), channel_id=1, source_target_pairs={{0,4},{1,5},{2,6},{3,7},{4,0},{5,1},{6,2},{7,3},{8,12},{9,13},{10,... | collective-permute-start | bytes 393224 | tf_op jit(solution)/shard_map/ppermute | solution.py:35
  103.8 13.4 %collective-permute-start.39 = (bf16[2,256,128]{2,1,0:T(8,128)(2,1)S(1)}, bf16[2,256,128]{2,1,0:T(8,128)(2,1)S(1)}, u32[]{:S(2)}, u32[]{:S(2)}) collective-permute-start(bf16[2,256,128]{2,1,0:T(8,128)(2,1)S(1)} %get-tuple-element.80), channel_id=1, source_target_pairs={{0,6},{1,7},{2,4},{3,5},{4,2},{5,3},{6,0},{7,1},{8,14},{9,15},{10,... | collective-permute-start | bytes 393224 | tf_op jit(solution)/shard_map/ppermute | solution.py:35
  105.4 9.3 %collective-permute-start.41 = (bf16[4,2,256,128]{3,2,1,0:T(8,128)(2,1)S(1)}, bf16[4,2,256,128]{3,2,1,0:T(8,128)(2,1)S(1)}, u32[]{:S(2)}, u32[]{:S(2)}) collective-permute-start(bf16[4,2,256,128]{3,2,1,0:T(8,128)(2,1)S(1)} %get-tuple-element.65), channel_id=1, source_target_pairs={{0,1},{1,0},{2,3},{3,2},{4,5},{5,4},{6,7},{7,6},{8,9},{9,8},{10,11... | collective-permute-start | bytes 1572872 | tf_op jit(solution)/shard_map/ppermute | solution.py:35
  105.4 23.9 %collective-permute-start.35 = (bf16[2,256,128]{2,1,0:T(8,128)(2,1)S(1)}, bf16[2,256,128]{2,1,0:T(8,128)(2,1)S(1)}, u32[]{:S(2)}, u32[]{:S(2)}) collective-permute-start(bf16[2,256,128]{2,1,0:T(8,128)(2,1)S(1)} %fusion.10), channel_id=1, source_target_pairs={{0,8},{8,16},{16,24},{24,0},{1,9},{9,17},{17,25},{25,1},{2,10},{10... | collective-permute-start | bytes 393224 | tf_op jit(solution)/shard_map/ppermute | solution.py:39
  114.7 12.7 %collective-permute-start.46 = (bf16[4,2,256,128]{3,2,1,0:T(8,128)(2,1)S(1)}, bf16[4,2,256,128]{3,2,1,0:T(8,128)(2,1)S(1)}, u32[]{:S(2)}, u32[]{:S(2)}) collective-permute-start(bf16[4,2,256,128]{3,2,1,0:T(8,128)(2,1)S(1)} %get-tuple-element.70), channel_id=1, source_target_pairs={{0,1},{1,0},{2,3},{3,2},{4,5},{5,4},{6,7},{7,6},{8,9},{9,8},{10,11... | collective-permute-start | bytes 1572872 | tf_op jit(solution)/shard_map/ppermute | solution.py:35
  116.7 8.2 %collective-permute-start.43 = (bf16[2,256,128]{2,1,0:T(8,128)(2,1)S(1)}, bf16[2,256,128]{2,1,0:T(8,128)(2,1)S(1)}, u32[]{:S(2)}, u32[]{:S(2)}) collective-permute-start(bf16[2,256,128]{2,1,0:T(8,128)(2,1)S(1)} %get-tuple-element.84), channel_id=1, source_target_pairs={{0,4},{1,5},{2,6},{3,7},{4,0},{5,1},{6,2},{7,3},{8,12},{9,13},{10,... | collective-permute-start | bytes 393224 | tf_op jit(solution)/shard_map/ppermute | solution.py:35
  117.3 7.7 %collective-permute-start.44 = (bf16[2,256,128]{2,1,0:T(8,128)(2,1)S(1)}, bf16[2,256,128]{2,1,0:T(8,128)(2,1)S(1)}, u32[]{:S(2)}, u32[]{:S(2)}) collective-permute-start(bf16[2,256,128]{2,1,0:T(8,128)(2,1)S(1)} %get-tuple-element.83), channel_id=1, source_target_pairs={{0,6},{1,7},{2,4},{3,5},{4,2},{5,3},{6,0},{7,1},{8,14},{9,15},{10,... | collective-permute-start | bytes 393224 | tf_op jit(solution)/shard_map/ppermute | solution.py:35
  121.3 9.9 %collective-permute-start.40 = (bf16[2,256,128]{2,1,0:T(8,128)(2,1)S(1)}, bf16[2,256,128]{2,1,0:T(8,128)(2,1)S(1)}, u32[]{:S(2)}, u32[]{:S(2)}) collective-permute-start(bf16[2,256,128]{2,1,0:T(8,128)(2,1)S(1)} %fusion.8), channel_id=1, source_target_pairs={{0,16},{8,24},{16,0},{24,8},{1,17},{9,25},{17,1},{25,9},{2,18},{10... | collective-permute-start | bytes 393224 | tf_op jit(solution)/shard_map/ppermute | solution.py:39
  128.1 7.7 %collective-permute-start.48 = (bf16[2,256,128]{2,1,0:T(8,128)(2,1)S(1)}, bf16[2,256,128]{2,1,0:T(8,128)(2,1)S(1)}, u32[]{:S(2)}, u32[]{:S(2)}) collective-permute-start(bf16[2,256,128]{2,1,0:T(8,128)(2,1)S(1)} %get-tuple-element.87), channel_id=1, source_target_pairs={{0,4},{1,5},{2,6},{3,7},{4,0},{5,1},{6,2},{7,3},{8,12},{9,13},{10,... | collective-permute-start | bytes 393224 | tf_op jit(solution)/shard_map/ppermute | solution.py:35
  (21 other events, 114.6 us)

commit v5 on v4

--- a/solution.py
+++ b/solution.py
@@ -340,31 +340,33 @@
         blocks = [block, *pieces]
         if away == 0:
             pieces = lax.optimization_barrier((*pieces, phase_t[1]))[:-1]
-        if away > 1:
-            pieces = lax.optimization_barrier((*pieces, images[1]))[:-1]
+        else:
+            pieces = lax.optimization_barrier((*pieces, images[min(away, 2) - 1]))[:-1]
         blocks += [tile_swap(piece, tiles, 1) for piece in (block, *pieces)]
         images.append(
             make_image(blocks, phase_t, image_col, lines, total_rows, groups, away)
         )
     foreground = filter_images(images, fg_filter)
 
-    parts, first_halves, second_halves = [], [], []
+    parts, first_halves, second_halves, passed_on = [], [], [], []
     for turn, away in enumerate(list(range(1, groups)) + [0]):
-        here = phase_t
+        waits = []
         if turn >= 2:
-            here = [*here[:3], after(here[3], first_halves[turn - 2])]
+            waits.append(first_halves[turn - 2])
         if turn >= 3:
-            here = [*here[:3], after(here[3], *second_halves[turn - 3])]
-        kept, sent = predict_part(
-            foreground[away], here, predict_col, groups, away
-        )
+            waits += second_halves[turn - 3]
+        if turn == groups - 1:
+            waits += passed_on[turn - 1]
+        here = [*phase_t[:3], after(phase_t[3], *waits)] if waits else phase_t
+        kept, sent = predict_part(foreground[away], here, predict_col, groups, away)
+        if turn == groups - 1:
+            sent = after(sent, *second_halves[turn - 1])
         received = tile_swap(sent, tiles, 1)
         first_halves.append(received)
         total = kept + received.astype(F32)
+        passed_on.append([total[spot].astype(BF16) for spot in range(1, len(masks))])
         received = [
-            tile_swap(total[spot].astype(BF16), tiles, mask)
-            for spot, mask in enumerate(masks)
-            if mask
+            tile_swap(piece, tiles, mask) for piece, mask in zip(passed_on[turn], masks[1:])
         ]
         second_halves.append(received)
         part = total[0] + functools.reduce(jnp.add, [piece.astype(F32) for piece in received])

time: 137 us -> 132 us (0.964)
  waiting for transfers between devices: 19.7 us -> 14.6 us
    ppermute x44, waiting for transfers between devices: 19.2 us -> 10.4 us  [tile_swap(): return lax.ppermute(block, 'tile', [(t, t ^ mask) for t in range(tiles)])]
    ppermute x6, waiting for transfers between devices: 0.58 us -> 4.21 us  [chan_shift(): lax.ppermute(block, 'chan', [(c, (c + away) % groups) for c in range(grou...]
    ppermute x6, starting transfers between devices: 10.5 us -> 8.58 us  [chan_shift(): lax.ppermute(block, 'chan', [(c, (c + away) % groups) for c in range(grou...]
  transfers between devices with their start and end apart: 50 -> 50, of which waited for: 9 -> 8; matrix products, arithmetic and copies ran while one was open for 1% -> 1% of each run, Pallas kernels for 33% -> 34%
where the time goes in v5:
time: 132 us; the launch traced here: 131 us
  Pallas kernels  68.1 us (52%)
  starting transfers between devices  42.1 us (32%)
  waiting for transfers between devices  14.6 us (11%)
  local copies, waits for them, and re-layouts  3.57 us (3%)
  other arithmetic  1.9 us (1%)
    ppermute x44, starting transfers between devices, tile_swap(): return lax.ppermute(block, 'tile', [(t, t ^ mask) for t in range(tiles)])  33.6 us
    pallas_call x4, Pallas kernels, predict_part(): pl.pallas_call(functools.partial(predict_kernel, 1.0 / math.sqrt(L * M),...  30.6 us
    pallas_call x4, Pallas kernels, make_image(): pl.pallas_call(functools.partial(image_kernel, 1.0 / math.sqrt(total_rows...  25.9 us
    ppermute x44, waiting for transfers between devices, tile_swap(): return lax.ppermute(block, 'tile', [(t, t ^ mask) for t in range(tiles)])  10.4 us
    pallas_call x1, Pallas kernels, filter_images(): pl.pallas_call(functools.partial(filter_kernel, groups, step), out_shape=...  9.61 us
    ppermute x6, starting transfers between devices, chan_shift(): lax.ppermute(block, 'chan', [(c, (c + away) % groups) for c in range(grou...  8.58 us
    ppermute x6, waiting for transfers between devices, chan_shift(): lax.ppermute(block, 'chan', [(c, (c + away) % groups) for c in range(grou...  4.21 us
  transfers between devices with their start and end apart: 50, of which 8 were waited for; matrix products, arithmetic and copies ran while one was open for 1% of the time, Pallas kernels for 34%

profile of v5, /device:TPU:0, one launch (start us, length us, event | category | flops | bytes accessed | tf_op | source)
XLA Modules:
  0.0 130.7 jit_solution(11633577163657709421)
XLA Ops:
  0.0 1.0 copy.7
  2.1 3.0 %collective-permute-start = (bf16[2,256,128]{2,1,0:T(8,128)(2,1)S(1)}, bf16[2,256,128]{2,1,0:T(8,128)(2,1)S(1)}, u32[]{:S(2)}, u32[]{:S(2)}) collective-permute-start(bf16[2,256,128]{2,1,0:T(8,128)(2,1)S(1)} %multiply_bitcast_fusion.refs_0_), channel_id=1, source_target_pairs={{0,2},{1,3},{2,0},{3,1},{4,6},{5,7},{6,4},{7,5},{8,10},{9,11},{10,... | collective-permute-start | bytes 393224 | tf_op jit(solution)/shard_map/ppermute | solution.py:35
  5.1 1.5 %collective-permute-start.1 = (bf16[2,256,128]{2,1,0:T(8,128)(2,1)S(1)}, bf16[2,256,128]{2,1,0:T(8,128)(2,1)S(1)}, u32[]{:S(2)}, u32[]{:S(2)}) collective-permute-start(bf16[2,256,128]{2,1,0:T(8,128)(2,1)S(1)} %multiply_bitcast_fusion.refs_0_), channel_id=1, source_target_pairs={{0,4},{1,5},{2,6},{3,7},{4,0},{5,1},{6,2},{7,3},{8,12},{9,13},{10,... | collective-permute-start | bytes 393224 | tf_op jit(solution)/shard_map/ppermute | solution.py:35
  6.6 2.0 %collective-permute-start.7 = (bf16[2,256,128]{2,1,0:T(8,128)(2,1)S(1)}, bf16[2,256,128]{2,1,0:T(8,128)(2,1)S(1)}, u32[]{:S(2)}, u32[]{:S(2)}) collective-permute-start(bf16[2,256,128]{2,1,0:T(8,128)(2,1)S(1)} %multiply_bitcast_fusion.refs_0_), channel_id=1, source_target_pairs={{0,8},{8,16},{16,24},{24,0},{1,9},{9,17},{17,25},{25,1},{2,10},{10... | collective-permute-start | bytes 393224 | tf_op jit(solution)/shard_map/ppermute | solution.py:39
  10.1 2.1 %tables.1 = (f32[128,16,128]{2,1,0:T(8,128)S(1)}, f32[2,8,8,128]{3,2,1,0:T(8,128)S(1)}, f32[128,16,128]{2,1,0:T(8,128)S(1)}, f32[2,8,8,128]{3,2,1,0:T(8,128)S(1)...) custom-call(s32[8,128]{1,0:T(8,128)S(1)} %bitcast.64, s32[8,128]{1,0:T(8,128)S(1)} %bitcast.65), custom_call_target="tpu_custom_call" | custom-call | flops 3221225472 | bytes 4194304 | tf_op jit(solution)/shard_map/tables/pallas_call | solution.py:105
  13.4 1.5 %collective-permute-done.7.refs_0_ = bf16[2,256,128]{2,1,0:T(8,128)(2,1)S(1)} collective-permute-done((bf16[2,256,128]{2,1,0:T(8,128)(2,1)S(1)}, bf16[2,256,128]{2,1,0:T(8,128)(2,1)S(1)}, u32[]{:S(2)}, u32[]{:S(2)}) %collective-permute-start.7) | collective-permute-done | bytes 131104 | tf_op jit(solution)/shard_map/ppermute | solution.py:39
  14.9 2.1 %collective-permute-start.23 = (bf16[2,256,128]{2,1,0:T(8,128)(2,1)S(1)}, bf16[2,256,128]{2,1,0:T(8,128)(2,1)S(1)}, u32[]{:S(2)}, u32[]{:S(2)}) collective-permute-start(bf16[2,256,128]{2,1,0:T(8,128)(2,1)S(1)} %multiply_bitcast_fusion.refs_0_), channel_id=1, source_target_pairs={{0,24},{8,0},{16,8},{24,16},{1,25},{9,1},{17,9},{25,17},{2,26},{10... | collective-permute-start | bytes 393224 | tf_op jit(solution)/shard_map/ppermute | solution.py:39
  17.0 2.1 %collective-permute-start.10 = (bf16[2,256,128]{2,1,0:T(8,128)(2,1)S(1)}, bf16[2,256,128]{2,1,0:T(8,128)(2,1)S(1)}, u32[]{:S(2)}, u32[]{:S(2)}) collective-permute-start(bf16[2,256,128]{2,1,0:T(8,128)(2,1)S(1)} %collective-permute-done.7.refs_0_), channel_id=1, source_target_pairs={{0,6},{1,7},{2,4},{3,5},{4,2},{5,3},{6,0},{7,1},{8,14},{9,15},{10,... | collective-permute-start | bytes 393224 | tf_op jit(solution)/shard_map/ppermute | solution.py:35
  20.6 6.6 %image.4.refs_0_ = bf16[16,256,256]{2,1,0:T(8,128)(2,1)S(1)} custom-call(f32[128,16,128]{2,1,0:T(8,128)S(1)} %get-tuple-element.41.step_c, f32[2,8,8,128]{3,2,1,0:T(8,128)S(1)} %get-tuple-element.42.step_f, f32[128,16,128]{2,1,0:T(8,128)S(1)} %get-tuple-element.43.start_c, f32[2,8,8,128]{3,2,1,0:T(8,128)S(1)} %get-tuple-element.73.start_f, ...), custom_call_target="tpu_custom_call" | custom-call | flops 8589934592 | bytes 8388608 | tf_op jit(solution)/shard_map/image/pallas_call | solution.py:188
  28.3 1.2 collective-permute-start.24
  29.5 1.4 %collective-permute-start.25 = (bf16[2,256,128]{2,1,0:T(8,128)(2,1)S(1)}, bf16[2,256,128]{2,1,0:T(8,128)(2,1)S(1)}, u32[]{:S(2)}, u32[]{:S(2)}) collective-permute-start(bf16[2,256,128]{2,1,0:T(8,128)(2,1)S(1)} %collective-permute-done.23.refs_0_), channel_id=1, source_target_pairs={{0,4},{1,5},{2,6},{3,7},{4,0},{5,1},{6,2},{7,3},{8,12},{9,13},{10,... | collective-permute-start | bytes 393224 | tf_op jit(solution)/shard_map/ppermute | solution.py:35
  31.8 1.2 collective-permute-start.16
  33.0 1.4 %collective-permute-start.17 = (bf16[2,256,128]{2,1,0:T(8,128)(2,1)S(1)}, bf16[2,256,128]{2,1,0:T(8,128)(2,1)S(1)}, u32[]{:S(2)}, u32[]{:S(2)}) collective-permute-start(bf16[2,256,128]{2,1,0:T(8,128)(2,1)S(1)} %collective-permute-done.15.refs_0_), channel_id=1, source_target_pairs={{0,4},{1,5},{2,6},{3,7},{4,0},{5,1},{6,2},{7,3},{8,12},{9,13},{10,... | collective-permute-start | bytes 393224 | tf_op jit(solution)/shard_map/ppermute | solution.py:35
  34.4 6.4 %image.5.refs_1_ = bf16[16,256,256]{2,1,0:T(8,128)(2,1)S(1)} custom-call(f32[128,16,128]{2,1,0:T(8,128)S(1)} %get-tuple-element.41.step_c, f32[2,8,8,128]{3,2,1,0:T(8,128)S(1)} %get-tuple-element.42.step_f, f32[128,16,128]{2,1,0:T(8,128)S(1)} %get-tuple-element.43.start_c, f32[2,8,8,128]{3,2,1,0:T(8,128)S(1)} %get-tuple-element.73.start_f, ...), custom_call_target="tpu_custom_call" | custom-call | flops 8589934592 | bytes 8388608 | tf_op jit(solution)/shard_map/image/pallas_call | solution.py:188
  42.9 4.0 %collective-permute-done.18.refs_3_ = bf16[2,256,128]{2,1,0:T(8,128)(2,1)S(1)} collective-permute-done((bf16[2,256,128]{2,1,0:T(8,128)(2,1)S(1)}, bf16[2,256,128]{2,1,0:T(8,128)(2,1)S(1)}, u32[]{:S(2)}, u32[]{:S(2)}) %collective-permute-start.18) | collective-permute-done | bytes 131104 | tf_op jit(solution)/shard_map/ppermute | solution.py:35
  47.9 6.4 %image.7.refs_3_ = bf16[16,256,256]{2,1,0:T(8,128)(2,1)S(1)} custom-call(f32[128,16,128]{2,1,0:T(8,128)S(1)} %get-tuple-element.41.step_c, f32[2,8,8,128]{3,2,1,0:T(8,128)S(1)} %get-tuple-element.42.step_f, f32[128,16,128]{2,1,0:T(8,128)S(1)} %get-tuple-element.43.start_c, f32[2,8,8,128]{3,2,1,0:T(8,128)S(1)} %get-tuple-element.73.start_f, ...), custom_call_target="tpu_custom_call" | custom-call | flops 8589934592 | bytes 8388608 | tf_op jit(solution)/shard_map/image/pallas_call | solution.py:188
  54.3 6.4 %image.6.refs_2_ = bf16[16,256,256]{2,1,0:T(8,128)(2,1)S(1)} custom-call(f32[128,16,128]{2,1,0:T(8,128)S(1)} %get-tuple-element.41.step_c, f32[2,8,8,128]{3,2,1,0:T(8,128)S(1)} %get-tuple-element.42.step_f, f32[128,16,128]{2,1,0:T(8,128)S(1)} %get-tuple-element.43.start_c, f32[2,8,8,128]{3,2,1,0:T(8,128)S(1)} %get-tuple-element.73.start_f, ...), custom_call_target="tpu_custom_call" | custom-call | flops 8589934592 | bytes 8388608 | tf_op jit(solution)/shard_map/image/pallas_call | solution.py:188
  60.8 9.6 %filter.1 = (bf16[16,256,256]{2,1,0:T(8,128)(2,1)S(1)}, bf16[16,256,256]{2,1,0:T(8,128)(2,1)S(1)}, bf16[16,256,256]{2,1,0:T(8,128)(2,1)S(1)}, bf16[16,256,256]{2,1,0:T(8,128)(2,1)S(1)}) custom-call(bf16[1024,1024]{1,0:T(8,128)(2,1)S(1)} %copy-done, bf16[16,256,256]{2,1,0:T(8,128)(2,1)S(1)} %image.4.refs_0_, bf16[16,256,256]{2,1,0:T(8,128)(2,1)S(1)} %image.5.refs_1_, ...), custom_call_target="tpu_custom_call" | custom-call | flops 8589934592 | bytes 18874368 | tf_op jit(solution)/shard_map/filter/pallas_call | solution.py:238
  70.4 7.6 %predict.4 = (f32[4,2,256,128]{3,2,1,0:T(8,128)S(1)}, bf16[4,2,256,128]{3,2,1,0:T(8,128)(2,1)S(1)}) custom-call(bf16[16,256,256]{2,1,0:T(8,128)(2,1)S(1)} %get-tuple-element.61.image_ref, bf16[256,2048]{1,0:T(8,128)(2,1)S(1)} %get-tuple-element.62.col_ref, f32[128,16,128]{2,1,0:T(8,128)S(1)} %get-tuple-element.41.step_c, ...), custom_call_target="tpu_custom_call" | custom-call | flops 8589934592 | bytes 8388608 | tf_op jit(solution)/shard_map/predict/pallas_call | solution.py:311
  78.1 7.6 %predict.5 = (f32[4,2,256,128]{3,2,1,0:T(8,128)S(1)}, bf16[4,2,256,128]{3,2,1,0:T(8,128)(2,1)S(1)}) custom-call(bf16[16,256,256]{2,1,0:T(8,128)(2,1)S(1)} %get-tuple-element.65.image_ref, bf16[256,2048]{1,0:T(8,128)(2,1)S(1)} %get-tuple-element.62.col_ref, f32[128,16,128]{2,1,0:T(8,128)S(1)} %get-tuple-element.41.step_c, ...), custom_call_target="tpu_custom_call" | custom-call | flops 8589934592 | bytes 8388608 | tf_op jit(solution)/shard_map/predict/pallas_call | solution.py:311
  87.9 2.1 %collective-permute-start.34 = (bf16[2,256,128]{2,1,0:T(8,128)(2,1)S(1)}, bf16[2,256,128]{2,1,0:T(8,128)(2,1)S(1)}, u32[]{:S(2)}, u32[]{:S(2)}) collective-permute-start(bf16[2,256,128]{2,1,0:T(8,128)(2,1)S(1)} %get-tuple-element.94), channel_id=1, source_target_pairs={{0,6},{1,7},{2,4},{3,5},{4,2},{5,3},{6,0},{7,1},{8,14},{9,15},{10,... | collective-permute-start | bytes 393224 | tf_op jit(solution)/shard_map/ppermute | solution.py:35
  90.0 7.8 %predict.6 = (f32[4,2,256,128]{3,2,1,0:T(8,128)S(1)}, bf16[4,2,256,128]{3,2,1,0:T(8,128)(2,1)S(1)}) custom-call(bf16[16,256,256]{2,1,0:T(8,128)(2,1)S(1)} %get-tuple-element.68.image_ref, bf16[256,2048]{1,0:T(8,128)(2,1)S(1)} %get-tuple-element.62.col_ref, f32[128,16,128]{2,1,0:T(8,128)S(1)} %get-tuple-element.41.step_c, ...), custom_call_target="tpu_custom_call" | custom-call | flops 8589934592 | bytes 8388608 | tf_op jit(solution)/shard_map/predict/pallas_call | solution.py:311
  101.5 1.5 %collective-permute-start.43 = (bf16[2,256,128]{2,1,0:T(8,128)(2,1)S(1)}, bf16[2,256,128]{2,1,0:T(8,128)(2,1)S(1)}, u32[]{:S(2)}, u32[]{:S(2)}) collective-permute-start(bf16[2,256,128]{2,1,0:T(8,128)(2,1)S(1)} %get-tuple-element.92), channel_id=1, source_target_pairs={{0,4},{1,5},{2,6},{3,7},{4,0},{5,1},{6,2},{7,3},{8,12},{9,13},{10,... | collective-permute-start | bytes 393224 | tf_op jit(solution)/shard_map/ppermute | solution.py:35
  103.0 1.2 collective-permute-start.44
  104.2 7.6 %predict.7 = (f32[4,2,256,128]{3,2,1,0:T(8,128)S(1)}, bf16[4,2,256,128]{3,2,1,0:T(8,128)(2,1)S(1)}) custom-call(bf16[16,256,256]{2,1,0:T(8,128)(2,1)S(1)} %get-tuple-element.72.image_ref, bf16[256,2048]{1,0:T(8,128)(2,1)S(1)} %get-tuple-element.62.col_ref, f32[128,16,128]{2,1,0:T(8,128)S(1)} %get-tuple-element.41.step_c, ...), custom_call_target="tpu_custom_call" | custom-call | flops 8589934592 | bytes 8388608 | tf_op jit(solution)/shard_map/predict/pallas_call | solution.py:311
  111.8 1.8 %collective-permute-start.39 = (bf16[2,256,128]{2,1,0:T(8,128)(2,1)S(1)}, bf16[2,256,128]{2,1,0:T(8,128)(2,1)S(1)}, u32[]{:S(2)}, u32[]{:S(2)}) collective-permute-start(bf16[2,256,128]{2,1,0:T(8,128)(2,1)S(1)} %get-tuple-element.86), channel_id=1, source_target_pairs={{0,6},{1,7},{2,4},{3,5},{4,2},{5,3},{6,0},{7,1},{8,14},{9,15},{10,... | collective-permute-start | bytes 393224 | tf_op jit(solution)/shard_map/ppermute | solution.py:35
  114.7 3.0 %collective-permute-done.39 = bf16[2,256,128]{2,1,0:T(8,128)(2,1)S(1)} collective-permute-done((bf16[2,256,128]{2,1,0:T(8,128)(2,1)S(1)}, bf16[2,256,128]{2,1,0:T(8,128)(2,1)S(1)}, u32[]{:S(2)}, u32[]{:S(2)}) %collective-permute-start.39) | collective-permute-done | bytes 131104 | tf_op jit(solution)/shard_map/ppermute | solution.py:35
  117.8 2.9 %collective-permute-start.40 = (bf16[2,256,128]{2,1,0:T(8,128)(2,1)S(1)}, bf16[2,256,128]{2,1,0:T(8,128)(2,1)S(1)}, u32[]{:S(2)}, u32[]{:S(2)}) collective-permute-start(bf16[2,256,128]{2,1,0:T(8,128)(2,1)S(1)} %fusion.8), channel_id=1, source_target_pairs={{0,16},{8,24},{16,0},{24,8},{1,17},{9,25},{17,1},{25,9},{2,18},{10... | collective-permute-start | bytes 393224 | tf_op jit(solution)/shard_map/ppermute | solution.py:39
  122.4 1.5 %collective-permute-start.48 = (bf16[2,256,128]{2,1,0:T(8,128)(2,1)S(1)}, bf16[2,256,128]{2,1,0:T(8,128)(2,1)S(1)}, u32[]{:S(2)}, u32[]{:S(2)}) collective-permute-start(bf16[2,256,128]{2,1,0:T(8,128)(2,1)S(1)} %get-tuple-element.90), channel_id=1, source_target_pairs={{0,4},{1,5},{2,6},{3,7},{4,0},{5,1},{6,2},{7,3},{8,12},{9,13},{10,... | collective-permute-start | bytes 393224 | tf_op jit(solution)/shard_map/ppermute | solution.py:35
  123.9 1.2 collective-permute-start.49
  125.1 2.1 %collective-permute-done.40 = bf16[2,256,128]{2,1,0:T(8,128)(2,1)S(1)} collective-permute-done((bf16[2,256,128]{2,1,0:T(8,128)(2,1)S(1)}, bf16[2,256,128]{2,1,0:T(8,128)(2,1)S(1)}, u32[]{:S(2)}, u32[]{:S(2)}) %collective-permute-start.40) | collective-permute-done | bytes 131104 | tf_op jit(solution)/shard_map/ppermute | solution.py:39
  127.9 1.9 %collective-permute-done.49 = bf16[2,256,128]{2,1,0:T(8,128)(2,1)S(1)} collective-permute-done((bf16[2,256,128]{2,1,0:T(8,128)(2,1)S(1)}, bf16[2,256,128]{2,1,0:T(8,128)(2,1)S(1)}, u32[]{:S(2)}, u32[]{:S(2)}) %collective-permute-start.49) | collective-permute-done | bytes 131104 | tf_op jit(solution)/shard_map/ppermute | solution.py:35
  (102 shorter events, 20.6 us)
Async XLA Ops:
  2.1 10.0 %collective-permute-start = (bf16[2,256,128]{2,1,0:T(8,128)(2,1)S(1)}, bf16[2,256,128]{2,1,0:T(8,128)(2,1)S(1)}, u32[]{:S(2)}, u32[]{:S(2)}) collective-permute-start(bf16[2,256,128]{2,1,0:T(8,128)(2,1)S(1)} %multiply_bitcast_fusion.refs_0_), channel_id=1, source_target_pairs={{0,2},{1,3},{2,0},{3,1},{4,6},{5,7},{6,4},{7,5},{8,10},{9,11},{10,... | collective-permute-start | bytes 393224 | tf_op jit(solution)/shard_map/ppermute | solution.py:35
  5.1 7.8 %collective-permute-start.1 = (bf16[2,256,128]{2,1,0:T(8,128)(2,1)S(1)}, bf16[2,256,128]{2,1,0:T(8,128)(2,1)S(1)}, u32[]{:S(2)}, u32[]{:S(2)}) collective-permute-start(bf16[2,256,128]{2,1,0:T(8,128)(2,1)S(1)} %multiply_bitcast_fusion.refs_0_), channel_id=1, source_target_pairs={{0,4},{1,5},{2,6},{3,7},{4,0},{5,1},{6,2},{7,3},{8,12},{9,13},{10,... | collective-permute-start | bytes 393224 | tf_op jit(solution)/shard_map/ppermute | solution.py:35
  6.6 10.4 %collective-permute-start.3 = (bf16[2,256,128]{2,1,0:T(8,128)(2,1)S(1)}, bf16[2,256,128]{2,1,0:T(8,128)(2,1)S(1)}, u32[]{:S(2)}, u32[]{:S(2)}) collective-permute-start(bf16[2,256,128]{2,1,0:T(8,128)(2,1)S(1)} %multiply_bitcast_fusion.refs_0_), channel_id=1, source_target_pairs={{0,1},{1,0},{2,3},{3,2},{4,5},{5,4},{6,7},{7,6},{8,9},{9,8},{10,11... | collective-permute-start | bytes 393224 | tf_op jit(solution)/shard_map/ppermute | solution.py:35
  6.6 8.2 %collective-permute-start.7 = (bf16[2,256,128]{2,1,0:T(8,128)(2,1)S(1)}, bf16[2,256,128]{2,1,0:T(8,128)(2,1)S(1)}, u32[]{:S(2)}, u32[]{:S(2)}) collective-permute-start(bf16[2,256,128]{2,1,0:T(8,128)(2,1)S(1)} %multiply_bitcast_fusion.refs_0_), channel_id=1, source_target_pairs={{0,8},{8,16},{16,24},{24,0},{1,9},{9,17},{17,25},{25,1},{2,10},{10... | collective-permute-start | bytes 393224 | tf_op jit(solution)/shard_map/ppermute | solution.py:39
  14.9 13.0 %collective-permute-start.23 = (bf16[2,256,128]{2,1,0:T(8,128)(2,1)S(1)}, bf16[2,256,128]{2,1,0:T(8,128)(2,1)S(1)}, u32[]{:S(2)}, u32[]{:S(2)}) collective-permute-start(bf16[2,256,128]{2,1,0:T(8,128)(2,1)S(1)} %multiply_bitcast_fusion.refs_0_), channel_id=1, source_target_pairs={{0,24},{8,0},{16,8},{24,16},{1,25},{9,1},{17,9},{25,17},{2,26},{10... | collective-permute-start | bytes 393224 | tf_op jit(solution)/shard_map/ppermute | solution.py:39
  17.0 11.3 %collective-permute-start.15 = (bf16[2,256,128]{2,1,0:T(8,128)(2,1)S(1)}, bf16[2,256,128]{2,1,0:T(8,128)(2,1)S(1)}, u32[]{:S(2)}, u32[]{:S(2)}) collective-permute-start(bf16[2,256,128]{2,1,0:T(8,128)(2,1)S(1)} %multiply_bitcast_fusion.refs_0_), channel_id=1, source_target_pairs={{0,16},{8,24},{16,0},{24,8},{1,17},{9,25},{17,1},{25,9},{2,18},{10... | collective-permute-start | bytes 393224 | tf_op jit(solution)/shard_map/ppermute | solution.py:39
  17.0 10.2 %collective-permute-start.10 = (bf16[2,256,128]{2,1,0:T(8,128)(2,1)S(1)}, bf16[2,256,128]{2,1,0:T(8,128)(2,1)S(1)}, u32[]{:S(2)}, u32[]{:S(2)}) collective-permute-start(bf16[2,256,128]{2,1,0:T(8,128)(2,1)S(1)} %collective-permute-done.7.refs_0_), channel_id=1, source_target_pairs={{0,6},{1,7},{2,4},{3,5},{4,2},{5,3},{6,0},{7,1},{8,14},{9,15},{10,... | collective-permute-start | bytes 393224 | tf_op jit(solution)/shard_map/ppermute | solution.py:35
  19.1 8.1 %collective-permute-start.8 = (bf16[2,256,128]{2,1,0:T(8,128)(2,1)S(1)}, bf16[2,256,128]{2,1,0:T(8,128)(2,1)S(1)}, u32[]{:S(2)}, u32[]{:S(2)}) collective-permute-start(bf16[2,256,128]{2,1,0:T(8,128)(2,1)S(1)} %collective-permute-done.7.refs_0_), channel_id=1, source_target_pairs={{0,2},{1,3},{2,0},{3,1},{4,6},{5,7},{6,4},{7,5},{8,10},{9,11},{10,... | collective-permute-start | bytes 393224 | tf_op jit(solution)/shard_map/ppermute | solution.py:35
  20.1 7.2 %collective-permute-start.9 = (bf16[2,256,128]{2,1,0:T(8,128)(2,1)S(1)}, bf16[2,256,128]{2,1,0:T(8,128)(2,1)S(1)}, u32[]{:S(2)}, u32[]{:S(2)}) collective-permute-start(bf16[2,256,128]{2,1,0:T(8,128)(2,1)S(1)} %collective-permute-done.7.refs_0_), channel_id=1, source_target_pairs={{0,4},{1,5},{2,6},{3,7},{4,0},{5,1},{6,2},{7,3},{8,12},{9,13},{10,... | collective-permute-start | bytes 393224 | tf_op jit(solution)/shard_map/ppermute | solution.py:35
  28.3 12.6 %collective-permute-start.24 = (bf16[2,256,128]{2,1,0:T(8,128)(2,1)S(1)}, bf16[2,256,128]{2,1,0:T(8,128)(2,1)S(1)}, u32[]{:S(2)}, u32[]{:S(2)}) collective-permute-start(bf16[2,256,128]{2,1,0:T(8,128)(2,1)S(1)} %collective-permute-done.23.refs_0_), channel_id=1, source_target_pairs={{0,2},{1,3},{2,0},{3,1},{4,6},{5,7},{6,4},{7,5},{8,10},{9,11},{10,... | collective-permute-start | bytes 393224 | tf_op jit(solution)/shard_map/ppermute | solution.py:35
  29.5 12.3 %collective-permute-start.25 = (bf16[2,256,128]{2,1,0:T(8,128)(2,1)S(1)}, bf16[2,256,128]{2,1,0:T(8,128)(2,1)S(1)}, u32[]{:S(2)}, u32[]{:S(2)}) collective-permute-start(bf16[2,256,128]{2,1,0:T(8,128)(2,1)S(1)} %collective-permute-done.23.refs_0_), channel_id=1, source_target_pairs={{0,4},{1,5},{2,6},{3,7},{4,0},{5,1},{6,2},{7,3},{8,12},{9,13},{10,... | collective-permute-start | bytes 393224 | tf_op jit(solution)/shard_map/ppermute | solution.py:35
  30.9 10.9 %collective-permute-start.26 = (bf16[2,256,128]{2,1,0:T(8,128)(2,1)S(1)}, bf16[2,256,128]{2,1,0:T(8,128)(2,1)S(1)}, u32[]{:S(2)}, u32[]{:S(2)}) collective-permute-start(bf16[2,256,128]{2,1,0:T(8,128)(2,1)S(1)} %collective-permute-done.23.refs_0_), channel_id=1, source_target_pairs={{0,6},{1,7},{2,4},{3,5},{4,2},{5,3},{6,0},{7,1},{8,14},{9,15},{10,... | collective-permute-start | bytes 393224 | tf_op jit(solution)/shard_map/ppermute | solution.py:35
  31.8 10.5 %collective-permute-start.16 = (bf16[2,256,128]{2,1,0:T(8,128)(2,1)S(1)}, bf16[2,256,128]{2,1,0:T(8,128)(2,1)S(1)}, u32[]{:S(2)}, u32[]{:S(2)}) collective-permute-start(bf16[2,256,128]{2,1,0:T(8,128)(2,1)S(1)} %collective-permute-done.15.refs_0_), channel_id=1, source_target_pairs={{0,2},{1,3},{2,0},{3,1},{4,6},{5,7},{6,4},{7,5},{8,10},{9,11},{10,... | collective-permute-start | bytes 393224 | tf_op jit(solution)/shard_map/ppermute | solution.py:35
  33.0 9.4 %collective-permute-start.17 = (bf16[2,256,128]{2,1,0:T(8,128)(2,1)S(1)}, bf16[2,256,128]{2,1,0:T(8,128)(2,1)S(1)}, u32[]{:S(2)}, u32[]{:S(2)}) collective-permute-start(bf16[2,256,128]{2,1,0:T(8,128)(2,1)S(1)} %collective-permute-done.15.refs_0_), channel_id=1, source_target_pairs={{0,4},{1,5},{2,6},{3,7},{4,0},{5,1},{6,2},{7,3},{8,12},{9,13},{10,... | collective-permute-start | bytes 393224 | tf_op jit(solution)/shard_map/ppermute | solution.py:35
  46.8 7.5 %collective-permute-start.19 = (bf16[2,256,128]{2,1,0:T(8,128)(2,1)S(1)}, bf16[2,256,128]{2,1,0:T(8,128)(2,1)S(1)}, u32[]{:S(2)}, u32[]{:S(2)}) collective-permute-start(bf16[2,256,128]{2,1,0:T(8,128)(2,1)S(1)} %collective-permute-done.15.refs_0_), channel_id=1, source_target_pairs={{0,1},{1,0},{2,3},{3,2},{4,5},{5,4},{6,7},{7,6},{8,9},{9,8},{10,11... | collective-permute-start | bytes 393224 | tf_op jit(solution)/shard_map/ppermute | solution.py:35
  46.8 7.5 %collective-permute-start.20 = (bf16[2,256,128]{2,1,0:T(8,128)(2,1)S(1)}, bf16[2,256,128]{2,1,0:T(8,128)(2,1)S(1)}, u32[]{:S(2)}, u32[]{:S(2)}) collective-permute-start(bf16[2,256,128]{2,1,0:T(8,128)(2,1)S(1)} %collective-permute-done.16.refs_1_), channel_id=1, source_target_pairs={{0,1},{1,0},{2,3},{3,2},{4,5},{5,4},{6,7},{7,6},{8,9},{9,8},{10,11... | collective-permute-start | bytes 393224 | tf_op jit(solution)/shard_map/ppermute | solution.py:35
  47.3 7.0 %collective-permute-start.21 = (bf16[2,256,128]{2,1,0:T(8,128)(2,1)S(1)}, bf16[2,256,128]{2,1,0:T(8,128)(2,1)S(1)}, u32[]{:S(2)}, u32[]{:S(2)}) collective-permute-start(bf16[2,256,128]{2,1,0:T(8,128)(2,1)S(1)} %collective-permute-done.17.refs_2_), channel_id=1, source_target_pairs={{0,1},{1,0},{2,3},{3,2},{4,5},{5,4},{6,7},{7,6},{8,9},{9,8},{10,11... | collective-permute-start | bytes 393224 | tf_op jit(solution)/shard_map/ppermute | solution.py:35
  47.4 6.9 %collective-permute-start.22 = (bf16[2,256,128]{2,1,0:T(8,128)(2,1)S(1)}, bf16[2,256,128]{2,1,0:T(8,128)(2,1)S(1)}, u32[]{:S(2)}, u32[]{:S(2)}) collective-permute-start(bf16[2,256,128]{2,1,0:T(8,128)(2,1)S(1)} %collective-permute-done.18.refs_3_), channel_id=1, source_target_pairs={{0,1},{1,0},{2,3},{3,2},{4,5},{5,4},{6,7},{7,6},{8,9},{9,8},{10,11... | collective-permute-start | bytes 393224 | tf_op jit(solution)/shard_map/ppermute | solution.py:35
  78.0 8.2 %collective-permute-start.31 = (bf16[4,2,256,128]{3,2,1,0:T(8,128)(2,1)S(1)}, bf16[4,2,256,128]{3,2,1,0:T(8,128)(2,1)S(1)}, u32[]{:S(2)}, u32[]{:S(2)}) collective-permute-start(bf16[4,2,256,128]{3,2,1,0:T(8,128)(2,1)S(1)} %get-tuple-element.64), channel_id=1, source_target_pairs={{0,1},{1,0},{2,3},{3,2},{4,5},{5,4},{6,7},{7,6},{8,9},{9,8},{10,11... | collective-permute-start | bytes 1572872 | tf_op jit(solution)/shard_map/ppermute | solution.py:35
  85.7 12.2 %collective-permute-start.36 = (bf16[4,2,256,128]{3,2,1,0:T(8,128)(2,1)S(1)}, bf16[4,2,256,128]{3,2,1,0:T(8,128)(2,1)S(1)}, u32[]{:S(2)}, u32[]{:S(2)}) collective-permute-start(bf16[4,2,256,128]{3,2,1,0:T(8,128)(2,1)S(1)} %get-tuple-element.67), channel_id=1, source_target_pairs={{0,1},{1,0},{2,3},{3,2},{4,5},{5,4},{6,7},{7,6},{8,9},{9,8},{10,11... | collective-permute-start | bytes 1572872 | tf_op jit(solution)/shard_map/ppermute | solution.py:35
  86.5 14.2 %collective-permute-start.32 = (bf16[2,256,128]{2,1,0:T(8,128)(2,1)S(1)}, bf16[2,256,128]{2,1,0:T(8,128)(2,1)S(1)}, u32[]{:S(2)}, u32[]{:S(2)}) collective-permute-start(bf16[2,256,128]{2,1,0:T(8,128)(2,1)S(1)} %get-tuple-element.96), channel_id=1, source_target_pairs={{0,2},{1,3},{2,0},{3,1},{4,6},{5,7},{6,4},{7,5},{8,10},{9,11},{10,... | collective-permute-start | bytes 393224 | tf_op jit(solution)/shard_map/ppermute | solution.py:35
  87.4 14.1 %collective-permute-start.33 = (bf16[2,256,128]{2,1,0:T(8,128)(2,1)S(1)}, bf16[2,256,128]{2,1,0:T(8,128)(2,1)S(1)}, u32[]{:S(2)}, u32[]{:S(2)}) collective-permute-start(bf16[2,256,128]{2,1,0:T(8,128)(2,1)S(1)} %get-tuple-element.95), channel_id=1, source_target_pairs={{0,4},{1,5},{2,6},{3,7},{4,0},{5,1},{6,2},{7,3},{8,12},{9,13},{10,... | collective-permute-start | bytes 393224 | tf_op jit(solution)/shard_map/ppermute | solution.py:35
  87.9 15.1 %collective-permute-start.34 = (bf16[2,256,128]{2,1,0:T(8,128)(2,1)S(1)}, bf16[2,256,128]{2,1,0:T(8,128)(2,1)S(1)}, u32[]{:S(2)}, u32[]{:S(2)}) collective-permute-start(bf16[2,256,128]{2,1,0:T(8,128)(2,1)S(1)} %get-tuple-element.94), channel_id=1, source_target_pairs={{0,6},{1,7},{2,4},{3,5},{4,2},{5,3},{6,0},{7,1},{8,14},{9,15},{10,... | collective-permute-start | bytes 393224 | tf_op jit(solution)/shard_map/ppermute | solution.py:35
  98.1 16.6 %collective-permute-start.37 = (bf16[2,256,128]{2,1,0:T(8,128)(2,1)S(1)}, bf16[2,256,128]{2,1,0:T(8,128)(2,1)S(1)}, u32[]{:S(2)}, u32[]{:S(2)}) collective-permute-start(bf16[2,256,128]{2,1,0:T(8,128)(2,1)S(1)} %get-tuple-element.85), channel_id=1, source_target_pairs={{0,2},{1,3},{2,0},{3,1},{4,6},{5,7},{6,4},{7,5},{8,10},{9,11},{10,... | collective-permute-start | bytes 393224 | tf_op jit(solution)/shard_map/ppermute | solution.py:35
  99.8 14.9 %collective-permute-start.38 = (bf16[2,256,128]{2,1,0:T(8,128)(2,1)S(1)}, bf16[2,256,128]{2,1,0:T(8,128)(2,1)S(1)}, u32[]{:S(2)}, u32[]{:S(2)}) collective-permute-start(bf16[2,256,128]{2,1,0:T(8,128)(2,1)S(1)} %get-tuple-element.87), channel_id=1, source_target_pairs={{0,4},{1,5},{2,6},{3,7},{4,0},{5,1},{6,2},{7,3},{8,12},{9,13},{10,... | collective-permute-start | bytes 393224 | tf_op jit(solution)/shard_map/ppermute | solution.py:35
  100.6 11.2 %collective-permute-start.42 = (bf16[2,256,128]{2,1,0:T(8,128)(2,1)S(1)}, bf16[2,256,128]{2,1,0:T(8,128)(2,1)S(1)}, u32[]{:S(2)}, u32[]{:S(2)}) collective-permute-start(bf16[2,256,128]{2,1,0:T(8,128)(2,1)S(1)} %get-tuple-element.93), channel_id=1, source_target_pairs={{0,2},{1,3},{2,0},{3,1},{4,6},{5,7},{6,4},{7,5},{8,10},{9,11},{10,... | collective-permute-start | bytes 393224 | tf_op jit(solution)/shard_map/ppermute | solution.py:35
  101.5 12.1 %collective-permute-start.43 = (bf16[2,256,128]{2,1,0:T(8,128)(2,1)S(1)}, bf16[2,256,128]{2,1,0:T(8,128)(2,1)S(1)}, u32[]{:S(2)}, u32[]{:S(2)}) collective-permute-start(bf16[2,256,128]{2,1,0:T(8,128)(2,1)S(1)} %get-tuple-element.92), channel_id=1, source_target_pairs={{0,4},{1,5},{2,6},{3,7},{4,0},{5,1},{6,2},{7,3},{8,12},{9,13},{10,... | collective-permute-start | bytes 393224 | tf_op jit(solution)/shard_map/ppermute | solution.py:35
  103.0 10.6 %collective-permute-start.44 = (bf16[2,256,128]{2,1,0:T(8,128)(2,1)S(1)}, bf16[2,256,128]{2,1,0:T(8,128)(2,1)S(1)}, u32[]{:S(2)}, u32[]{:S(2)}) collective-permute-start(bf16[2,256,128]{2,1,0:T(8,128)(2,1)S(1)} %get-tuple-element.91), channel_id=1, source_target_pairs={{0,6},{1,7},{2,4},{3,5},{4,2},{5,3},{6,0},{7,1},{8,14},{9,15},{10,... | collective-permute-start | bytes 393224 | tf_op jit(solution)/shard_map/ppermute | solution.py:35
  113.6 7.7 %collective-permute-start.46 = (bf16[4,2,256,128]{3,2,1,0:T(8,128)(2,1)S(1)}, bf16[4,2,256,128]{3,2,1,0:T(8,128)(2,1)S(1)}, u32[]{:S(2)}, u32[]{:S(2)}) collective-permute-start(bf16[4,2,256,128]{3,2,1,0:T(8,128)(2,1)S(1)} %get-tuple-element.76), channel_id=1, source_target_pairs={{0,1},{1,0},{2,3},{3,2},{4,5},{5,4},{6,7},{7,6},{8,9},{9,8},{10,11... | collective-permute-start | bytes 1572872 | tf_op jit(solution)/shard_map/ppermute | solution.py:35
  113.7 10.2 %collective-permute-start.35 = (bf16[2,256,128]{2,1,0:T(8,128)(2,1)S(1)}, bf16[2,256,128]{2,1,0:T(8,128)(2,1)S(1)}, u32[]{:S(2)}, u32[]{:S(2)}) collective-permute-start(bf16[2,256,128]{2,1,0:T(8,128)(2,1)S(1)} %fusion.10), channel_id=1, source_target_pairs={{0,8},{8,16},{16,24},{24,0},{1,9},{9,17},{17,25},{25,1},{2,10},{10... | collective-permute-start | bytes 393224 | tf_op jit(solution)/shard_map/ppermute | solution.py:39
  117.8 9.4 %collective-permute-start.40 = (bf16[2,256,128]{2,1,0:T(8,128)(2,1)S(1)}, bf16[2,256,128]{2,1,0:T(8,128)(2,1)S(1)}, u32[]{:S(2)}, u32[]{:S(2)}) collective-permute-start(bf16[2,256,128]{2,1,0:T(8,128)(2,1)S(1)} %fusion.8), channel_id=1, source_target_pairs={{0,16},{8,24},{16,0},{24,8},{1,17},{9,25},{17,1},{25,9},{2,18},{10... | collective-permute-start | bytes 393224 | tf_op jit(solution)/shard_map/ppermute | solution.py:39
  120.8 7.1 %collective-permute-start.45 = (bf16[2,256,128]{2,1,0:T(8,128)(2,1)S(1)}, bf16[2,256,128]{2,1,0:T(8,128)(2,1)S(1)}, u32[]{:S(2)}, u32[]{:S(2)}) collective-permute-start(bf16[2,256,128]{2,1,0:T(8,128)(2,1)S(1)} %fusion.6), channel_id=1, source_target_pairs={{0,24},{8,0},{16,8},{24,16},{1,25},{9,1},{17,9},{25,17},{2,26},{10... | collective-permute-start | bytes 393224 | tf_op jit(solution)/shard_map/ppermute | solution.py:39
  (21 other events, 99.0 us)

commit v6 on v5

--- a/solution.py
+++ b/solution.py
@@ -28,7 +28,7 @@
 
 
 def chip_masks(tiles):
-    return [mask for mask in range(0, tiles, 2)]
+    return [0] + sorted(range(2, tiles, 2), key=lambda mask: -mask.bit_count())
 
 
 def tile_swap(block, tiles, mask):

time: 132 us -> 129 us (0.977)
  waiting for transfers between devices: 14.6 us -> 13.2 us
    ppermute x44, waiting for transfers between devices: 10.4 us -> 9.04 us  [tile_swap(): return lax.ppermute(block, 'tile', [(t, t ^ mask) for t in range(tiles)])]
  transfers between devices with their start and end apart: 50 -> 50, of which waited for: 8 -> 10; matrix products, arithmetic and copies ran while one was open for 1% -> 1% of each run, Pallas kernels for 34% -> 35%
where the time goes in v6:
time: 129 us
  Pallas kernels  68.1 us (53%)
  starting transfers between devices  41.7 us (32%)
  waiting for transfers between devices  13.2 us (10%)
  local copies, waits for them, and re-layouts  3.57 us (3%)
  other arithmetic  1.9 us (1%)
    ppermute x44, starting transfers between devices, tile_swap(): return lax.ppermute(block, 'tile', [(t, t ^ mask) for t in range(tiles)])  33.4 us
    pallas_call x4, Pallas kernels, predict_part(): pl.pallas_call(functools.partial(predict_kernel, 1.0 / math.sqrt(L * M),...  30.6 us
    pallas_call x4, Pallas kernels, make_image(): pl.pallas_call(functools.partial(image_kernel, 1.0 / math.sqrt(total_rows...  25.9 us
    pallas_call x1, Pallas kernels, filter_images(): pl.pallas_call(functools.partial(filter_kernel, groups, step), out_shape=...  9.61 us
    ppermute x44, waiting for transfers between devices, tile_swap(): return lax.ppermute(block, 'tile', [(t, t ^ mask) for t in range(tiles)])  9.04 us
    ppermute x6, starting transfers between devices, chan_shift(): lax.ppermute(block, 'chan', [(c, (c + away) % groups) for c in range(grou...  8.27 us
    ppermute x6, waiting for transfers between devices, chan_shift(): lax.ppermute(block, 'chan', [(c, (c + away) % groups) for c in range(grou...  4.19 us
  transfers between devices with their start and end apart: 50, of which 10 were waited for; matrix products, arithmetic and copies ran while one was open for 1% of the time, Pallas kernels for 35%

profile of v6, /device:TPU:0, one launch (start us, length us, event | category | flops | bytes accessed | tf_op | source)
XLA Modules:
  0.0 128.9 jit_solution(15202170827980545688)
XLA Ops:
  0.0 1.0 copy.7
  2.1 4.0 %collective-permute-start = (bf16[2,256,128]{2,1,0:T(8,128)(2,1)S(1)}, bf16[2,256,128]{2,1,0:T(8,128)(2,1)S(1)}, u32[]{:S(2)}, u32[]{:S(2)}) collective-permute-start(bf16[2,256,128]{2,1,0:T(8,128)(2,1)S(1)} %multiply_bitcast_fusion.refs_0_), channel_id=1, source_target_pairs={{0,6},{1,7},{2,4},{3,5},{4,2},{5,3},{6,0},{7,1},{8,14},{9,15},{10,... | collective-permute-start | bytes 393224 | tf_op jit(solution)/shard_map/ppermute | solution.py:35
  6.7 2.0 %collective-permute-start.7 = (bf16[2,256,128]{2,1,0:T(8,128)(2,1)S(1)}, bf16[2,256,128]{2,1,0:T(8,128)(2,1)S(1)}, u32[]{:S(2)}, u32[]{:S(2)}) collective-permute-start(bf16[2,256,128]{2,1,0:T(8,128)(2,1)S(1)} %multiply_bitcast_fusion.refs_0_), channel_id=1, source_target_pairs={{0,8},{8,16},{16,24},{24,0},{1,9},{9,17},{17,25},{25,1},{2,10},{10... | collective-permute-start | bytes 393224 | tf_op jit(solution)/shard_map/ppermute | solution.py:39
  10.1 2.1 %tables.1 = (f32[128,16,128]{2,1,0:T(8,128)S(1)}, f32[2,8,8,128]{3,2,1,0:T(8,128)S(1)}, f32[128,16,128]{2,1,0:T(8,128)S(1)}, f32[2,8,8,128]{3,2,1,0:T(8,128)S(1)...) custom-call(s32[8,128]{1,0:T(8,128)S(1)} %bitcast.64, s32[8,128]{1,0:T(8,128)S(1)} %bitcast.65), custom_call_target="tpu_custom_call" | custom-call | flops 3221225472 | bytes 4194304 | tf_op jit(solution)/shard_map/tables/pallas_call | solution.py:105
  13.1 1.7 %collective-permute-done.7.refs_0_ = bf16[2,256,128]{2,1,0:T(8,128)(2,1)S(1)} collective-permute-done((bf16[2,256,128]{2,1,0:T(8,128)(2,1)S(1)}, bf16[2,256,128]{2,1,0:T(8,128)(2,1)S(1)}, u32[]{:S(2)}, u32[]{:S(2)}) %collective-permute-start.7) | collective-permute-done | bytes 131104 | tf_op jit(solution)/shard_map/ppermute | solution.py:39
  14.9 1.9 %collective-permute-start.23 = (bf16[2,256,128]{2,1,0:T(8,128)(2,1)S(1)}, bf16[2,256,128]{2,1,0:T(8,128)(2,1)S(1)}, u32[]{:S(2)}, u32[]{:S(2)}) collective-permute-start(bf16[2,256,128]{2,1,0:T(8,128)(2,1)S(1)} %multiply_bitcast_fusion.refs_0_), channel_id=1, source_target_pairs={{0,24},{8,0},{16,8},{24,16},{1,25},{9,1},{17,9},{25,17},{2,26},{10... | collective-permute-start | bytes 393224 | tf_op jit(solution)/shard_map/ppermute | solution.py:39
  16.8 1.5 %collective-permute-start.10 = (bf16[2,256,128]{2,1,0:T(8,128)(2,1)S(1)}, bf16[2,256,128]{2,1,0:T(8,128)(2,1)S(1)}, u32[]{:S(2)}, u32[]{:S(2)}) collective-permute-start(bf16[2,256,128]{2,1,0:T(8,128)(2,1)S(1)} %collective-permute-done.7.refs_0_), channel_id=1, source_target_pairs={{0,4},{1,5},{2,6},{3,7},{4,0},{5,1},{6,2},{7,3},{8,12},{9,13},{10,... | collective-permute-start | bytes 393224 | tf_op jit(solution)/shard_map/ppermute | solution.py:35
  18.3 1.5 %collective-permute-start.8 = (bf16[2,256,128]{2,1,0:T(8,128)(2,1)S(1)}, bf16[2,256,128]{2,1,0:T(8,128)(2,1)S(1)}, u32[]{:S(2)}, u32[]{:S(2)}) collective-permute-start(bf16[2,256,128]{2,1,0:T(8,128)(2,1)S(1)} %collective-permute-done.7.refs_0_), channel_id=1, source_target_pairs={{0,6},{1,7},{2,4},{3,5},{4,2},{5,3},{6,0},{7,1},{8,14},{9,15},{10,... | collective-permute-start | bytes 393224 | tf_op jit(solution)/shard_map/ppermute | solution.py:35
  20.3 6.6 %image.4.refs_0_ = bf16[16,256,256]{2,1,0:T(8,128)(2,1)S(1)} custom-call(f32[128,16,128]{2,1,0:T(8,128)S(1)} %get-tuple-element.41.step_c, f32[2,8,8,128]{3,2,1,0:T(8,128)S(1)} %get-tuple-element.42.step_f, f32[128,16,128]{2,1,0:T(8,128)S(1)} %get-tuple-element.43.start_c, f32[2,8,8,128]{3,2,1,0:T(8,128)S(1)} %get-tuple-element.73.start_f, ...), custom_call_target="tpu_custom_call" | custom-call | flops 8589934592 | bytes 8388608 | tf_op jit(solution)/shard_map/image/pallas_call | solution.py:188
  28.0 2.4 %collective-permute-start.24 = (bf16[2,256,128]{2,1,0:T(8,128)(2,1)S(1)}, bf16[2,256,128]{2,1,0:T(8,128)(2,1)S(1)}, u32[]{:S(2)}, u32[]{:S(2)}) collective-permute-start(bf16[2,256,128]{2,1,0:T(8,128)(2,1)S(1)} %collective-permute-done.23.refs_0_), channel_id=1, source_target_pairs={{0,6},{1,7},{2,4},{3,5},{4,2},{5,3},{6,0},{7,1},{8,14},{9,15},{10,... | collective-permute-start | bytes 393224 | tf_op jit(solution)/shard_map/ppermute | solution.py:35
  31.5 2.4 %collective-permute-start.16 = (bf16[2,256,128]{2,1,0:T(8,128)(2,1)S(1)}, bf16[2,256,128]{2,1,0:T(8,128)(2,1)S(1)}, u32[]{:S(2)}, u32[]{:S(2)}) collective-permute-start(bf16[2,256,128]{2,1,0:T(8,128)(2,1)S(1)} %collective-permute-done.15.refs_0_), channel_id=1, source_target_pairs={{0,6},{1,7},{2,4},{3,5},{4,2},{5,3},{6,0},{7,1},{8,14},{9,15},{10,... | collective-permute-start | bytes 393224 | tf_op jit(solution)/shard_map/ppermute | solution.py:35
  34.5 6.4 %image.5.refs_1_ = bf16[16,256,256]{2,1,0:T(8,128)(2,1)S(1)} custom-call(f32[128,16,128]{2,1,0:T(8,128)S(1)} %get-tuple-element.41.step_c, f32[2,8,8,128]{3,2,1,0:T(8,128)S(1)} %get-tuple-element.42.step_f, f32[128,16,128]{2,1,0:T(8,128)S(1)} %get-tuple-element.43.start_c, f32[2,8,8,128]{3,2,1,0:T(8,128)S(1)} %get-tuple-element.73.start_f, ...), custom_call_target="tpu_custom_call" | custom-call | flops 8589934592 | bytes 8388608 | tf_op jit(solution)/shard_map/image/pallas_call | solution.py:188
  42.9 3.1 %collective-permute-done.18.refs_3_ = bf16[2,256,128]{2,1,0:T(8,128)(2,1)S(1)} collective-permute-done((bf16[2,256,128]{2,1,0:T(8,128)(2,1)S(1)}, bf16[2,256,128]{2,1,0:T(8,128)(2,1)S(1)}, u32[]{:S(2)}, u32[]{:S(2)}) %collective-permute-start.18) | collective-permute-done | bytes 131104 | tf_op jit(solution)/shard_map/ppermute | solution.py:35
  47.0 6.4 %image.7.refs_3_ = bf16[16,256,256]{2,1,0:T(8,128)(2,1)S(1)} custom-call(f32[128,16,128]{2,1,0:T(8,128)S(1)} %get-tuple-element.41.step_c, f32[2,8,8,128]{3,2,1,0:T(8,128)S(1)} %get-tuple-element.42.step_f, f32[128,16,128]{2,1,0:T(8,128)S(1)} %get-tuple-element.43.start_c, f32[2,8,8,128]{3,2,1,0:T(8,128)S(1)} %get-tuple-element.73.start_f, ...), custom_call_target="tpu_custom_call" | custom-call | flops 8589934592 | bytes 8388608 | tf_op jit(solution)/shard_map/image/pallas_call | solution.py:188
  53.5 6.4 %image.6.refs_2_ = bf16[16,256,256]{2,1,0:T(8,128)(2,1)S(1)} custom-call(f32[128,16,128]{2,1,0:T(8,128)S(1)} %get-tuple-element.41.step_c, f32[2,8,8,128]{3,2,1,0:T(8,128)S(1)} %get-tuple-element.42.step_f, f32[128,16,128]{2,1,0:T(8,128)S(1)} %get-tuple-element.43.start_c, f32[2,8,8,128]{3,2,1,0:T(8,128)S(1)} %get-tuple-element.73.start_f, ...), custom_call_target="tpu_custom_call" | custom-call | flops 8589934592 | bytes 8388608 | tf_op jit(solution)/shard_map/image/pallas_call | solution.py:188
  59.9 9.6 %filter.1 = (bf16[16,256,256]{2,1,0:T(8,128)(2,1)S(1)}, bf16[16,256,256]{2,1,0:T(8,128)(2,1)S(1)}, bf16[16,256,256]{2,1,0:T(8,128)(2,1)S(1)}, bf16[16,256,256]{2,1,0:T(8,128)(2,1)S(1)}) custom-call(bf16[1024,1024]{1,0:T(8,128)(2,1)S(1)} %copy-done, bf16[16,256,256]{2,1,0:T(8,128)(2,1)S(1)} %image.4.refs_0_, bf16[16,256,256]{2,1,0:T(8,128)(2,1)S(1)} %image.5.refs_1_, ...), custom_call_target="tpu_custom_call" | custom-call | flops 8589934592 | bytes 18874368 | tf_op jit(solution)/shard_map/filter/pallas_call | solution.py:238
  69.6 7.6 %predict.4 = (f32[4,2,256,128]{3,2,1,0:T(8,128)S(1)}, bf16[4,2,256,128]{3,2,1,0:T(8,128)(2,1)S(1)}) custom-call(bf16[16,256,256]{2,1,0:T(8,128)(2,1)S(1)} %get-tuple-element.61.image_ref, bf16[256,2048]{1,0:T(8,128)(2,1)S(1)} %get-tuple-element.62.col_ref, f32[128,16,128]{2,1,0:T(8,128)S(1)} %get-tuple-element.41.step_c, ...), custom_call_target="tpu_custom_call" | custom-call | flops 8589934592 | bytes 8388608 | tf_op jit(solution)/shard_map/predict/pallas_call | solution.py:311
  77.3 7.6 %predict.5 = (f32[4,2,256,128]{3,2,1,0:T(8,128)S(1)}, bf16[4,2,256,128]{3,2,1,0:T(8,128)(2,1)S(1)}) custom-call(bf16[16,256,256]{2,1,0:T(8,128)(2,1)S(1)} %get-tuple-element.65.image_ref, bf16[256,2048]{1,0:T(8,128)(2,1)S(1)} %get-tuple-element.62.col_ref, f32[128,16,128]{2,1,0:T(8,128)S(1)} %get-tuple-element.41.step_c, ...), custom_call_target="tpu_custom_call" | custom-call | flops 8589934592 | bytes 8388608 | tf_op jit(solution)/shard_map/predict/pallas_call | solution.py:311
  85.6 1.6 %collective-permute-start.32 = (bf16[2,256,128]{2,1,0:T(8,128)(2,1)S(1)}, bf16[2,256,128]{2,1,0:T(8,128)(2,1)S(1)}, u32[]{:S(2)}, u32[]{:S(2)}) collective-permute-start(bf16[2,256,128]{2,1,0:T(8,128)(2,1)S(1)} %get-tuple-element.96), channel_id=1, source_target_pairs={{0,6},{1,7},{2,4},{3,5},{4,2},{5,3},{6,0},{7,1},{8,14},{9,15},{10,... | collective-permute-start | bytes 393224 | tf_op jit(solution)/shard_map/ppermute | solution.py:35
  87.7 1.5 %collective-permute-start.34 = (bf16[2,256,128]{2,1,0:T(8,128)(2,1)S(1)}, bf16[2,256,128]{2,1,0:T(8,128)(2,1)S(1)}, u32[]{:S(2)}, u32[]{:S(2)}) collective-permute-start(bf16[2,256,128]{2,1,0:T(8,128)(2,1)S(1)} %get-tuple-element.94), channel_id=1, source_target_pairs={{0,4},{1,5},{2,6},{3,7},{4,0},{5,1},{6,2},{7,3},{8,12},{9,13},{10,... | collective-permute-start | bytes 393224 | tf_op jit(solution)/shard_map/ppermute | solution.py:35
  89.1 7.8 %predict.6 = (f32[4,2,256,128]{3,2,1,0:T(8,128)S(1)}, bf16[4,2,256,128]{3,2,1,0:T(8,128)(2,1)S(1)}) custom-call(bf16[16,256,256]{2,1,0:T(8,128)(2,1)S(1)} %get-tuple-element.68.image_ref, bf16[256,2048]{1,0:T(8,128)(2,1)S(1)} %get-tuple-element.62.col_ref, f32[128,16,128]{2,1,0:T(8,128)S(1)} %get-tuple-element.41.step_c, ...), custom_call_target="tpu_custom_call" | custom-call | flops 8589934592 | bytes 8388608 | tf_op jit(solution)/shard_map/predict/pallas_call | solution.py:311
  97.2 1.6 %collective-permute-start.37 = (bf16[2,256,128]{2,1,0:T(8,128)(2,1)S(1)}, bf16[2,256,128]{2,1,0:T(8,128)(2,1)S(1)}, u32[]{:S(2)}, u32[]{:S(2)}) collective-permute-start(bf16[2,256,128]{2,1,0:T(8,128)(2,1)S(1)} %get-tuple-element.85), channel_id=1, source_target_pairs={{0,6},{1,7},{2,4},{3,5},{4,2},{5,3},{6,0},{7,1},{8,14},{9,15},{10,... | collective-permute-start | bytes 393224 | tf_op jit(solution)/shard_map/ppermute | solution.py:35
  98.9 1.5 %collective-permute-start.38 = (bf16[2,256,128]{2,1,0:T(8,128)(2,1)S(1)}, bf16[2,256,128]{2,1,0:T(8,128)(2,1)S(1)}, u32[]{:S(2)}, u32[]{:S(2)}) collective-permute-start(bf16[2,256,128]{2,1,0:T(8,128)(2,1)S(1)} %get-tuple-element.87), channel_id=1, source_target_pairs={{0,2},{1,3},{2,0},{3,1},{4,6},{5,7},{6,4},{7,5},{8,10},{9,11},{10,... | collective-permute-start | bytes 393224 | tf_op jit(solution)/shard_map/ppermute | solution.py:35
  100.6 1.4 %collective-permute-start.42 = (bf16[2,256,128]{2,1,0:T(8,128)(2,1)S(1)}, bf16[2,256,128]{2,1,0:T(8,128)(2,1)S(1)}, u32[]{:S(2)}, u32[]{:S(2)}) collective-permute-start(bf16[2,256,128]{2,1,0:T(8,128)(2,1)S(1)} %get-tuple-element.93), channel_id=1, source_target_pairs={{0,6},{1,7},{2,4},{3,5},{4,2},{5,3},{6,0},{7,1},{8,14},{9,15},{10,... | collective-permute-start | bytes 393224 | tf_op jit(solution)/shard_map/ppermute | solution.py:35
  102.7 1.5 %collective-permute-start.44 = (bf16[2,256,128]{2,1,0:T(8,128)(2,1)S(1)}, bf16[2,256,128]{2,1,0:T(8,128)(2,1)S(1)}, u32[]{:S(2)}, u32[]{:S(2)}) collective-permute-start(bf16[2,256,128]{2,1,0:T(8,128)(2,1)S(1)} %get-tuple-element.91), channel_id=1, source_target_pairs={{0,4},{1,5},{2,6},{3,7},{4,0},{5,1},{6,2},{7,3},{8,12},{9,13},{10,... | collective-permute-start | bytes 393224 | tf_op jit(solution)/shard_map/ppermute | solution.py:35
  104.2 7.6 %predict.7 = (f32[4,2,256,128]{3,2,1,0:T(8,128)S(1)}, bf16[4,2,256,128]{3,2,1,0:T(8,128)(2,1)S(1)}) custom-call(bf16[16,256,256]{2,1,0:T(8,128)(2,1)S(1)} %get-tuple-element.72.image_ref, bf16[256,2048]{1,0:T(8,128)(2,1)S(1)} %get-tuple-element.62.col_ref, f32[128,16,128]{2,1,0:T(8,128)S(1)} %get-tuple-element.41.step_c, ...), custom_call_target="tpu_custom_call" | custom-call | flops 8589934592 | bytes 8388608 | tf_op jit(solution)/shard_map/predict/pallas_call | solution.py:311
  112.5 1.0 collective-permute-start.35
  113.5 3.3 %collective-permute-done.39 = bf16[2,256,128]{2,1,0:T(8,128)(2,1)S(1)} collective-permute-done((bf16[2,256,128]{2,1,0:T(8,128)(2,1)S(1)}, bf16[2,256,128]{2,1,0:T(8,128)(2,1)S(1)}, u32[]{:S(2)}, u32[]{:S(2)}) %collective-permute-start.39) | collective-permute-done | bytes 131104 | tf_op jit(solution)/shard_map/ppermute | solution.py:35
  116.9 2.9 %collective-permute-start.40 = (bf16[2,256,128]{2,1,0:T(8,128)(2,1)S(1)}, bf16[2,256,128]{2,1,0:T(8,128)(2,1)S(1)}, u32[]{:S(2)}, u32[]{:S(2)}) collective-permute-start(bf16[2,256,128]{2,1,0:T(8,128)(2,1)S(1)} %fusion.8), channel_id=1, source_target_pairs={{0,16},{8,24},{16,0},{24,8},{1,17},{9,25},{17,1},{25,9},{2,18},{10... | collective-permute-start | bytes 393224 | tf_op jit(solution)/shard_map/ppermute | solution.py:39
  120.6 1.4 %collective-permute-start.47 = (bf16[2,256,128]{2,1,0:T(8,128)(2,1)S(1)}, bf16[2,256,128]{2,1,0:T(8,128)(2,1)S(1)}, u32[]{:S(2)}, u32[]{:S(2)}) collective-permute-start(bf16[2,256,128]{2,1,0:T(8,128)(2,1)S(1)} %get-tuple-element.88), channel_id=1, source_target_pairs={{0,6},{1,7},{2,4},{3,5},{4,2},{5,3},{6,0},{7,1},{8,14},{9,15},{10,... | collective-permute-start | bytes 393224 | tf_op jit(solution)/shard_map/ppermute | solution.py:35
  122.7 1.5 %collective-permute-start.49 = (bf16[2,256,128]{2,1,0:T(8,128)(2,1)S(1)}, bf16[2,256,128]{2,1,0:T(8,128)(2,1)S(1)}, u32[]{:S(2)}, u32[]{:S(2)}) collective-permute-start(bf16[2,256,128]{2,1,0:T(8,128)(2,1)S(1)} %get-tuple-element.89), channel_id=1, source_target_pairs={{0,4},{1,5},{2,6},{3,7},{4,0},{5,1},{6,2},{7,3},{8,12},{9,13},{10,... | collective-permute-start | bytes 393224 | tf_op jit(solution)/shard_map/ppermute | solution.py:35
  124.2 1.7 %collective-permute-done.40 = bf16[2,256,128]{2,1,0:T(8,128)(2,1)S(1)} collective-permute-done((bf16[2,256,128]{2,1,0:T(8,128)(2,1)S(1)}, bf16[2,256,128]{2,1,0:T(8,128)(2,1)S(1)}, u32[]{:S(2)}, u32[]{:S(2)}) %collective-permute-start.40) | collective-permute-done | bytes 131104 | tf_op jit(solution)/shard_map/ppermute | solution.py:39
  (102 shorter events, 18.3 us)
Async XLA Ops:
  2.1 10.0 %collective-permute-start = (bf16[2,256,128]{2,1,0:T(8,128)(2,1)S(1)}, bf16[2,256,128]{2,1,0:T(8,128)(2,1)S(1)}, u32[]{:S(2)}, u32[]{:S(2)}) collective-permute-start(bf16[2,256,128]{2,1,0:T(8,128)(2,1)S(1)} %multiply_bitcast_fusion.refs_0_), channel_id=1, source_target_pairs={{0,6},{1,7},{2,4},{3,5},{4,2},{5,3},{6,0},{7,1},{8,14},{9,15},{10,... | collective-permute-start | bytes 393224 | tf_op jit(solution)/shard_map/ppermute | solution.py:35
  6.7 10.0 %collective-permute-start.3 = (bf16[2,256,128]{2,1,0:T(8,128)(2,1)S(1)}, bf16[2,256,128]{2,1,0:T(8,128)(2,1)S(1)}, u32[]{:S(2)}, u32[]{:S(2)}) collective-permute-start(bf16[2,256,128]{2,1,0:T(8,128)(2,1)S(1)} %multiply_bitcast_fusion.refs_0_), channel_id=1, source_target_pairs={{0,1},{1,0},{2,3},{3,2},{4,5},{5,4},{6,7},{7,6},{8,9},{9,8},{10,11... | collective-permute-start | bytes 393224 | tf_op jit(solution)/shard_map/ppermute | solution.py:35
  6.7 8.2 %collective-permute-start.7 = (bf16[2,256,128]{2,1,0:T(8,128)(2,1)S(1)}, bf16[2,256,128]{2,1,0:T(8,128)(2,1)S(1)}, u32[]{:S(2)}, u32[]{:S(2)}) collective-permute-start(bf16[2,256,128]{2,1,0:T(8,128)(2,1)S(1)} %multiply_bitcast_fusion.refs_0_), channel_id=1, source_target_pairs={{0,8},{8,16},{16,24},{24,0},{1,9},{9,17},{17,25},{25,1},{2,10},{10... | collective-permute-start | bytes 393224 | tf_op jit(solution)/shard_map/ppermute | solution.py:39
  13.1 6.6 %collective-permute-start.6 = (bf16[2,256,128]{2,1,0:T(8,128)(2,1)S(1)}, bf16[2,256,128]{2,1,0:T(8,128)(2,1)S(1)}, u32[]{:S(2)}, u32[]{:S(2)}) collective-permute-start(bf16[2,256,128]{2,1,0:T(8,128)(2,1)S(1)} %collective-permute-done.2.refs_3_), channel_id=1, source_target_pairs={{0,1},{1,0},{2,3},{3,2},{4,5},{5,4},{6,7},{7,6},{8,9},{9,8},{10,11... | collective-permute-start | bytes 393224 | tf_op jit(solution)/shard_map/ppermute | solution.py:35
  14.9 12.7 %collective-permute-start.23 = (bf16[2,256,128]{2,1,0:T(8,128)(2,1)S(1)}, bf16[2,256,128]{2,1,0:T(8,128)(2,1)S(1)}, u32[]{:S(2)}, u32[]{:S(2)}) collective-permute-start(bf16[2,256,128]{2,1,0:T(8,128)(2,1)S(1)} %multiply_bitcast_fusion.refs_0_), channel_id=1, source_target_pairs={{0,24},{8,0},{16,8},{24,16},{1,25},{9,1},{17,9},{25,17},{2,26},{10... | collective-permute-start | bytes 393224 | tf_op jit(solution)/shard_map/ppermute | solution.py:39
  16.7 11.3 %collective-permute-start.15 = (bf16[2,256,128]{2,1,0:T(8,128)(2,1)S(1)}, bf16[2,256,128]{2,1,0:T(8,128)(2,1)S(1)}, u32[]{:S(2)}, u32[]{:S(2)}) collective-permute-start(bf16[2,256,128]{2,1,0:T(8,128)(2,1)S(1)} %multiply_bitcast_fusion.refs_0_), channel_id=1, source_target_pairs={{0,16},{8,24},{16,0},{24,8},{1,17},{9,25},{17,1},{25,9},{2,18},{10... | collective-permute-start | bytes 393224 | tf_op jit(solution)/shard_map/ppermute | solution.py:39
  16.8 10.2 %collective-permute-start.10 = (bf16[2,256,128]{2,1,0:T(8,128)(2,1)S(1)}, bf16[2,256,128]{2,1,0:T(8,128)(2,1)S(1)}, u32[]{:S(2)}, u32[]{:S(2)}) collective-permute-start(bf16[2,256,128]{2,1,0:T(8,128)(2,1)S(1)} %collective-permute-done.7.refs_0_), channel_id=1, source_target_pairs={{0,4},{1,5},{2,6},{3,7},{4,0},{5,1},{6,2},{7,3},{8,12},{9,13},{10,... | collective-permute-start | bytes 393224 | tf_op jit(solution)/shard_map/ppermute | solution.py:35
  18.3 8.7 %collective-permute-start.8 = (bf16[2,256,128]{2,1,0:T(8,128)(2,1)S(1)}, bf16[2,256,128]{2,1,0:T(8,128)(2,1)S(1)}, u32[]{:S(2)}, u32[]{:S(2)}) collective-permute-start(bf16[2,256,128]{2,1,0:T(8,128)(2,1)S(1)} %collective-permute-done.7.refs_0_), channel_id=1, source_target_pairs={{0,6},{1,7},{2,4},{3,5},{4,2},{5,3},{6,0},{7,1},{8,14},{9,15},{10,... | collective-permute-start | bytes 393224 | tf_op jit(solution)/shard_map/ppermute | solution.py:35
  19.8 7.3 %collective-permute-start.9 = (bf16[2,256,128]{2,1,0:T(8,128)(2,1)S(1)}, bf16[2,256,128]{2,1,0:T(8,128)(2,1)S(1)}, u32[]{:S(2)}, u32[]{:S(2)}) collective-permute-start(bf16[2,256,128]{2,1,0:T(8,128)(2,1)S(1)} %collective-permute-done.7.refs_0_), channel_id=1, source_target_pairs={{0,2},{1,3},{2,0},{3,1},{4,6},{5,7},{6,4},{7,5},{8,10},{9,11},{10,... | collective-permute-start | bytes 393224 | tf_op jit(solution)/shard_map/ppermute | solution.py:35
  28.0 12.9 %collective-permute-start.24 = (bf16[2,256,128]{2,1,0:T(8,128)(2,1)S(1)}, bf16[2,256,128]{2,1,0:T(8,128)(2,1)S(1)}, u32[]{:S(2)}, u32[]{:S(2)}) collective-permute-start(bf16[2,256,128]{2,1,0:T(8,128)(2,1)S(1)} %collective-permute-done.23.refs_0_), channel_id=1, source_target_pairs={{0,6},{1,7},{2,4},{3,5},{4,2},{5,3},{6,0},{7,1},{8,14},{9,15},{10,... | collective-permute-start | bytes 393224 | tf_op jit(solution)/shard_map/ppermute | solution.py:35
  30.4 11.1 %collective-permute-start.25 = (bf16[2,256,128]{2,1,0:T(8,128)(2,1)S(1)}, bf16[2,256,128]{2,1,0:T(8,128)(2,1)S(1)}, u32[]{:S(2)}, u32[]{:S(2)}) collective-permute-start(bf16[2,256,128]{2,1,0:T(8,128)(2,1)S(1)} %collective-permute-done.23.refs_0_), channel_id=1, source_target_pairs={{0,2},{1,3},{2,0},{3,1},{4,6},{5,7},{6,4},{7,5},{8,10},{9,11},{10,... | collective-permute-start | bytes 393224 | tf_op jit(solution)/shard_map/ppermute | solution.py:35
  31.0 10.6 %collective-permute-start.26 = (bf16[2,256,128]{2,1,0:T(8,128)(2,1)S(1)}, bf16[2,256,128]{2,1,0:T(8,128)(2,1)S(1)}, u32[]{:S(2)}, u32[]{:S(2)}) collective-permute-start(bf16[2,256,128]{2,1,0:T(8,128)(2,1)S(1)} %collective-permute-done.23.refs_0_), channel_id=1, source_target_pairs={{0,4},{1,5},{2,6},{3,7},{4,0},{5,1},{6,2},{7,3},{8,12},{9,13},{10,... | collective-permute-start | bytes 393224 | tf_op jit(solution)/shard_map/ppermute | solution.py:35
  31.5 10.5 %collective-permute-start.16 = (bf16[2,256,128]{2,1,0:T(8,128)(2,1)S(1)}, bf16[2,256,128]{2,1,0:T(8,128)(2,1)S(1)}, u32[]{:S(2)}, u32[]{:S(2)}) collective-permute-start(bf16[2,256,128]{2,1,0:T(8,128)(2,1)S(1)} %collective-permute-done.15.refs_0_), channel_id=1, source_target_pairs={{0,6},{1,7},{2,4},{3,5},{4,2},{5,3},{6,0},{7,1},{8,14},{9,15},{10,... | collective-permute-start | bytes 393224 | tf_op jit(solution)/shard_map/ppermute | solution.py:35
  33.9 8.9 %collective-permute-start.17 = (bf16[2,256,128]{2,1,0:T(8,128)(2,1)S(1)}, bf16[2,256,128]{2,1,0:T(8,128)(2,1)S(1)}, u32[]{:S(2)}, u32[]{:S(2)}) collective-permute-start(bf16[2,256,128]{2,1,0:T(8,128)(2,1)S(1)} %collective-permute-done.15.refs_0_), channel_id=1, source_target_pairs={{0,2},{1,3},{2,0},{3,1},{4,6},{5,7},{6,4},{7,5},{8,10},{9,11},{10,... | collective-permute-start | bytes 393224 | tf_op jit(solution)/shard_map/ppermute | solution.py:35
  45.9 7.5 %collective-permute-start.19 = (bf16[2,256,128]{2,1,0:T(8,128)(2,1)S(1)}, bf16[2,256,128]{2,1,0:T(8,128)(2,1)S(1)}, u32[]{:S(2)}, u32[]{:S(2)}) collective-permute-start(bf16[2,256,128]{2,1,0:T(8,128)(2,1)S(1)} %collective-permute-done.15.refs_0_), channel_id=1, source_target_pairs={{0,1},{1,0},{2,3},{3,2},{4,5},{5,4},{6,7},{7,6},{8,9},{9,8},{10,11... | collective-permute-start | bytes 393224 | tf_op jit(solution)/shard_map/ppermute | solution.py:35
  46.0 7.5 %collective-permute-start.20 = (bf16[2,256,128]{2,1,0:T(8,128)(2,1)S(1)}, bf16[2,256,128]{2,1,0:T(8,128)(2,1)S(1)}, u32[]{:S(2)}, u32[]{:S(2)}) collective-permute-start(bf16[2,256,128]{2,1,0:T(8,128)(2,1)S(1)} %collective-permute-done.16.refs_1_), channel_id=1, source_target_pairs={{0,1},{1,0},{2,3},{3,2},{4,5},{5,4},{6,7},{7,6},{8,9},{9,8},{10,11... | collective-permute-start | bytes 393224 | tf_op jit(solution)/shard_map/ppermute | solution.py:35
  46.5 7.0 %collective-permute-start.21 = (bf16[2,256,128]{2,1,0:T(8,128)(2,1)S(1)}, bf16[2,256,128]{2,1,0:T(8,128)(2,1)S(1)}, u32[]{:S(2)}, u32[]{:S(2)}) collective-permute-start(bf16[2,256,128]{2,1,0:T(8,128)(2,1)S(1)} %collective-permute-done.17.refs_2_), channel_id=1, source_target_pairs={{0,1},{1,0},{2,3},{3,2},{4,5},{5,4},{6,7},{7,6},{8,9},{9,8},{10,11... | collective-permute-start | bytes 393224 | tf_op jit(solution)/shard_map/ppermute | solution.py:35
  46.5 6.9 %collective-permute-start.22 = (bf16[2,256,128]{2,1,0:T(8,128)(2,1)S(1)}, bf16[2,256,128]{2,1,0:T(8,128)(2,1)S(1)}, u32[]{:S(2)}, u32[]{:S(2)}) collective-permute-start(bf16[2,256,128]{2,1,0:T(8,128)(2,1)S(1)} %collective-permute-done.18.refs_3_), channel_id=1, source_target_pairs={{0,1},{1,0},{2,3},{3,2},{4,5},{5,4},{6,7},{7,6},{8,9},{9,8},{10,11... | collective-permute-start | bytes 393224 | tf_op jit(solution)/shard_map/ppermute | solution.py:35
  77.1 8.2 %collective-permute-start.31 = (bf16[4,2,256,128]{3,2,1,0:T(8,128)(2,1)S(1)}, bf16[4,2,256,128]{3,2,1,0:T(8,128)(2,1)S(1)}, u32[]{:S(2)}, u32[]{:S(2)}) collective-permute-start(bf16[4,2,256,128]{3,2,1,0:T(8,128)(2,1)S(1)} %get-tuple-element.64), channel_id=1, source_target_pairs={{0,1},{1,0},{2,3},{3,2},{4,5},{5,4},{6,7},{7,6},{8,9},{9,8},{10,11... | collective-permute-start | bytes 1572872 | tf_op jit(solution)/shard_map/ppermute | solution.py:35
  84.9 12.2 %collective-permute-start.36 = (bf16[4,2,256,128]{3,2,1,0:T(8,128)(2,1)S(1)}, bf16[4,2,256,128]{3,2,1,0:T(8,128)(2,1)S(1)}, u32[]{:S(2)}, u32[]{:S(2)}) collective-permute-start(bf16[4,2,256,128]{3,2,1,0:T(8,128)(2,1)S(1)} %get-tuple-element.67), channel_id=1, source_target_pairs={{0,1},{1,0},{2,3},{3,2},{4,5},{5,4},{6,7},{7,6},{8,9},{9,8},{10,11... | collective-permute-start | bytes 1572872 | tf_op jit(solution)/shard_map/ppermute | solution.py:35
  85.6 15.0 %collective-permute-start.32 = (bf16[2,256,128]{2,1,0:T(8,128)(2,1)S(1)}, bf16[2,256,128]{2,1,0:T(8,128)(2,1)S(1)}, u32[]{:S(2)}, u32[]{:S(2)}) collective-permute-start(bf16[2,256,128]{2,1,0:T(8,128)(2,1)S(1)} %get-tuple-element.96), channel_id=1, source_target_pairs={{0,6},{1,7},{2,4},{3,5},{4,2},{5,3},{6,0},{7,1},{8,14},{9,15},{10,... | collective-permute-start | bytes 393224 | tf_op jit(solution)/shard_map/ppermute | solution.py:35
  87.1 14.9 %collective-permute-start.33 = (bf16[2,256,128]{2,1,0:T(8,128)(2,1)S(1)}, bf16[2,256,128]{2,1,0:T(8,128)(2,1)S(1)}, u32[]{:S(2)}, u32[]{:S(2)}) collective-permute-start(bf16[2,256,128]{2,1,0:T(8,128)(2,1)S(1)} %get-tuple-element.95), channel_id=1, source_target_pairs={{0,2},{1,3},{2,0},{3,1},{4,6},{5,7},{6,4},{7,5},{8,10},{9,11},{10,... | collective-permute-start | bytes 393224 | tf_op jit(solution)/shard_map/ppermute | solution.py:35
  87.7 15.0 %collective-permute-start.34 = (bf16[2,256,128]{2,1,0:T(8,128)(2,1)S(1)}, bf16[2,256,128]{2,1,0:T(8,128)(2,1)S(1)}, u32[]{:S(2)}, u32[]{:S(2)}) collective-permute-start(bf16[2,256,128]{2,1,0:T(8,128)(2,1)S(1)} %get-tuple-element.94), channel_id=1, source_target_pairs={{0,4},{1,5},{2,6},{3,7},{4,0},{5,1},{6,2},{7,3},{8,12},{9,13},{10,... | collective-permute-start | bytes 393224 | tf_op jit(solution)/shard_map/ppermute | solution.py:35
  97.2 16.3 %collective-permute-start.37 = (bf16[2,256,128]{2,1,0:T(8,128)(2,1)S(1)}, bf16[2,256,128]{2,1,0:T(8,128)(2,1)S(1)}, u32[]{:S(2)}, u32[]{:S(2)}) collective-permute-start(bf16[2,256,128]{2,1,0:T(8,128)(2,1)S(1)} %get-tuple-element.85), channel_id=1, source_target_pairs={{0,6},{1,7},{2,4},{3,5},{4,2},{5,3},{6,0},{7,1},{8,14},{9,15},{10,... | collective-permute-start | bytes 393224 | tf_op jit(solution)/shard_map/ppermute | solution.py:35
  98.9 14.6 %collective-permute-start.38 = (bf16[2,256,128]{2,1,0:T(8,128)(2,1)S(1)}, bf16[2,256,128]{2,1,0:T(8,128)(2,1)S(1)}, u32[]{:S(2)}, u32[]{:S(2)}) collective-permute-start(bf16[2,256,128]{2,1,0:T(8,128)(2,1)S(1)} %get-tuple-element.87), channel_id=1, source_target_pairs={{0,2},{1,3},{2,0},{3,1},{4,6},{5,7},{6,4},{7,5},{8,10},{9,11},{10,... | collective-permute-start | bytes 393224 | tf_op jit(solution)/shard_map/ppermute | solution.py:35
  100.6 11.2 %collective-permute-start.42 = (bf16[2,256,128]{2,1,0:T(8,128)(2,1)S(1)}, bf16[2,256,128]{2,1,0:T(8,128)(2,1)S(1)}, u32[]{:S(2)}, u32[]{:S(2)}) collective-permute-start(bf16[2,256,128]{2,1,0:T(8,128)(2,1)S(1)} %get-tuple-element.93), channel_id=1, source_target_pairs={{0,6},{1,7},{2,4},{3,5},{4,2},{5,3},{6,0},{7,1},{8,14},{9,15},{10,... | collective-permute-start | bytes 393224 | tf_op jit(solution)/shard_map/ppermute | solution.py:35
  102.0 10.4 %collective-permute-start.43 = (bf16[2,256,128]{2,1,0:T(8,128)(2,1)S(1)}, bf16[2,256,128]{2,1,0:T(8,128)(2,1)S(1)}, u32[]{:S(2)}, u32[]{:S(2)}) collective-permute-start(bf16[2,256,128]{2,1,0:T(8,128)(2,1)S(1)} %get-tuple-element.92), channel_id=1, source_target_pairs={{0,2},{1,3},{2,0},{3,1},{4,6},{5,7},{6,4},{7,5},{8,10},{9,11},{10,... | collective-permute-start | bytes 393224 | tf_op jit(solution)/shard_map/ppermute | solution.py:35
  102.7 9.7 %collective-permute-start.44 = (bf16[2,256,128]{2,1,0:T(8,128)(2,1)S(1)}, bf16[2,256,128]{2,1,0:T(8,128)(2,1)S(1)}, u32[]{:S(2)}, u32[]{:S(2)}) collective-permute-start(bf16[2,256,128]{2,1,0:T(8,128)(2,1)S(1)} %get-tuple-element.91), channel_id=1, source_target_pairs={{0,4},{1,5},{2,6},{3,7},{4,0},{5,1},{6,2},{7,3},{8,12},{9,13},{10,... | collective-permute-start | bytes 393224 | tf_op jit(solution)/shard_map/ppermute | solution.py:35
  112.4 8.0 %collective-permute-start.46 = (bf16[4,2,256,128]{3,2,1,0:T(8,128)(2,1)S(1)}, bf16[4,2,256,128]{3,2,1,0:T(8,128)(2,1)S(1)}, u32[]{:S(2)}, u32[]{:S(2)}) collective-permute-start(bf16[4,2,256,128]{3,2,1,0:T(8,128)(2,1)S(1)} %get-tuple-element.76), channel_id=1, source_target_pairs={{0,1},{1,0},{2,3},{3,2},{4,5},{5,4},{6,7},{7,6},{8,9},{9,8},{10,11... | collective-permute-start | bytes 1572872 | tf_op jit(solution)/shard_map/ppermute | solution.py:35
  112.5 10.2 %collective-permute-start.35 = (bf16[2,256,128]{2,1,0:T(8,128)(2,1)S(1)}, bf16[2,256,128]{2,1,0:T(8,128)(2,1)S(1)}, u32[]{:S(2)}, u32[]{:S(2)}) collective-permute-start(bf16[2,256,128]{2,1,0:T(8,128)(2,1)S(1)} %fusion.10), channel_id=1, source_target_pairs={{0,8},{8,16},{16,24},{24,0},{1,9},{9,17},{17,25},{25,1},{2,10},{10... | collective-permute-start | bytes 393224 | tf_op jit(solution)/shard_map/ppermute | solution.py:39
  116.9 9.1 %collective-permute-start.40 = (bf16[2,256,128]{2,1,0:T(8,128)(2,1)S(1)}, bf16[2,256,128]{2,1,0:T(8,128)(2,1)S(1)}, u32[]{:S(2)}, u32[]{:S(2)}) collective-permute-start(bf16[2,256,128]{2,1,0:T(8,128)(2,1)S(1)} %fusion.8), channel_id=1, source_target_pairs={{0,16},{8,24},{16,0},{24,8},{1,17},{9,25},{17,1},{25,9},{2,18},{10... | collective-permute-start | bytes 393224 | tf_op jit(solution)/shard_map/ppermute | solution.py:39
  119.9 6.8 %collective-permute-start.45 = (bf16[2,256,128]{2,1,0:T(8,128)(2,1)S(1)}, bf16[2,256,128]{2,1,0:T(8,128)(2,1)S(1)}, u32[]{:S(2)}, u32[]{:S(2)}) collective-permute-start(bf16[2,256,128]{2,1,0:T(8,128)(2,1)S(1)} %fusion.6), channel_id=1, source_target_pairs={{0,24},{8,0},{16,8},{24,16},{1,25},{9,1},{17,9},{25,17},{2,26},{10... | collective-permute-start | bytes 393224 | tf_op jit(solution)/shard_map/ppermute | solution.py:39
  (21 other events, 95.0 us)
